TPU v7x, 256 devices: a whole 4x4x8 slice. The times are simulated.
256 devices in a mesh: tm: 64 (over x, z, core), rows: 4 (over y).
Axes of the slice: x: 4, y: 4, z: 8, core: 2. Of those that a mesh axis runs over, the one named last changes fastest.
Arguments:
- features: bfloat16 [128, 4, 160, 512], P('tm', 'rows'), may hold values from -25 to 25
- norm_gain: float32 [512], replicated, may hold values from 0.1 to 1.9
- norm_bias: float32 [512], replicated, may hold values from -1 to 1
- weight: bfloat16 [3, 3, 3, 512, 256], replicated, may hold values from -0.0546875 to 0.0546875
- upstream: bfloat16 [128, 4, 160, 256], P('tm', 'rows'), may hold values from -20 to 20
Outputs:
- grad_features: bfloat16 [128, 4, 160, 512], P('tm', 'rows')
- grad_weight: float32 [3, 3, 3, 512, 256], P(None, None, None, 'tm', 'rows')
- grad_gain: float32 [512], replicated
- grad_bias: float32 [512], replicated
All inputs are finite; a program needn't handle non-finite values.
Results may differ from a plain program's by a relative error of at most 0.0015.
Values may be sent and summed in bfloat16 or wider, within the bound.
No kernel may reach another device: no remote copies, remote signals or barrier semaphores. Data moves between devices by JAX's collectives and lax.ppermute only.
A program may use at most 64 MiB of HBM per device.

v0:
```python
import jax
import jax.numpy as jnp
from jax import lax
from jax.sharding import PartitionSpec as P

GROUPS = 32
CLIPS = 1


epsilon = 1e-06


def from_behind(value, axis, steps):
    count = lax.axis_size(axis)
    initial, last = (max(0, -steps), min(count, count - steps))
    return lax.ppermute(value, axis, [(source, source + steps) for source in range(initial, last)])


def padded(cells, sides, width):
    for axis, dim in sides:
        count = lax.axis_size(axis)
        ends = count - 1
        head = lax.slice_in_dim(cells, 0, width, axis=dim)
        tail = lax.slice_in_dim(cells, cells.shape[dim] - width, cells.shape[dim], axis=dim)
        cells = jnp.concatenate(
            [
                lax.ppermute(tail, axis, [(i, (i + 1) % count) for i in range(ends)]),
                cells,
                lax.ppermute(head, axis, [((i + 1) % count, i) for i in range(ends)]),
            ],
            axis=dim,
        )
    return cells


def on_device(features, norm_gain, norm_bias, weight, upstream):
    frames_dev, rows_dev, cols, chans = features.shape
    outs = upstream.shape[3]
    group_size = chans // GROUPS
    per_clip = lax.axis_size("tm") // CLIPS
    time_index = lax.axis_index("tm")
    clip_index = time_index // per_clip
    first_dev = time_index % per_clip == 0
    last_dev = time_index % per_clip == per_clip - 1
    selector = (jnp.arange(CLIPS) == clip_index).astype(jnp.float32)
    count_clip = frames_dev * rows_dev * cols * group_size * per_clip * lax.axis_size("rows")
    floats = features.astype(jnp.float32)
    grouped = floats.reshape(frames_dev, rows_dev, cols, GROUPS, group_size)
    local_sum = jnp.sum(grouped, axis=(0, 1, 2, 4))
    total_sum = lax.psum(selector[:, None] * local_sum, ("tm", "rows"))
    centre_val = jnp.sum(selector[:, None] * total_sum, axis=0) / count_clip
    diffs = grouped - centre_val[:, None]
    local_dev = jnp.sum(diffs * diffs, axis=(0, 1, 2, 4))
    total_dev = lax.psum(selector[:, None] * local_dev, ("tm", "rows"))
    spread = jnp.sum(selector[:, None] * total_dev, axis=0) / count_clip
    inverse = lax.rsqrt(spread + epsilon)
    normed = (diffs * inverse[:, None]).reshape(frames_dev, rows_dev, cols, chans)
    preact = normed * norm_gain + norm_bias
    sig_val = jax.nn.sigmoid(preact)
    hidden = (preact * sig_val).astype(jnp.bfloat16)
    earlier = from_behind(hidden, "tm", 1)
    earlier = jnp.where(first_dev, jnp.concatenate([hidden[:1], hidden[:1]], axis=0), earlier)
    extended = jnp.concatenate([earlier, hidden], axis=0)
    extended = padded(extended, (("rows", 1),), 1)
    extended = jnp.pad(extended, ((0, 0), (0, 0), (1, 1), (0, 0)))
    up_flat = upstream.reshape(-1, outs)
    grad_taps = []
    for time_tap in range(3):
        for row_tap in range(3):
            for col_tap in range(3):
                slab = extended[
                    time_tap : time_tap + frames_dev,
                    row_tap : row_tap + rows_dev,
                    col_tap : col_tap + cols,
                ].reshape(-1, chans)
                grad_taps.append(
                    lax.dot_general(
                        slab, up_flat, (((0,), (0,)), ((), ())), preferred_element_type=jnp.float32
                    )
                )
    local_grad = jnp.stack(grad_taps).reshape(3, 3, 3, chans, outs)
    halfway = lax.psum_scatter(local_grad, "tm", scatter_dimension=3, tiled=True)
    grad_weight = lax.psum_scatter(halfway, "rows", scatter_dimension=4, tiled=True)
    later = from_behind(upstream, "tm", -1)
    later = jnp.where(last_dev, jnp.zeros_like(later), later)
    up_ext = jnp.concatenate([upstream, later], axis=0)
    up_ext = padded(up_ext, (("rows", 1),), 1)
    up_ext = jnp.pad(up_ext, ((0, 0), (0, 0), (1, 1), (0, 0)))
    dense = jnp.zeros((frames_dev * rows_dev * cols, chans), jnp.float32)
    for time_tap in range(3):
        for row_tap in range(3):
            for col_tap in range(3):
                slab = up_ext[
                    2 - time_tap : 2 - time_tap + frames_dev,
                    2 - row_tap : 2 - row_tap + rows_dev,
                    2 - col_tap : 2 - col_tap + cols,
                ].reshape(-1, outs)
                dense = dense + jnp.dot(
                    slab, weight[time_tap, row_tap, col_tap].T, preferred_element_type=jnp.float32
                )
    dense = dense.reshape(frames_dev, rows_dev, cols, chans)

    def pad_terms(unused):
        total = jnp.zeros((rows_dev * cols, chans), jnp.float32)
        for row_tap in range(3):
            for col_tap in range(3):
                first_slab = up_ext[
                    0, 2 - row_tap : 2 - row_tap + rows_dev, 2 - col_tap : 2 - col_tap + cols
                ].reshape(-1, outs)
                second_slab = up_ext[
                    1, 2 - row_tap : 2 - row_tap + rows_dev, 2 - col_tap : 2 - col_tap + cols
                ].reshape(-1, outs)
                total = total + jnp.dot(
                    first_slab, weight[0, row_tap, col_tap].T, preferred_element_type=jnp.float32
                )
                total = total + jnp.dot(
                    first_slab, weight[1, row_tap, col_tap].T, preferred_element_type=jnp.float32
                )
                total = total + jnp.dot(
                    second_slab, weight[0, row_tap, col_tap].T, preferred_element_type=jnp.float32
                )
        return total.reshape(rows_dev, cols, chans)

    def skip_terms(unused):
        return jnp.zeros((rows_dev, cols, chans), jnp.float32)

    extra = lax.cond(first_dev, pad_terms, skip_terms, 0)
    grad_hidden = dense.at[0].add(extra)
    grad_act = grad_hidden * sig_val * (1.0 + preact * (1.0 - sig_val))
    local_gain = jnp.sum(grad_act * normed, axis=(0, 1, 2))
    local_bias = jnp.sum(grad_act, axis=(0, 1, 2))
    clip_gain, clip_bias = lax.psum(
        (selector[:, None] * local_gain, selector[:, None] * local_bias), ("tm", "rows")
    )
    grad_gain = jnp.sum(clip_gain, axis=0)
    grad_bias = jnp.sum(clip_bias, axis=0)
    own_gain = jnp.sum(selector[:, None] * clip_gain, axis=0)
    own_bias = jnp.sum(selector[:, None] * clip_bias, axis=0)
    first_term = jnp.repeat(
        jnp.sum((norm_gain * own_bias).reshape(GROUPS, -1), axis=1) / count_clip, group_size
    )
    second_term = jnp.repeat(
        jnp.sum((norm_gain * own_gain).reshape(GROUPS, -1), axis=1) / count_clip, group_size
    )
    inverse_chan = jnp.repeat(inverse, group_size)
    grad_features = (
        inverse_chan * (grad_act * norm_gain - first_term - normed * second_term)
    ).astype(jnp.bfloat16)
    return (grad_features, grad_weight, grad_gain, grad_bias)


def solution(mesh):
    in_specs = (P("tm", "rows", None, None), P(), P(), P(), P("tm", "rows", None, None))
    out_specs = (P("tm", "rows", None, None), P(None, None, None, "tm", "rows"), P(), P())
    return jax.shard_map(
        on_device, mesh=mesh, in_specs=in_specs, out_specs=out_specs, check_vma=False
    )
```

profile of v0, /device:TPU:1, one launch (start us, length us, event | category | flops | bytes accessed | tf_op | source)
XLA Modules:
  0.0 454.3 jit_solution(16119461968592886430)
XLA Ops:
  8.5 5.1 %collective-permute-start = (bf16[2,1,160,256]{3,2,1,0:T(8,128)(2,1)}, bf16[2,1,160,256]{3,2,1,0:T(8,128)(2,1)S(1)}, u32[]{:S(2)}, u32[]{:S(2)}) collective-permute-start(bf16[2,1,160,256]{3,2,1,0:T(8,128)(2,1)} %param.13), channel_id=1, source_target_pairs={{4,0},{8,4},{12,8},{16,12},{20,16},{24,20},{28,24},{32,28},{36,32}... | collective-permute-start | bytes 491528 | tf_op jit(solution)/shard_map/ppermute | solution.py:16
  13.6 78.8 %psum.28 = f32[1,32]{1,0:T(1,128)S(1)} all-reduce(f32[1,32]{1,0:T(1,128)S(1)} %multiply_bitcast_fusion.2), channel_id=1, replica_groups=mesh['tm'=64,'rows'=4] {'tm','rows'}, use_global_device_ids=true, to_apply=%region_2.3 | all-reduce | flops 32 | bytes 256 | tf_op jit(solution)/shard_map/psum | solution.py:50
  93.9 72.6 %psum.29 = f32[1,32]{1,0:T(1,128)S(1)} all-reduce(f32[1,32]{1,0:T(1,128)S(1)} %multiply_bitcast_fusion), channel_id=1, replica_groups=mesh['tm'=64,'rows'=4] {'tm','rows'}, use_global_device_ids=true, to_apply=%region_5.6 | all-reduce | flops 32 | bytes 256 | tf_op jit(solution)/shard_map/psum | solution.py:54
  167.5 1.3 collective-permute-start.2
  168.8 4.0 collective-permute-start.1
  174.0 3.9 collective-permute-done.2
  178.9 1.2 select_maximum_fusion.2
  189.8 5.2 %collective-permute-start.3 = (bf16[2,1,160,512]{3,2,0,1:T(8,128)(2,1)S(1)}, bf16[2,1,160,512]{3,2,0,1:T(8,128)(2,1)S(1)}, u32[]{:S(2)}, u32[]{:S(2)}) collective-permute-start(bf16[2,1,160,512]{3,2,0,1:T(8,128)(2,1)S(1)} %get-tuple-element.61), channel_id=1, source_target_pairs={{0,4},{4,8},{8,12},{12,16},{16,20},{20,24},{24,28},{28,32},{32,36}... | collective-permute-start | bytes 983048 | tf_op jit(solution)/shard_map/ppermute | solution.py:16
  195.0 4.6 %collective-permute-done.3 = bf16[2,1,160,512]{3,2,0,1:T(8,128)(2,1)S(1)} collective-permute-done((bf16[2,1,160,512]{3,2,0,1:T(8,128)(2,1)S(1)}, bf16[2,1,160,512]{3,2,0,1:T(8,128)(2,1)S(1)}, u32[]{:S(2)}, u32[]{:S(2)}) %collective-permute-start.3) | collective-permute-done | bytes 327712 | tf_op jit(solution)/shard_map/ppermute | solution.py:16
  199.7 1.3 collective-permute-start.5
  201.0 5.0 %collective-permute-start.4 = (bf16[4,1,160,512]{3,2,0,1:T(8,128)(2,1)S(1)}, bf16[4,1,160,512]{3,2,0,1:T(8,128)(2,1)S(1)}, u32[]{:S(2)}, u32[]{:S(2)}) collective-permute-start(bf16[4,1,160,512]{3,2,0,1:T(8,128)(2,1)S(1)} %pad_maximum_fusion), channel_id=1, source_target_pairs={{0,1},{1,2},{2,3},{4,5},{5,6},{6,7},{8,9},{9,10},{10,11},{12,13},{... | collective-permute-start | bytes 1966088 | tf_op jit(solution)/shard_map/ppermute | solution.py:27
  206.0 12.8 %collective-permute-done.5 = bf16[4,1,160,512]{3,2,0,1:T(8,128)(2,1)S(1)} collective-permute-done((bf16[4,1,160,512]{3,2,0,1:T(8,128)(2,1)S(1)}, bf16[4,1,160,512]{3,2,0,1:T(8,128)(2,1)S(1)}, u32[]{:S(2)}, u32[]{:S(2)}) %collective-permute-start.5) | collective-permute-done | bytes 655392 | tf_op jit(solution)/shard_map/ppermute | solution.py:29
  235.4 1.2 fusion.134
  238.8 1.2 fusion.131
  240.0 1.2 fusion.130
  243.5 1.2 fusion.127
  248.1 1.2 fusion.123
  249.2 1.2 fusion.122
  251.6 75.4 %all-reduce.2 = (f32[1,512]{1,0:T(1,128)S(1)}, f32[1,512]{1,0:T(1,128)S(1)}) all-reduce(f32[1,512]{1,0:T(1,128)S(1)} %bitcast.622, f32[1,512]{1,0:T(1,128)S(1)} %bitcast.623), channel_id=1, replica_groups=mesh['tm'=64,'rows'=4] {'tm','rows'}, use_global_device_ids=true, to_apply=%region_12.13 | all-reduce | flops 1024 | bytes 8192 | tf_op jit(solution)/shard_map/psum | solution.py:132
  327.6 83.4 %reduce-scatter.5.cloned.1.call-done = f32[3,3,3,8,256]{4,3,2,1,0:T(8,128)} async-done(((f32[3,3,3,512,256]{4,3,2,1,0:T(8,128)}), f32[3,3,3,8,256]{4,3,2,1,0:T(8,128)}) %reduce-scatter.5.cloned.1.call-update) | async-done | bytes 221200 | tf_op jit(solution)/shard_map/reduce_scatter | solution.py:82
  411.0 5.2 %copy.18 = f32[3,3,3,8,256]{3,2,1,0,4:T(4,128)} copy(f32[3,3,3,8,256]{4,3,2,1,0:T(8,128)} %reduce-scatter.5.cloned.1.call-done) | data formatting | bytes 442368
  416.3 5.4 %reshape.499 = f32[256,216]{1,0:T(8,128)} reshape(f32[256,3,3,3,8]{4,3,2,1,0:T(4,128)} %bitcast.592) | data formatting | bytes 442368
  422.7 22.4 %reduce-scatter.7.cloned.1.call-done = f32[64,216]{1,0:T(8,128)} async-done(((f32[256,216]{1,0:T(8,128)}), f32[64,216]{1,0:T(8,128)}) %reduce-scatter.7.cloned.1.call-update) | async-done | bytes 55312
  445.1 1.4 reshape.500
  (114 shorter events, 43.7 us)
Async XLA Ops:
  7.2 403.9 %reduce-scatter.5.cloned.1.call-start = ((), (), s32[]{:S(2)}) async-start(), calls=%async_computation.2 | async-start | bytes 14376960 | tf_op jit(solution)/shard_map/reduce_scatter | solution.py:82
  8.5 158.0 %collective-permute-start = (bf16[2,1,160,256]{3,2,1,0:T(8,128)(2,1)}, bf16[2,1,160,256]{3,2,1,0:T(8,128)(2,1)S(1)}, u32[]{:S(2)}, u32[]{:S(2)}) collective-permute-start(bf16[2,1,160,256]{3,2,1,0:T(8,128)(2,1)} %param.13), channel_id=1, source_target_pairs={{4,0},{8,4},{12,8},{16,12},{20,16},{24,20},{28,24},{32,28},{36,32}... | collective-permute-start | bytes 491528 | tf_op jit(solution)/shard_map/ppermute | solution.py:16
  167.5 10.5 %collective-permute-start.2 = (bf16[4,1,160,256]{3,2,1,0:T(8,128)(2,1)S(1)}, bf16[4,1,160,256]{3,2,1,0:T(8,128)(2,1)S(1)}, u32[]{:S(2)}, u32[]{:S(2)}) collective-permute-start(bf16[4,1,160,256]{3,2,1,0:T(8,128)(2,1)S(1)} %pad_maximum_fusion.1), channel_id=1, source_target_pairs={{1,0},{2,1},{3,2},{5,4},{6,5},{7,6},{9,8},{10,9},{11,10},{13,12},{... | collective-permute-start | bytes 983048 | tf_op jit(solution)/shard_map/ppermute | solution.py:29
  168.8 10.1 %collective-permute-start.1 = (bf16[4,1,160,256]{3,2,1,0:T(8,128)(2,1)S(1)}, bf16[4,1,160,256]{3,2,1,0:T(8,128)(2,1)S(1)}, u32[]{:S(2)}, u32[]{:S(2)}) collective-permute-start(bf16[4,1,160,256]{3,2,1,0:T(8,128)(2,1)S(1)} %pad_maximum_fusion.1), channel_id=1, source_target_pairs={{0,1},{1,2},{2,3},{4,5},{5,6},{6,7},{8,9},{9,10},{10,11},{12,13},{... | collective-permute-start | bytes 983048 | tf_op jit(solution)/shard_map/ppermute | solution.py:27
  172.9 7.6 %copy-start = (bf16[3,3,3,512,256]{4,3,2,1,0:T(8,128)(2,1)S(1)}, bf16[3,3,3,512,256]{4,3,2,1,0:T(8,128)(2,1)}, u32[]{:S(2)}) copy-start(bf16[3,3,3,512,256]{4,3,2,1,0:T(8,128)(2,1)} %param.12) | copy-start | bytes 21233668
  185.2 2.0 copy-start.1
  188.4 1.0 copy-start.2
  188.4 1.0 copy-start.3
  188.4 1.0 copy-start.6
  189.8 9.8 %collective-permute-start.3 = (bf16[2,1,160,512]{3,2,0,1:T(8,128)(2,1)S(1)}, bf16[2,1,160,512]{3,2,0,1:T(8,128)(2,1)S(1)}, u32[]{:S(2)}, u32[]{:S(2)}) collective-permute-start(bf16[2,1,160,512]{3,2,0,1:T(8,128)(2,1)S(1)} %get-tuple-element.61), channel_id=1, source_target_pairs={{0,4},{4,8},{8,12},{12,16},{16,20},{20,24},{24,28},{28,32},{32,36}... | collective-permute-start | bytes 983048 | tf_op jit(solution)/shard_map/ppermute | solution.py:16
  199.7 19.1 %collective-permute-start.5 = (bf16[4,1,160,512]{3,2,0,1:T(8,128)(2,1)S(1)}, bf16[4,1,160,512]{3,2,0,1:T(8,128)(2,1)S(1)}, u32[]{:S(2)}, u32[]{:S(2)}) collective-permute-start(bf16[4,1,160,512]{3,2,0,1:T(8,128)(2,1)S(1)} %pad_maximum_fusion), channel_id=1, source_target_pairs={{1,0},{2,1},{3,2},{5,4},{6,5},{7,6},{9,8},{10,9},{11,10},{13,12},{... | collective-permute-start | bytes 1966088 | tf_op jit(solution)/shard_map/ppermute | solution.py:29
  201.0 18.7 %collective-permute-start.4 = (bf16[4,1,160,512]{3,2,0,1:T(8,128)(2,1)S(1)}, bf16[4,1,160,512]{3,2,0,1:T(8,128)(2,1)S(1)}, u32[]{:S(2)}, u32[]{:S(2)}) collective-permute-start(bf16[4,1,160,512]{3,2,0,1:T(8,128)(2,1)S(1)} %pad_maximum_fusion), channel_id=1, source_target_pairs={{0,1},{1,2},{2,3},{4,5},{5,6},{6,7},{8,9},{9,10},{10,11},{12,13},{... | collective-permute-start | bytes 1966088 | tf_op jit(solution)/shard_map/ppermute | solution.py:27
  251.6 193.5 %reduce-scatter.7.cloned.1.call-start = ((), (), s32[]{:S(2)}) async-start(), calls=%async_computation.3 | async-start | bytes 327680
  327.0 120.5 %copy-start.4 = (f32[1,512]{1,0:T(1,128)}, f32[1,512]{1,0:T(1,128)S(1)}, u32[]{:S(2)}) copy-start(f32[1,512]{1,0:T(1,128)S(1)} %get-tuple-element.40) | copy-start | bytes 6148
  327.0 120.5 %copy-start.5 = (f32[1,512]{1,0:T(1,128)}, f32[1,512]{1,0:T(1,128)S(1)}, u32[]{:S(2)}) copy-start(f32[1,512]{1,0:T(1,128)S(1)} %get-tuple-element.41) | copy-start | bytes 6148
Sparse Core Ops, SparseCore 0:
  251.7 159.2 reduce-scatter.4
  421.8 23.2 reduce-scatter.6
where the time goes:
time: 457 us; the launch traced here: 454 us
  blocking collectives  227 us (50%)
  waiting for transfers between devices  129 us (28%)
  matrix products  38.5 us (8%)
  starting transfers between devices  21.9 us (5%)
  local copies, waits for them, and re-layouts  15.4 us (3%)
  between operations  14.6 us (3%)
  other arithmetic  8.17 us (2%)
    reduce_scatter x1, waiting for transfers between devices, on_device(): lax.psum_scatter(local_grad, 'tm', scatter_dimension=3, tiled=True)  83.4 us
    psum x1, blocking collectives, on_device(): total_sum = lax.psum(selector[:, None] * local_sum, ('tm', 'rows'))  78.8 us
    psum x1, blocking collectives, on_device(): lax.psum((selector[:, None] * local_gain, selector[:, None] * local_bias)...  75.4 us
    psum x1, blocking collectives, on_device(): total_dev = lax.psum(selector[:, None] * local_dev, ('tm', 'rows'))  72.6 us
    dot_general x27, matrix products, on_device(): lax.dot_general(slab, up_flat, (((0,), (0,)), ((), ())), preferred_elemen...  31 us
    unnamed x3, waiting for transfers between devices  22.4 us
    ppermute x2, waiting for transfers between devices, padded(): lax.ppermute(head, axis, [((i + 1) % count, i) for i in range(ends)])  16.8 us
    unnamed x19, local copies, waits for them, and re-layouts  13.9 us
  transfers between devices with their start and end apart: 8, of which 7 were waited for; matrix products, arithmetic and copies ran while one was open for 1% of the time, Pallas kernels for 0%

commit v1 on v0

v1 whole, which is shorter than its diff:
```python
import functools

import jax
import jax.numpy as jnp
from jax import lax
from jax.experimental import pallas as pl
from jax.experimental.pallas import tpu as pltpu
from jax.sharding import PartitionSpec as P

GROUPS = 32
EPS = 1e-06
TEAM = 4
F32 = jnp.float32
BF16 = jnp.bfloat16


def iota(shape, dim):
    return lax.broadcasted_iota(jnp.int32, shape, dim)


def exact_dot(a, b, dims=((1,), (0,))):
    return lax.dot_general(
        a, b, (dims, ((), ())), precision=lax.Precision.HIGHEST, preferred_element_type=F32
    )


def members(chans, offset):
    size = chans // GROUPS
    return (iota((chans, 128), 0) // size + offset == iota((chans, 128), 1)).astype(F32)


def col_shifts(slab):
    cols = slab.shape[0]
    wide = slab.astype(F32)
    row = iota(wide.shape, 0)
    ahead = jnp.where(row < cols - 1, pltpu.roll(wide, cols - 1, 0), 0.0).astype(BF16)
    behind = jnp.where(row > 0, pltpu.roll(wide, 1, 0), 0.0).astype(BF16)
    return ahead, slab, behind


def pack_kernel(teams, feats_ref, up_ref, load_ref, stat_ref):
    positions, chans = feats_ref.shape
    cols = up_ref.shape[1]
    rows = load_ref.shape[1]
    feats = feats_ref[...]
    lane = iota((chans, chans), 1)
    wide = chans // TEAM
    step = chans // teams
    source = (lane % wide) // step * (step * TEAM) + lane // wide * step + lane % step
    mover = (iota((chans, chans), 0) == source).astype(BF16)
    moved = jnp.dot(feats, mover, preferred_element_type=F32).astype(BF16)
    outs = up_ref.shape[2] // rows
    for r in range(rows):
        pair = jnp.concatenate(
            [up_ref[0, :, r * outs : (r + 1) * outs], up_ref[1, :, r * outs : (r + 1) * outs]], axis=1
        )
        for j in range(TEAM):
            load_ref[j, r, 0:positions, :] = moved[:, j * wide : (j + 1) * wide]
            load_ref[j, r, positions : positions + cols, :] = pair
    floats = feats.astype(F32)
    first = members(chans, 0)
    second = members(chans, GROUPS)
    total = jnp.broadcast_to(jnp.sum(floats, axis=0, keepdims=True), (8, chans))
    mean = exact_dot(total, first) / (positions * (chans // GROUPS))
    diffs = floats - exact_dot(mean, first, ((1,), (1,)))[0:1]
    squares = jnp.broadcast_to(jnp.sum(diffs * diffs, axis=0, keepdims=True), (8, chans))
    stat = mean + exact_dot(squares, second)
    stat_ref[...] = jnp.broadcast_to(stat[0:1], stat_ref.shape)


def act_kernel(
    feats_ref, gain_ref, bias_ref, stats_ref, up_ref, later_ref, above_ref, below_ref, weight_ref,
    act_ref, sums_ref, norm_ref, slabs, acc,
):
    step = pl.program_id(0)
    time_tap = step // 3
    row_tap = step % 3
    time_index = lax.axis_index("tm")
    row_index = lax.axis_index("rows")
    positions, chans = acc.shape
    cols = up_ref.shape[1]

    @pl.when(step == 0)
    def _():
        acc[...] = jnp.zeros_like(acc)
        more = (time_index < lax.axis_size("tm") - 1).astype(F32)
        up_ok = (row_index > 0).astype(F32)
        down_ok = (row_index < lax.axis_size("rows") - 1).astype(F32)
        for f in range(4):
            own = up_ref[f] if f < 2 else later_ref[f - 2]
            tail = jnp.float32(1.0) if f < 2 else more
            for r, slab, keep in ((0, above_ref[f], up_ok), (1, own, None), (2, below_ref[f], down_ok)):
                scale = tail if keep is None else keep * tail
                slab = (slab.astype(F32) * scale).astype(BF16)
                for c, moved in enumerate(col_shifts(slab)):
                    slabs[c, r, f] = moved

    def product(slab, c):
        return lax.dot_general(
            slab, weight_ref[0, 0, c], (((1,), (1,)), ((), ())), preferred_element_type=F32
        )

    total = acc[...]
    for c in range(3):
        slab = slabs[c, 2 - row_tap, pl.ds(2 - time_tap, 2)].reshape(positions, -1)
        total = total + product(slab, c)
    acc[...] = total

    @pl.when(jnp.logical_and(time_index == 0, time_tap == 0))
    def _():
        for c in range(3):
            both = slabs[c, 2 - row_tap, pl.ds(0, 2)].reshape(positions, -1)
            both = product(both, c)
            acc[0:cols, :] += both[0:cols] + both[cols:]

    @pl.when(jnp.logical_and(time_index == 0, time_tap == 1))
    def _():
        for c in range(3):
            acc[0:cols, :] += product(slabs[c, 2 - row_tap, 0], c)

    @pl.when(step == pl.num_programs(0) - 1)
    def _():
        stats = stats_ref[...]
        devices = stats.shape[0]
        size = chans // GROUPS
        first = members(chans, 0)
        second = members(chans, GROUPS)
        centre = jnp.sum(stats, axis=0, keepdims=True) / devices
        spans = stats - centre
        spans = jnp.sum(spans * spans, axis=0, keepdims=True)
        dims = ((1,), (1,))
        parts = exact_dot(jnp.broadcast_to(jnp.sum(stats, axis=0, keepdims=True), (8, 128)), second, dims)
        parts = parts / (devices * positions * size)
        parts = parts + exact_dot(jnp.broadcast_to(spans, (8, 128)), first, dims) / devices
        inverse = lax.rsqrt(parts + EPS)
        centre = exact_dot(jnp.broadcast_to(centre, (8, 128)), first, dims)
        norm_ref[0:8] = centre
        norm_ref[8:16] = inverse
        normed = (feats_ref[...].astype(F32) - centre[0:1]) * inverse[0:1]
        preact = normed * gain_ref[...] + bias_ref[...]
        sig = 1.0 / (1.0 + jnp.exp(-preact))
        act = acc[...] * sig * (1.0 + preact * (1.0 - sig))
        act_ref[...] = act
        gains = jnp.sum(act * normed, axis=0, keepdims=True)
        biases = jnp.sum(act, axis=0, keepdims=True)
        pieces = chans // 128
        for p in range(pieces):
            sums_ref[p : p + 1, :] = gains[:, p * 128 : (p + 1) * 128]
            sums_ref[pieces + p : pieces + p + 1, :] = biases[:, p * 128 : (p + 1) * 128]


def weight_kernel(teams, load_ref, halo_ref, norm_ref, gain_ref, bias_ref, sums_ref, out_ref, hidden, acc):
    time_index = lax.axis_index("tm")
    rows = load_ref.shape[1]
    cols = hidden.shape[2]
    chans = gain_ref.shape[1]
    wide = chans // TEAM
    step = chans // teams
    spot = time_index % TEAM
    lane = iota((chans, wide), 1)
    mover = (iota((chans, wide), 0) == lane // step * (step * TEAM) + spot * step + lane % step).astype(F32)

    def slice_of(value):
        return exact_dot(value, mover)[0:1]

    centre = slice_of(norm_ref[0:8])
    inverse = slice_of(norm_ref[8:16])
    gain = slice_of(jnp.broadcast_to(gain_ref[...], (8, chans)))
    bias = slice_of(jnp.broadcast_to(bias_ref[...], (8, chans)))

    def silu(value):
        preact = (value.astype(F32) - centre) * inverse * gain + bias
        return (preact * (1.0 / (1.0 + jnp.exp(-preact)))).astype(BF16)

    frames = 2 * TEAM
    for f in range(frames + 2):
        hidden[f, 0] = jnp.zeros(hidden.shape[2:], BF16)
        hidden[f, rows + 1] = jnp.zeros(hidden.shape[2:], BF16)
    for j in range(TEAM):
        for r in range(rows):
            for f in range(2):
                hidden[2 + 2 * j + f, 1 + r] = silu(load_ref[j, r, f * cols : (f + 1) * cols, :])
    for r in range(rows):
        for f in range(2):
            source = jnp.where(time_index < TEAM, load_ref[0, r, 0:cols, :], halo_ref[r, f * cols : (f + 1) * cols, :])
            hidden[f, 1 + r] = silu(source)

    lanes = iota((cols, 128), 1) < 64
    for j in range(TEAM):
        halves = [[], []]
        for r in range(rows):
            pair = load_ref[j, r, 2 * cols : 3 * cols, :].astype(F32)
            row = iota(pair.shape, 0)
            ahead = jnp.where(row < cols - 1, pltpu.roll(pair, cols - 1, 0), 0.0)
            behind = jnp.where(row > 0, pltpu.roll(pair, 1, 0), 0.0)
            left = jnp.where(lanes, ahead, pltpu.roll(pair, 64, 1))
            right = jnp.where(lanes, pltpu.roll(ahead, 64, 1), pair)
            halves[0].append(jnp.concatenate([left, behind[:, 0:64]], axis=1))
            halves[1].append(jnp.concatenate([right, behind[:, 64:128]], axis=1))
        for f in range(2):
            ups = jnp.concatenate(halves[f], axis=0).astype(BF16)
            taps = [
                hidden[2 * j + f + a, b : b + rows].reshape(rows * cols, wide) for a in range(3) for b in range(3)
            ]
            term = lax.dot_general(
                ups, jnp.concatenate(taps, axis=1), (((0,), (0,)), ((), ())), preferred_element_type=F32
            )
            if j == 0 and f == 0:
                acc[...] = term
            else:
                acc[...] += term

    groups = out_ref.shape[0]
    tail = None
    for ab in range(9):
        block = acc[:, ab * wide : (ab + 1) * wide].T
        out_ref[:, ab * step : (ab + 1) * step, :] = block[:, 0:128].reshape(groups, step, 128)
        last = block[:, 128:192]
        if ab % 2 == 0:
            tail = last
        if ab % 2 == 1 or ab == 8:
            both = jnp.concatenate([tail, last], axis=1)
            at = (9 + ab // 2) * step
            out_ref[:, at : at + step, :] = both.reshape(groups, step, 128)
    out_ref[:, 14 * step :, :] = jnp.broadcast_to(sums_ref[...][None], (groups,) + sums_ref.shape)


def unpack_kernel(load_ref, grad_ref, sums_ref):
    step = grad_ref.shape[2]
    total = load_ref[0]
    for g in range(1, load_ref.shape[0]):
        total = total + load_ref[g]
    for ab in range(9):
        part = total[ab * step : (ab + 1) * step]
        grad_ref[ab, 0] = part[:, 0:64]
        grad_ref[ab, 1] = part[:, 64:128]
        at = (9 + ab // 2) * step
        side = 64 * (ab % 2)
        grad_ref[ab, 2] = total[at : at + step, side : side + 64]
    sums_ref[...] = jnp.broadcast_to(total[14 * step :][None], sums_ref.shape)


def final_kernel(count, sums_ref, act_ref, feats_ref, norm_ref, gain_ref, out_ref, gain_out_ref, bias_out_ref):
    chans = gain_ref.shape[1]
    pieces = chans // 128
    total = sums_ref[0]
    for g in range(1, sums_ref.shape[0]):
        total = total + sums_ref[g]
    gains = jnp.concatenate([total[p : p + 1] for p in range(pieces)], axis=1)
    biases = jnp.concatenate([total[pieces + p : pieces + p + 1] for p in range(pieces)], axis=1)
    gain_out_ref[...] = gains
    bias_out_ref[...] = biases
    gain = gain_ref[...]
    owner = members(chans, 0)

    def spread(value):
        value = exact_dot(jnp.broadcast_to(value, (8, chans)), owner) / count
        return exact_dot(value, owner, ((1,), (1,)))[0:1]

    first = spread(gain * biases)
    second = spread(gain * gains)
    centre = norm_ref[0:1]
    inverse = norm_ref[8:9]
    normed = (feats_ref[...].astype(F32) - centre) * inverse
    out_ref[...] = (inverse * (act_ref[...] * gain - first - normed * second)).astype(BF16)


def on_device(features, norm_gain, norm_bias, weight, upstream):
    frames, rows_dev, cols, chans = features.shape
    outs = upstream.shape[3]
    tms = lax.axis_size("tm")
    rows = lax.axis_size("rows")
    devices = tms * rows
    positions = frames * rows_dev * cols
    step = chans // tms
    groups = tms // TEAM
    wide = chans // TEAM
    count = positions * devices * (chans // GROUPS)
    params = pltpu.CompilerParams(vmem_limit_bytes=60 * 1024 * 1024)

    feats = features.reshape(positions, chans)
    ups = upstream.reshape(frames, cols, outs)
    gain = norm_gain.reshape(1, chans)
    bias = norm_bias.reshape(1, chans)

    later = lax.ppermute(ups, "tm", [((i + 1) % tms, i) for i in range(tms)])
    four = jnp.concatenate([ups, later], axis=0)
    above = lax.ppermute(four, "rows", [(i, (i + 1) % rows) for i in range(rows)])
    below = lax.ppermute(four, "rows", [((i + 1) % rows, i) for i in range(rows)])

    load, stat = pl.pallas_call(
        functools.partial(pack_kernel, tms),
        out_shape=(
            jax.ShapeDtypeStruct((TEAM, rows, positions + cols, wide), BF16),
            jax.ShapeDtypeStruct((devices, 128), F32),
        ),
        compiler_params=params,
        name="pack",
    )(feats, ups)
    teams = [[TEAM * rows * g + i for i in range(TEAM * rows)] for g in range(groups)]
    load = lax.all_to_all(
        load.reshape(TEAM * rows, positions + cols, wide),
        ("tm", "rows"), 0, 0, tiled=True, axis_index_groups=teams,
    ).reshape(TEAM, rows, positions + cols, wide)
    halo = lax.ppermute(load[TEAM - 1, :, :positions], "tm", [(i, (i + TEAM) % tms) for i in range(tms)])
    stats = lax.all_to_all(stat, ("tm", "rows"), 0, 0, tiled=True)

    whole = lambda shape: pl.BlockSpec(shape, lambda s: (0,) * len(shape))
    act, sums, norm = pl.pallas_call(
        act_kernel,
        grid=(9,),
        in_specs=[
            whole((positions, chans)), whole((1, chans)), whole((1, chans)), whole((devices, 128)),
            whole((2, cols, outs)), whole((2, cols, outs)), whole((4, cols, outs)), whole((4, cols, outs)),
            pl.BlockSpec((1, 1, 3, chans, outs), lambda s: (s // 3, s % 3, 0, 0, 0)),
        ],
        out_specs=(whole((positions, chans)), whole((8, 128)), whole((16, chans))),
        out_shape=(
            jax.ShapeDtypeStruct((positions, chans), F32),
            jax.ShapeDtypeStruct((8, 128), F32),
            jax.ShapeDtypeStruct((16, chans), F32),
        ),
        scratch_shapes=[pltpu.VMEM((3, 3, 4, cols, outs), BF16), pltpu.VMEM((positions, chans), F32)],
        compiler_params=params,
        name="act",
    )(feats, gain, bias, stats, ups, later, above, below, weight)

    part = pl.pallas_call(
        functools.partial(weight_kernel, tms),
        out_shape=jax.ShapeDtypeStruct((groups, 14 * step + 8, 128), F32),
        scratch_shapes=[
            pltpu.VMEM((2 * TEAM + 2, rows + 2, cols, wide), BF16),
            pltpu.VMEM((3 * 64, 9 * wide), F32),
        ],
        compiler_params=params,
        name="wgrad",
    )(load, halo, norm, gain, bias, sums)
    ranks = [[TEAM * g + j for g in range(groups)] for j in range(TEAM)]
    part = lax.all_to_all(part, "tm", 0, 0, tiled=True, axis_index_groups=ranks)

    grad_weight, sums = pl.pallas_call(
        unpack_kernel,
        out_shape=(
            jax.ShapeDtypeStruct((9, 3, step, outs // rows), F32),
            jax.ShapeDtypeStruct((TEAM * rows, 8, 128), F32),
        ),
        compiler_params=params,
        name="unpack",
    )(part)
    sums = lax.all_to_all(sums, ("tm", "rows"), 0, 0, tiled=True, axis_index_groups=teams)

    grad_features, grad_gain, grad_bias = pl.pallas_call(
        functools.partial(final_kernel, count),
        out_shape=(
            jax.ShapeDtypeStruct((positions, chans), BF16),
            jax.ShapeDtypeStruct((1, chans), F32),
            jax.ShapeDtypeStruct((1, chans), F32),
        ),
        compiler_params=params,
        name="final",
    )(sums, act, feats, norm, gain)
    return (
        grad_features.reshape(features.shape),
        grad_weight.reshape(3, 3, 3, step, outs // rows),
        grad_gain.reshape(chans),
        grad_bias.reshape(chans),
    )


def solution(mesh):
    in_specs = (P("tm", "rows", None, None), P(), P(), P(), P("tm", "rows", None, None))
    out_specs = (P("tm", "rows", None, None), P(None, None, None, "tm", "rows"), P(), P())
    return jax.shard_map(
        on_device, mesh=mesh, in_specs=in_specs, out_specs=out_specs, check_vma=False
    )
```

time: 457 us -> 137 us (0.30)
  blocking collectives: 227 us -> 67 us
  waiting for transfers between devices: 129 us -> 26.2 us
  matrix products: 38.5 us -> 0 us
  Pallas kernels: 0 us -> 27 us
  between operations: 14.6 us -> 0.69 us
  local copies, waits for them, and re-layouts: 15.4 us -> 1.55 us
  starting transfers between devices: 21.9 us -> 13.5 us
  other arithmetic: 8.17 us -> 0.03 us
    psum x3 -> x0, blocking collectives: 227 us -> none  [the longest x1 78.8 us: on_device(): total_sum = lax.psum(selector[:, None] * local_sum, ('tm', 'rows'))]
    reduce_scatter x1 -> x0, waiting for transfers between devices: 83.4 us -> none  [on_device(): lax.psum_scatter(local_grad, 'tm', scatter_dimension=3, tiled=True)]
    all_to_all x0 -> x3, blocking collectives: none -> 67 us  [the longest x1 31.5 us: on_device(): part = lax.all_to_all(part, 'tm', 0, 0, tiled=True, axis_index_groups=ranks)]
    dot_general x54 -> x0, matrix products: 38.5 us -> none  [the longest x27 31 us: on_device(): lax.dot_general(slab, up_flat, (((0,), (0,)), ((), ())), preferred_elemen...]
    pallas_call x0 -> x5, Pallas kernels: none -> 27 us  [the longest x1 11.4 us: on_device(): pl.pallas_call(act_kernel, grid=(9,), in_specs=[whole((positions, chans))...]
    unnamed x3 -> x0, waiting for transfers between devices: 22.4 us -> none
    ppermute x6 -> x4, starting transfers between devices: 21.8 us -> 5.99 us  [the longest x1 3.06 us: on_device(): lax.ppermute(load[TEAM - 1, :, :positions], 'tm', [(i, (i + TEAM) % tms)...]
    unnamed x19 -> x14, local copies, waits for them, and re-layouts: 13.9 us -> 1.53 us
  transfers between devices with their start and end apart: 8 -> 5, of which waited for: 7 -> 1; matrix products, arithmetic and copies ran while one was open for 1% -> 0% of each run, Pallas kernels for 0% -> 8%
where the time goes in v1:
time: 137 us; the launch traced here: 136 us
  blocking collectives  67 us (49%)
  Pallas kernels  27 us (20%)
  waiting for transfers between devices  26.2 us (19%)
  starting transfers between devices  13.5 us (10%)
  local copies, waits for them, and re-layouts  1.55 us (1%)
    all_to_all x1, blocking collectives, on_device(): part = lax.all_to_all(part, 'tm', 0, 0, tiled=True, axis_index_groups=ranks)  31.5 us
    ppermute x1, waiting for transfers between devices, on_device(): later = lax.ppermute(ups, 'tm', [((i + 1) % tms, i) for i in range(tms)])  26.2 us
    all_to_all x1, blocking collectives, on_device(): stats = lax.all_to_all(stat, ('tm', 'rows'), 0, 0, tiled=True)  23.4 us
    all_to_all x1, blocking collectives, on_device(): lax.all_to_all(sums, ('tm', 'rows'), 0, 0, tiled=True, axis_index_groups=...  12.1 us
    pallas_call x1, Pallas kernels, on_device(): pl.pallas_call(act_kernel, grid=(9,), in_specs=[whole((positions, chans))...  11.4 us
    all_to_all x1, starting transfers between devices, on_device(): lax.all_to_all(load.reshape(TEAM * rows, positions + cols, wide), ('tm',...  7.47 us
    pallas_call x1, Pallas kernels, on_device(): pl.pallas_call(functools.partial(weight_kernel, tms), out_shape=jax.Shape...  7.18 us
    pallas_call x1, Pallas kernels, on_device(): pl.pallas_call(functools.partial(pack_kernel, tms), out_shape=(jax.ShapeD...  3.41 us
  transfers between devices with their start and end apart: 5, of which 1 were waited for; matrix products, arithmetic and copies ran while one was open for 0% of the time, Pallas kernels for 8%

profile of v1, /device:TPU:1, one launch (start us, length us, event | category | flops | bytes accessed | tf_op | source)
XLA Modules:
  0.0 135.9 jit_solution(16481112233807635607)
XLA Ops:
  0.6 3.4 %pack.1 = (bf16[4,4,480,128]{3,2,1,0:T(8,128)(2,1)}, f32[256,128]{1,0:T(8,128)}) custom-call(bf16[320,512]{1,0:T(8,128)(2,1)} %bitcast.20, bf16[2,160,256]{2,1,0:T(8,128)(2,1)} %bitcast.24), custom_call_target="tpu_custom_call" | custom-call | tf_op jit(solution)/shard_map/pack/pallas_call | solution.py:291
  4.0 7.5 %all-to-all-start = ((bf16[16,480,128]{2,1,0:T(8,128)(2,1)}), bf16[16,480,128]{2,1,0:T(8,128)(2,1)S(1)}, u32[]{:S(2)}, u32[]{:S(2)}) async-start(bf16[16,480,128]{2,1,0:T(8,128)(2,1)} %bitcast.23), calls=%async_computation | async-start | bytes 3932160 | tf_op jit(solution)/shard_map/all_to_all | solution.py:301
  11.5 0.2 collective-permute-start.1
  11.7 26.2 %collective-permute-done.1.later_ref = bf16[2,160,256]{2,1,0:T(8,128)(2,1)S(1)} collective-permute-done((bf16[2,160,256]{2,1,0:T(8,128)(2,1)S(1)}, bf16[2,160,256]{2,1,0:T(8,128)(2,1)S(1)}, u32[]{:S(2)}, u32[]{:S(2)}) %collective-permute-start.1) | collective-permute-done | bytes 163872 | tf_op jit(solution)/shard_map/ppermute | solution.py:286
  37.9 1.6 %collective-permute-start.2 = (bf16[4,160,256]{2,1,0:T(8,128)(2,1)S(1)}, bf16[4,160,256]{2,1,0:T(8,128)(2,1)S(1)}, u32[]{:S(2)}, u32[]{:S(2)}) collective-permute-start(bf16[4,160,256]{2,1,0:T(8,128)(2,1)S(1)} %pad_maximum_fusion), channel_id=1, source_target_pairs={{0,1},{1,2},{2,3},{3,0},{4,5},{5,6},{6,7},{7,4},{8,9},{9,10},{10,1... | collective-permute-start | bytes 983048 | tf_op jit(solution)/shard_map/ppermute | solution.py:288
  39.5 1.1 collective-permute-start.3
  40.7 0.0 all-to-all-done
  40.7 3.1 %collective-permute-start = (bf16[4,320,128]{2,1,0:T(8,128)(2,1)S(1)}, bf16[4,320,128]{2,1,0:T(8,128)(2,1)S(1)}, u32[]{:S(2)}, u32[]{:S(2)}) collective-permute-start(bf16[4,320,128]{2,1,0:T(8,128)(2,1)S(1)} %slice_bitcast_fusion), channel_id=1, source_target_pairs={{0,16},{4,20},{8,24},{12,28},{16,32},{20,36},{24,40},{28,44},{32,4... | collective-permute-start | bytes 983048 | tf_op jit(solution)/shard_map/ppermute | solution.py:305
  43.7 23.4 %all_to_all.26 = f32[256,1,128]{2,1,0:T(1,128)} all-to-all(f32[256,1,128]{2,1,0:T(1,128)S(1)} %bitcast.29), channel_id=1, replica_groups=mesh['tm'=64,'rows'=4] {'tm','rows'}, dimensions={0} | all-to-all | bytes 262144 | tf_op jit(solution)/shard_map/all_to_all | solution.py:306
  67.2 0.0 collective-permute-done.2.above_ref
  67.2 0.0 collective-permute-done.3.below_ref
  67.2 0.0 copy-start.5
  67.2 0.0 copy-done.2
  67.2 0.7 copy-done.4
  67.9 0.1 copy-done.5
  68.0 11.4 %act.1 = (f32[320,512]{1,0:T(8,128)}, f32[8,128]{1,0:T(8,128)}, f32[16,512]{1,0:T(8,128)}) custom-call(bf16[320,512]{1,0:T(8,128)(2,1)} %bitcast.21, f32[1,512]{1,0:T(1,128)} %bitcast.30, f32[1,512]{1,0:T(1,128)} %bitcast.33, f32[256,128]{1,0:T(8,128)} %bitcast.28, bf16[2,160,256]{2,1,0:T(8,128)(2,1)} %bitcast.25, bf16[2,160,256]{2,1,0:T(8,128)(2,1)} %copy-done.2, ...), custom_call_target="tpu_custom_call" | custom-call | tf_op jit(solution)/shard_map/act/pallas_call | solution.py:309
  79.4 0.0 collective-permute-done.halo_ref
  79.4 0.0 copy-start.3
  79.4 0.7 copy-done.3
  80.1 7.2 %wgrad.1 = f32[16,120,128]{2,1,0:T(8,128)} custom-call(bf16[4,4,480,128]{3,2,1,0:T(8,128)(2,1)} %bitcast.19, bf16[4,320,128]{2,1,0:T(8,128)(2,1)} %copy-done.3, f32[16,512]{1,0:T(8,128)} %get-tuple-element.16.norm_ref, f32[1,512]{1,0:T(1,128)} %bitcast.31, f32[1,512]{1,0:T(1,128)} %bitcast.34, f32[8,128]{1,0:T(8,128)} %get-tuple-element.17.sums_ref), custom_call_target="tpu_custom_call" | custom-call | tf_op jit(solution)/shard_map/wgrad/pallas_call | solution.py:328
  87.3 31.5 %all_to_all.27.load_ref = f32[16,120,128]{2,1,0:T(8,128)} all-to-all(f32[16,120,128]{2,1,0:T(8,128)} %wgrad.1), channel_id=1, replica_groups={{0,16,32,48,64,80,96,112,128,144,160,176,192,208,224,240},{4,20,36,52,6..., dimensions={0} | all-to-all | bytes 1966080 | tf_op jit(solution)/shard_map/all_to_all | solution.py:339
  118.8 2.0 %unpack.1 = (f32[9,3,8,64]{3,2,1,0:T(8,128)}, f32[16,8,128]{2,1,0:T(8,128)}) custom-call(f32[16,120,128]{2,1,0:T(8,128)} %all_to_all.27.load_ref), custom_call_target="tpu_custom_call" | custom-call | tf_op jit(solution)/shard_map/unpack/pallas_call | solution.py:341
  120.8 12.1 %all_to_all.28.sums_ref = f32[16,8,128]{2,1,0:T(8,128)} all-to-all(f32[16,8,128]{2,1,0:T(8,128)} %get-tuple-element.18), channel_id=1, replica_groups={{0,1,2,3,4,5,6,7,8,9,10,11,12,13,14,15},{16,17,18,19,20,21,22,23,24,25,..., dimensions={0} | all-to-all | bytes 131072 | tf_op jit(solution)/shard_map/all_to_all | solution.py:350
  132.9 3.1 %final.1 = (bf16[320,512]{1,0:T(8,128)(2,1)}, f32[1,512]{1,0:T(1,128)}, f32[1,512]{1,0:T(1,128)}) custom-call(f32[16,8,128]{2,1,0:T(8,128)} %all_to_all.28.sums_ref, f32[320,512]{1,0:T(8,128)} %get-tuple-element.19.act_ref, bf16[320,512]{1,0:T(8,128)(2,1)} %bitcast.22, f32[16,512]{1,0:T(8,128)} %get-tuple-element.16.norm_ref, f32[1,512]{1,0:T(1,128)} %bitcast.32), custom_call_target="tpu_custom_call" | custom-call | tf_op jit(solution)/shard_map/final/pallas_call | solution.py:352
  (10 shorter events, 0.1 us)
Async XLA Ops:
  4.0 7.5 %copy-start.1 = (bf16[2,1,160,256]{3,2,1,0:T(8,128)(2,1)S(1)}, bf16[2,1,160,256]{3,2,1,0:T(8,128)(2,1)}, u32[]{:S(2)}) copy-start(bf16[2,1,160,256]{3,2,1,0:T(8,128)(2,1)} %param.9) | copy-start | bytes 491524
  4.0 39.7 %copy-start.6 = (f32[256,128]{1,0:T(8,128)S(1)}, f32[256,128]{1,0:T(8,128)}, u32[]{:S(2)}) copy-start(f32[256,128]{1,0:T(8,128)} %get-tuple-element.15) | copy-start | bytes 393220
  4.0 36.6 %all-to-all-start = ((bf16[16,480,128]{2,1,0:T(8,128)(2,1)}), bf16[16,480,128]{2,1,0:T(8,128)(2,1)S(1)}, u32[]{:S(2)}, u32[]{:S(2)}) async-start(bf16[16,480,128]{2,1,0:T(8,128)(2,1)} %bitcast.23), calls=%async_computation | async-start | bytes 3932160 | tf_op jit(solution)/shard_map/all_to_all | solution.py:301
  11.5 26.3 %collective-permute-start.1 = (bf16[2,160,256]{2,1,0:T(8,128)(2,1)S(1)}, bf16[2,160,256]{2,1,0:T(8,128)(2,1)S(1)}, u32[]{:S(2)}, u32[]{:S(2)}) collective-permute-start(bf16[2,160,256]{2,1,0:T(8,128)(2,1)S(1)} %bitcast.26), channel_id=1, source_target_pairs={{4,0},{8,4},{12,8},{16,12},{20,16},{24,20},{28,24},{32,28},{36,32}... | collective-permute-start | bytes 491528 | tf_op jit(solution)/shard_map/ppermute | solution.py:286
  37.9 29.3 %copy-start.2 = (bf16[2,160,256]{2,1,0:T(8,128)(2,1)}, bf16[2,160,256]{2,1,0:T(8,128)(2,1)S(1)}, u32[]{:S(2)}) copy-start(bf16[2,160,256]{2,1,0:T(8,128)(2,1)S(1)} %collective-permute-done.1.later_ref) | copy-start | bytes 491524
  37.9 29.3 %collective-permute-start.2 = (bf16[4,160,256]{2,1,0:T(8,128)(2,1)S(1)}, bf16[4,160,256]{2,1,0:T(8,128)(2,1)S(1)}, u32[]{:S(2)}, u32[]{:S(2)}) collective-permute-start(bf16[4,160,256]{2,1,0:T(8,128)(2,1)S(1)} %pad_maximum_fusion), channel_id=1, source_target_pairs={{0,1},{1,2},{2,3},{3,0},{4,5},{5,6},{6,7},{7,4},{8,9},{9,10},{10,1... | collective-permute-start | bytes 983048 | tf_op jit(solution)/shard_map/ppermute | solution.py:288
  39.5 27.7 %collective-permute-start.3 = (bf16[4,160,256]{2,1,0:T(8,128)(2,1)S(1)}, bf16[4,160,256]{2,1,0:T(8,128)(2,1)S(1)}, u32[]{:S(2)}, u32[]{:S(2)}) collective-permute-start(bf16[4,160,256]{2,1,0:T(8,128)(2,1)S(1)} %pad_maximum_fusion), channel_id=1, source_target_pairs={{1,0},{2,1},{3,2},{0,3},{5,4},{6,5},{7,6},{4,7},{9,8},{10,9},{11,1... | collective-permute-start | bytes 983048 | tf_op jit(solution)/shard_map/ppermute | solution.py:289
  40.7 38.7 %copy-start = (bf16[16,480,128]{2,1,0:T(8,128)(2,1)}, bf16[16,480,128]{2,1,0:T(8,128)(2,1)S(1)}, u32[]{:S(2)}) copy-start(bf16[16,480,128]{2,1,0:T(8,128)(2,1)S(1)} %all-to-all-done) | copy-start | bytes 5898244
  40.7 38.7 %collective-permute-start = (bf16[4,320,128]{2,1,0:T(8,128)(2,1)S(1)}, bf16[4,320,128]{2,1,0:T(8,128)(2,1)S(1)}, u32[]{:S(2)}, u32[]{:S(2)}) collective-permute-start(bf16[4,320,128]{2,1,0:T(8,128)(2,1)S(1)} %slice_bitcast_fusion), channel_id=1, source_target_pairs={{0,16},{4,20},{8,24},{12,28},{16,32},{20,36},{24,40},{28,44},{32,4... | collective-permute-start | bytes 983048 | tf_op jit(solution)/shard_map/ppermute | solution.py:305
  67.2 0.7 copy-start.4
  67.2 0.8 copy-start.5
  79.4 0.7 copy-start.3

commit v2 on v1

--- a/solution.py
+++ b/solution.py
@@ -6,6 +6,7 @@
 from jax.experimental import pallas as pl
 from jax.experimental.pallas import tpu as pltpu
 from jax.sharding import PartitionSpec as P
+
 
 GROUPS = 32
 EPS = 1e-06
@@ -38,7 +39,7 @@
     return ahead, slab, behind
 
 
-def pack_kernel(teams, feats_ref, up_ref, load_ref, stat_ref):
+def pack_kernel(teams, feats_ref, up_ref, load_ref):
     positions, chans = feats_ref.shape
     cols = up_ref.shape[1]
     rows = load_ref.shape[1]
@@ -65,24 +66,48 @@
     diffs = floats - exact_dot(mean, first, ((1,), (1,)))[0:1]
     squares = jnp.broadcast_to(jnp.sum(diffs * diffs, axis=0, keepdims=True), (8, chans))
     stat = mean + exact_dot(squares, second)
-    stat_ref[...] = jnp.broadcast_to(stat[0:1], stat_ref.shape)
-
-
-def act_kernel(
-    feats_ref, gain_ref, bias_ref, stats_ref, up_ref, later_ref, above_ref, below_ref, weight_ref,
-    act_ref, sums_ref, norm_ref, slabs, acc,
-):
+    high = stat.astype(BF16).astype(F32)
+    mid = (stat - high).astype(BF16).astype(F32)
+    low = stat - high - mid
+    row = iota((8, 128), 0)
+    parts = jnp.where(row == 0, high, jnp.where(row == 1, mid, jnp.where(row == 2, low, 0.0)))
+    parts = jnp.concatenate([parts, jnp.zeros_like(parts)], axis=0).astype(BF16)
+    for r in range(rows):
+        for j in range(TEAM):
+            load_ref[j, r, positions + cols :, :] = parts
+
+
+def combine_kernel(count, load_ref, dense_ref, out_ref):
+    stats = []
+    for j in range(load_ref.shape[0]):
+        for r in range(load_ref.shape[1]):
+            parts = load_ref[j, r].astype(F32)
+            stats.append(parts[0:1] + parts[1:2] + parts[2:3])
+    total = stats[0]
+    for stat in stats[1:]:
+        total = total + stat
+    mean = total / len(stats)
+    spans = jnp.zeros_like(mean)
+    for stat in stats:
+        spans = spans + (stat - mean) * (stat - mean)
+    lane = iota((8, 128), 1)
+    moved = pltpu.roll(jnp.broadcast_to(spans, (8, 128)), GROUPS, 1)
+    result = jnp.where(lane < GROUPS, jnp.broadcast_to(mean, (8, 128)), total + count * moved)
+    out_ref[...] = jnp.broadcast_to(result[None], out_ref.shape)
+
+
+def dense_kernel(up_ref, later_ref, above_ref, below_ref, weight_ref, out_ref, slabs):
     step = pl.program_id(0)
     time_tap = step // 3
     row_tap = step % 3
     time_index = lax.axis_index("tm")
     row_index = lax.axis_index("rows")
-    positions, chans = acc.shape
+    positions = out_ref.shape[0]
     cols = up_ref.shape[1]
 
     @pl.when(step == 0)
     def _():
-        acc[...] = jnp.zeros_like(acc)
+        out_ref[...] = jnp.zeros_like(out_ref)
         more = (time_index < lax.axis_size("tm") - 1).astype(F32)
         up_ok = (row_index > 0).astype(F32)
         down_ok = (row_index < lax.axis_size("rows") - 1).astype(F32)
@@ -100,56 +125,71 @@
             slab, weight_ref[0, 0, c], (((1,), (1,)), ((), ())), preferred_element_type=F32
         )
 
-    total = acc[...]
+    total = out_ref[...]
     for c in range(3):
         slab = slabs[c, 2 - row_tap, pl.ds(2 - time_tap, 2)].reshape(positions, -1)
         total = total + product(slab, c)
-    acc[...] = total
+    out_ref[...] = total
 
     @pl.when(jnp.logical_and(time_index == 0, time_tap == 0))
     def _():
         for c in range(3):
             both = slabs[c, 2 - row_tap, pl.ds(0, 2)].reshape(positions, -1)
             both = product(both, c)
-            acc[0:cols, :] += both[0:cols] + both[cols:]
+            out_ref[0:cols, :] += both[0:cols] + both[cols:]
 
     @pl.when(jnp.logical_and(time_index == 0, time_tap == 1))
     def _():
         for c in range(3):
-            acc[0:cols, :] += product(slabs[c, 2 - row_tap, 0], c)
-
-    @pl.when(step == pl.num_programs(0) - 1)
-    def _():
-        stats = stats_ref[...]
-        devices = stats.shape[0]
-        size = chans // GROUPS
-        first = members(chans, 0)
-        second = members(chans, GROUPS)
-        centre = jnp.sum(stats, axis=0, keepdims=True) / devices
-        spans = stats - centre
-        spans = jnp.sum(spans * spans, axis=0, keepdims=True)
-        dims = ((1,), (1,))
-        parts = exact_dot(jnp.broadcast_to(jnp.sum(stats, axis=0, keepdims=True), (8, 128)), second, dims)
-        parts = parts / (devices * positions * size)
-        parts = parts + exact_dot(jnp.broadcast_to(spans, (8, 128)), first, dims) / devices
-        inverse = lax.rsqrt(parts + EPS)
-        centre = exact_dot(jnp.broadcast_to(centre, (8, 128)), first, dims)
-        norm_ref[0:8] = centre
-        norm_ref[8:16] = inverse
-        normed = (feats_ref[...].astype(F32) - centre[0:1]) * inverse[0:1]
-        preact = normed * gain_ref[...] + bias_ref[...]
-        sig = 1.0 / (1.0 + jnp.exp(-preact))
-        act = acc[...] * sig * (1.0 + preact * (1.0 - sig))
-        act_ref[...] = act
-        gains = jnp.sum(act * normed, axis=0, keepdims=True)
-        biases = jnp.sum(act, axis=0, keepdims=True)
-        pieces = chans // 128
-        for p in range(pieces):
-            sums_ref[p : p + 1, :] = gains[:, p * 128 : (p + 1) * 128]
-            sums_ref[pieces + p : pieces + p + 1, :] = biases[:, p * 128 : (p + 1) * 128]
-
-
-def weight_kernel(teams, load_ref, halo_ref, norm_ref, gain_ref, bias_ref, sums_ref, out_ref, hidden, acc):
+            out_ref[0:cols, :] += product(slabs[c, 2 - row_tap, 0], c)
+
+
+def norm_rows(stats_ref, chans, positions):
+    stats = jnp.concatenate([stats_ref[g, 0:1] for g in range(stats_ref.shape[0])], axis=0)
+    devices = stats.shape[0]
+    size = chans // GROUPS
+    first = members(chans, 0)
+    second = members(chans, GROUPS)
+    total = jnp.sum(stats, axis=0, keepdims=True)
+    centre = total / devices
+    spans = stats - centre
+    spans = jnp.sum(spans * spans, axis=0, keepdims=True)
+    dims = ((1,), (1,))
+    parts = exact_dot(jnp.broadcast_to(total, (8, 128)), second, dims) / (devices * positions * size)
+    parts = parts + exact_dot(jnp.broadcast_to(spans, (8, 128)), first, dims) / devices
+    inverse = lax.rsqrt(parts + EPS)
+    centre = exact_dot(jnp.broadcast_to(centre, (8, 128)), first, dims)
+    return centre, inverse
+
+
+def act_kernel(positions, feats_ref, gain_ref, bias_ref, stats_ref, dense_ref, act_ref, sums_ref, norm_ref):
+    chans = gain_ref.shape[1]
+    centre, inverse = norm_rows(stats_ref, chans, positions)
+    norm_ref[0:8] = centre
+    norm_ref[8:16] = inverse
+    centre = centre[0:1]
+    inverse = inverse[0:1]
+    normed = (feats_ref[...].astype(F32) - centre) * inverse
+    preact = normed * gain_ref[...] + bias_ref[...]
+    sig = 1.0 / (1.0 + jnp.exp(-preact))
+    act = dense_ref[...] * sig * (1.0 + preact * (1.0 - sig))
+    act_ref[...] = act
+    gains = jnp.sum(act * normed, axis=0, keepdims=True)
+    biases = jnp.sum(act, axis=0, keepdims=True)
+    pieces = chans // 128
+    rows = [gains[:, p * 128 : (p + 1) * 128] for p in range(pieces)]
+    rows = rows + [biases[:, p * 128 : (p + 1) * 128] for p in range(pieces)]
+    sums_ref[...] = jnp.broadcast_to(jnp.concatenate(rows, axis=0)[None], sums_ref.shape)
+
+
+def append_kernel(part_ref, load_ref, out_ref):
+    total = load_ref[0]
+    for g in range(1, load_ref.shape[0]):
+        total = total + load_ref[g]
+    out_ref[...] = jnp.broadcast_to(total[None], out_ref.shape)
+
+
+def weight_kernel(teams, load_ref, halo_ref, norm_ref, gain_ref, bias_ref, out_ref, hidden, acc):
     time_index = lax.axis_index("tm")
     rows = load_ref.shape[1]
     cols = hidden.shape[2]
@@ -222,10 +262,13 @@
             both = jnp.concatenate([tail, last], axis=1)
             at = (9 + ab // 2) * step
             out_ref[:, at : at + step, :] = both.reshape(groups, step, 128)
-    out_ref[:, 14 * step :, :] = jnp.broadcast_to(sums_ref[...][None], (groups,) + sums_ref.shape)
-
-
-def unpack_kernel(load_ref, grad_ref, sums_ref):
+
+
+def final_kernel(
+    count, load_ref, act_ref, feats_ref, norm_ref, gain_ref, out_ref, grad_ref, gain_out_ref, bias_out_ref
+):
+    chans = gain_ref.shape[1]
+    pieces = chans // 128
     step = grad_ref.shape[2]
     total = load_ref[0]
     for g in range(1, load_ref.shape[0]):
@@ -237,15 +280,7 @@
         at = (9 + ab // 2) * step
         side = 64 * (ab % 2)
         grad_ref[ab, 2] = total[at : at + step, side : side + 64]
-    sums_ref[...] = jnp.broadcast_to(total[14 * step :][None], sums_ref.shape)
-
-
-def final_kernel(count, sums_ref, act_ref, feats_ref, norm_ref, gain_ref, out_ref, gain_out_ref, bias_out_ref):
-    chans = gain_ref.shape[1]
-    pieces = chans // 128
-    total = sums_ref[0]
-    for g in range(1, sums_ref.shape[0]):
-        total = total + sums_ref[g]
+    total = total[14 * step :]
     gains = jnp.concatenate([total[p : p + 1] for p in range(pieces)], axis=1)
     biases = jnp.concatenate([total[pieces + p : pieces + p + 1] for p in range(pieces)], axis=1)
     gain_out_ref[...] = gains
@@ -288,42 +323,69 @@
     above = lax.ppermute(four, "rows", [(i, (i + 1) % rows) for i in range(rows)])
     below = lax.ppermute(four, "rows", [((i + 1) % rows, i) for i in range(rows)])
 
-    load, stat = pl.pallas_call(
+    length = positions + cols + 16
+    load = pl.pallas_call(
         functools.partial(pack_kernel, tms),
-        out_shape=(
-            jax.ShapeDtypeStruct((TEAM, rows, positions + cols, wide), BF16),
-            jax.ShapeDtypeStruct((devices, 128), F32),
-        ),
+        out_shape=jax.ShapeDtypeStruct((TEAM, rows, length, wide), BF16),
         compiler_params=params,
         name="pack",
     )(feats, ups)
-    teams = [[TEAM * rows * g + i for i in range(TEAM * rows)] for g in range(groups)]
-    load = lax.all_to_all(
-        load.reshape(TEAM * rows, positions + cols, wide),
-        ("tm", "rows"), 0, 0, tiled=True, axis_index_groups=teams,
-    ).reshape(TEAM, rows, positions + cols, wide)
+    size = TEAM * rows
+    teams = [[size * g + i for i in range(size)] for g in range(groups)]
+    ranks = [[TEAM * g + j for g in range(groups)] for j in range(TEAM)]
+
+    def in_teams(value):
+        return lax.all_to_all(value, ("tm", "rows"), 0, 0, tiled=True, axis_index_groups=teams)
+
+    def in_ranks(value):
+        return lax.all_to_all(value, "tm", 0, 0, tiled=True, axis_index_groups=ranks)
+
+    load = in_teams(load.reshape(size, length, wide)).reshape(TEAM, rows, length, wide)
     halo = lax.ppermute(load[TEAM - 1, :, :positions], "tm", [(i, (i + TEAM) % tms) for i in range(tms)])
-    stats = lax.all_to_all(stat, ("tm", "rows"), 0, 0, tiled=True)
-
-    whole = lambda shape: pl.BlockSpec(shape, lambda s: (0,) * len(shape))
-    act, sums, norm = pl.pallas_call(
-        act_kernel,
+
+    def whole(shape):
+        return pl.BlockSpec(shape, lambda *s: (0,) * len(shape))
+
+    dense_call = pl.pallas_call(
+        dense_kernel,
         grid=(9,),
         in_specs=[
-            whole((positions, chans)), whole((1, chans)), whole((1, chans)), whole((devices, 128)),
             whole((2, cols, outs)), whole((2, cols, outs)), whole((4, cols, outs)), whole((4, cols, outs)),
             pl.BlockSpec((1, 1, 3, chans, outs), lambda s: (s // 3, s % 3, 0, 0, 0)),
         ],
-        out_specs=(whole((positions, chans)), whole((8, 128)), whole((16, chans))),
+        out_specs=whole((positions, chans)),
+        out_shape=jax.ShapeDtypeStruct((positions, chans), F32),
+        scratch_shapes=[pltpu.VMEM((3, 3, 4, cols, outs), BF16)],
+        compiler_params=params,
+        name="dense",
+    )
+    dense = dense_call(ups, later, above, below, weight)
+
+    stats = pl.pallas_call(
+        functools.partial(combine_kernel, float(positions * (chans // GROUPS))),
+        grid=(1,),
+        in_specs=[
+            pl.BlockSpec((TEAM, rows, 16, wide), lambda s: (0, 0, (positions + cols) // 16, 0)),
+            pl.BlockSpec(memory_space=pl.ANY),
+        ],
+        out_specs=whole((groups, 8, 128)),
+        out_shape=jax.ShapeDtypeStruct((groups, 8, 128), F32),
+        compiler_params=params,
+        name="combine",
+    )(load, dense)
+    stats = in_ranks(stats)
+
+    act, sums, norm = pl.pallas_call(
+        functools.partial(act_kernel, positions * size),
         out_shape=(
             jax.ShapeDtypeStruct((positions, chans), F32),
-            jax.ShapeDtypeStruct((8, 128), F32),
+            jax.ShapeDtypeStruct((size, 8, 128), F32),
             jax.ShapeDtypeStruct((16, chans), F32),
         ),
-        scratch_shapes=[pltpu.VMEM((3, 3, 4, cols, outs), BF16), pltpu.VMEM((positions, chans), F32)],
         compiler_params=params,
         name="act",
-    )(feats, gain, bias, stats, ups, later, above, below, weight)
+    )(feats, gain, bias, stats, dense)
+    sums = in_teams(sums)
 
     part = pl.pallas_call(
         functools.partial(weight_kernel, tms),
@@ -334,31 +396,30 @@
         ],
         compiler_params=params,
         name="wgrad",
-    )(load, halo, norm, gain, bias, sums)
-    ranks = [[TEAM * g + j for g in range(groups)] for j in range(TEAM)]
-    part = lax.all_to_all(part, "tm", 0, 0, tiled=True, axis_index_groups=ranks)
-
-    grad_weight, sums = pl.pallas_call(
-        unpack_kernel,
-        out_shape=(
-            jax.ShapeDtypeStruct((9, 3, step, outs // rows), F32),
-            jax.ShapeDtypeStruct((TEAM * rows, 8, 128), F32),
-        ),
-        compiler_params=params,
-        name="unpack",
-    )(part)
-    sums = lax.all_to_all(sums, ("tm", "rows"), 0, 0, tiled=True, axis_index_groups=teams)
-
-    grad_features, grad_gain, grad_bias = pl.pallas_call(
+    )(load, halo, norm, gain, bias)
+    part = pl.pallas_call(
+        append_kernel,
+        grid=(1,),
+        in_specs=[pl.BlockSpec(memory_space=pl.ANY), whole((size, 8, 128))],
+        out_specs=pl.BlockSpec((groups, 8, 128), lambda s: (0, 14 * step // 8, 0)),
+        out_shape=jax.ShapeDtypeStruct((groups, 14 * step + 8, 128), F32),
+        input_output_aliases={0: 0},
+        compiler_params=params,
+        name="append",
+    )(part, sums)
+    part = in_ranks(part)
+
+    grad_features, grad_weight, grad_gain, grad_bias = pl.pallas_call(
         functools.partial(final_kernel, count),
         out_shape=(
             jax.ShapeDtypeStruct((positions, chans), BF16),
+            jax.ShapeDtypeStruct((9, 3, step, outs // rows), F32),
             jax.ShapeDtypeStruct((1, chans), F32),
             jax.ShapeDtypeStruct((1, chans), F32),
         ),
         compiler_params=params,
         name="final",
-    )(sums, act, feats, norm, gain)
+    )(part, act, feats, norm, gain)
     return (
         grad_features.reshape(features.shape),
         grad_weight.reshape(3, 3, 3, step, outs // rows),
@@ -370,6 +431,4 @@
 def solution(mesh):
     in_specs = (P("tm", "rows", None, None), P(), P(), P(), P("tm", "rows", None, None))
     out_specs = (P("tm", "rows", None, None), P(None, None, None, "tm", "rows"), P(), P())
-    return jax.shard_map(
-        on_device, mesh=mesh, in_specs=in_specs, out_specs=out_specs, check_vma=False
-    )
+    return jax.shard_map(on_device, mesh=mesh, in_specs=in_specs, out_specs=out_specs, check_vma=False)

time: 137 us -> 135 us (0.985)
  the two profiles are of different devices: /device:TPU:1 before, /device:TPU:8 now
where the time goes in v2:
time: 135 us; the launch traced here: 134 us
  blocking collectives  51.6 us (38%)
  Pallas kernels  31.5 us (23%)
  starting transfers between devices  31 us (23%)
  waiting for transfers between devices  15.3 us (11%)
  local copies, waits for them, and re-layouts  3.59 us (3%)
    all_to_all x2, blocking collectives, in_ranks(): lax.all_to_all(value, 'tm', 0, 0, tiled=True, axis_index_groups=ranks)  51.6 us
    all_to_all x2, starting transfers between devices, in_teams(): lax.all_to_all(value, ('tm', 'rows'), 0, 0, tiled=True, axis_index_groups...  18.3 us
    all_to_all x2, waiting for transfers between devices, in_teams(): lax.all_to_all(value, ('tm', 'rows'), 0, 0, tiled=True, axis_index_groups...  12.4 us
    pallas_call x1, Pallas kernels, on_device(): dense = dense_call(ups, later, above, below, weight)  11.1 us
    ppermute x1, starting transfers between devices, on_device(): later = lax.ppermute(ups, 'tm', [((i + 1) % tms, i) for i in range(tms)])  7.4 us
    pallas_call x1, Pallas kernels, on_device(): pl.pallas_call(functools.partial(weight_kernel, tms), out_shape=jax.Shape...  7.19 us
    pallas_call x1, Pallas kernels, on_device(): pl.pallas_call(functools.partial(pack_kernel, tms), out_shape=jax.ShapeDt...  3.46 us
    pallas_call x1, Pallas kernels, on_device(): pl.pallas_call(functools.partial(final_kernel, count), out_shape=(jax.Sha...  3.36 us
  transfers between devices with their start and end apart: 6, of which 2 were waited for; matrix products, arithmetic and copies ran while one was open for 1% of the time, Pallas kernels for 17%

profile of v2, /device:TPU:8, one launch (start us, length us, event | category | flops | bytes accessed | tf_op | source)
XLA Modules:
  0.0 134.4 jit_solution(4326948060631295240)
XLA Ops:
  0.6 3.5 %pack.1 = bf16[4,4,496,128]{3,2,1,0:T(8,128)(2,1)} custom-call(bf16[320,512]{1,0:T(8,128)(2,1)} %bitcast.18, bf16[2,160,256]{2,1,0:T(8,128)(2,1)} %bitcast.21), custom_call_target="tpu_custom_call" | custom-call | tf_op jit(solution)/shard_map/pack/pallas_call | solution.py:327
  4.1 6.4 %all-to-all-start = ((bf16[16,496,128]{2,1,0:T(8,128)(2,1)}), bf16[16,496,128]{2,1,0:T(8,128)(2,1)S(1)}, u32[]{:S(2)}, u32[]{:S(2)}) async-start(bf16[16,496,128]{2,1,0:T(8,128)(2,1)} %bitcast.17), calls=%async_computation | async-start | bytes 4063232 | tf_op jit(solution)/shard_map/all_to_all | solution.py:338
  10.5 7.4 %collective-permute-start.1 = (bf16[2,160,256]{2,1,0:T(8,128)(2,1)S(1)}, bf16[2,160,256]{2,1,0:T(8,128)(2,1)S(1)}, u32[]{:S(2)}, u32[]{:S(2)}) collective-permute-start(bf16[2,160,256]{2,1,0:T(8,128)(2,1)S(1)} %bitcast.23), channel_id=1, source_target_pairs={{4,0},{8,4},{12,8},{16,12},{20,16},{24,20},{28,24},{32,28},{36,32}... | collective-permute-start | bytes 491528 | tf_op jit(solution)/shard_map/ppermute | solution.py:321
  17.9 2.8 %collective-permute-done.1.later_ref = bf16[2,160,256]{2,1,0:T(8,128)(2,1)S(1)} collective-permute-done((bf16[2,160,256]{2,1,0:T(8,128)(2,1)S(1)}, bf16[2,160,256]{2,1,0:T(8,128)(2,1)S(1)}, u32[]{:S(2)}, u32[]{:S(2)}) %collective-permute-start.1) | collective-permute-done | bytes 163872 | tf_op jit(solution)/shard_map/ppermute | solution.py:321
  20.8 0.8 pad_maximum_fusion
  21.5 1.5 %collective-permute-start.2 = (bf16[4,160,256]{2,1,0:T(8,128)(2,1)}, bf16[4,160,256]{2,1,0:T(8,128)(2,1)S(1)}, u32[]{:S(2)}, u32[]{:S(2)}) collective-permute-start(bf16[4,160,256]{2,1,0:T(8,128)(2,1)} %pad_maximum_fusion), channel_id=1, source_target_pairs={{0,1},{1,2},{2,3},{3,0},{4,5},{5,6},{6,7},{7,4},{8,9},{9,10},{10,1... | collective-permute-start | bytes 983048 | tf_op jit(solution)/shard_map/ppermute | solution.py:323
  23.0 0.6 collective-permute-start.3
  23.6 12.4 %all-to-all-done = bf16[16,496,128]{2,1,0:T(8,128)(2,1)S(1)} async-done(((bf16[16,496,128]{2,1,0:T(8,128)(2,1)}), bf16[16,496,128]{2,1,0:T(8,128)(2,1)S(1)}, u32[]{:S(2)}, u32[]{:S(2)}) %all-to-all-start) | async-done | bytes 2031648 | tf_op jit(solution)/shard_map/all_to_all | solution.py:338
  36.0 0.8 slice_bitcast_fusion
  36.8 3.3 %collective-permute-start = (bf16[4,320,128]{2,1,0:T(8,128)(2,1)}, bf16[4,320,128]{2,1,0:T(8,128)(2,1)S(1)}, u32[]{:S(2)}, u32[]{:S(2)}) collective-permute-start(bf16[4,320,128]{2,1,0:T(8,128)(2,1)} %slice_bitcast_fusion), channel_id=1, source_target_pairs={{0,16},{4,20},{8,24},{12,28},{16,32},{20,36},{24,40},{28,44},{32,4... | collective-permute-start | bytes 983048 | tf_op jit(solution)/shard_map/ppermute | solution.py:344
  40.1 0.7 copy-done.3
  40.8 0.7 copy-done.4
  41.5 11.1 %dense.1.dense_ref = f32[320,512]{1,0:T(8,128)} custom-call(bf16[2,160,256]{2,1,0:T(8,128)(2,1)} %bitcast.22, bf16[2,160,256]{2,1,0:T(8,128)(2,1)} %copy-done.2, bf16[4,160,256]{2,1,0:T(8,128)(2,1)} %copy-done.3, bf16[4,160,256]{2,1,0:T(8,128)(2,1)} %copy-done.4, bf16[3,3,3,512,256]{4,3,2,1,0:T(8,128)(2,1)} %weight_ref.1), custom_call_target="tpu_custom_call" | custom-call | tf_op jit(solution)/shard_map/dense/pallas_call | solution.py:362
  52.6 1.6 %combine.1 = f32[16,8,128]{2,1,0:T(8,128)} custom-call(bf16[4,4,496,128]{3,2,1,0:T(8,128)(2,1)} %bitcast.15, f32[320,512]{1,0:T(8,128)} %dense.1.dense_ref), custom_call_target="tpu_custom_call" | custom-call | tf_op jit(solution)/shard_map/combine/pallas_call | solution.py:364
  54.2 17.3 %all_to_all.20.stats_ref = f32[16,8,128]{2,1,0:T(8,128)} all-to-all(f32[16,8,128]{2,1,0:T(8,128)} %combine.1), channel_id=1, replica_groups={{0,16,32,48,64,80,96,112,128,144,160,176,192,208,224,240},{4,20,36,52,6..., dimensions={0} | all-to-all | bytes 131072 | tf_op jit(solution)/shard_map/all_to_all | solution.py:341
  71.5 3.3 %act.1 = (f32[320,512]{1,0:T(8,128)}, f32[16,8,128]{2,1,0:T(8,128)}, f32[16,512]{1,0:T(8,128)}) custom-call(bf16[320,512]{1,0:T(8,128)(2,1)} %bitcast.19, f32[1,512]{1,0:T(1,128)} %bitcast.25, f32[1,512]{1,0:T(1,128)} %bitcast.28, f32[16,8,128]{2,1,0:T(8,128)} %all_to_all.20.stats_ref, f32[320,512]{1,0:T(8,128)} %dense.1.dense_ref), custom_call_target="tpu_custom_call" | custom-call | tf_op jit(solution)/shard_map/act/pallas_call | solution.py:378
  74.9 11.9 %all-to-all-start.2 = ((f32[16,8,128]{2,1,0:T(8,128)}), f32[16,8,128]{2,1,0:T(8,128)S(1)}, u32[]{:S(2)}, u32[]{:S(2)}) async-start(f32[16,8,128]{2,1,0:T(8,128)} %get-tuple-element.12), calls=%async_computation.2 | async-start | bytes 131072 | tf_op jit(solution)/shard_map/all_to_all | solution.py:338
  86.7 0.0 copy-start.5
  86.8 0.7 copy-done.5
  87.5 7.2 %wgrad.1.part_ref = f32[16,120,128]{2,1,0:T(8,128)} custom-call(bf16[4,4,496,128]{3,2,1,0:T(8,128)(2,1)} %bitcast.16, bf16[4,320,128]{2,1,0:T(8,128)(2,1)} %copy-done.5, f32[16,512]{1,0:T(8,128)} %get-tuple-element.11.norm_ref, f32[1,512]{1,0:T(1,128)} %bitcast.26, f32[1,512]{1,0:T(1,128)} %bitcast.29), custom_call_target="tpu_custom_call" | custom-call | tf_op jit(solution)/shard_map/wgrad/pallas_call | solution.py:390
  94.7 0.6 copy-done.6
  95.3 1.5 %append.1 = f32[16,120,128]{2,1,0:T(8,128)} custom-call(f32[16,120,128]{2,1,0:T(8,128)} %wgrad.1.part_ref, f32[16,8,128]{2,1,0:T(8,128)} %copy-done.6), custom_call_target="tpu_custom_call", output_to_operand_aliasing={{}: (0, {})} | custom-call | tf_op jit(solution)/shard_map/append/pallas_call | solution.py:400
  96.8 34.2 %all_to_all.21.load_ref = f32[16,120,128]{2,1,0:T(8,128)} all-to-all(f32[16,120,128]{2,1,0:T(8,128)} %append.1), channel_id=1, replica_groups={{0,16,32,48,64,80,96,112,128,144,160,176,192,208,224,240},{4,20,36,52,6..., dimensions={0} | all-to-all | bytes 1966080 | tf_op jit(solution)/shard_map/all_to_all | solution.py:341
  131.0 3.4 %final.1 = (bf16[320,512]{1,0:T(8,128)(2,1)}, f32[9,3,8,64]{3,2,1,0:T(8,128)}, f32[1,512]{1,0:T(1,128)}, f32[1,512]{1,0:T(1,128)}) custom-call(f32[16,120,128]{2,1,0:T(8,128)} %all_to_all.21.load_ref, f32[320,512]{1,0:T(8,128)} %get-tuple-element.13.act_ref, bf16[320,512]{1,0:T(8,128)(2,1)} %bitcast.20, f32[16,512]{1,0:T(8,128)} %get-tuple-element.11.norm_ref, ...), custom_call_target="tpu_custom_call" | custom-call | tf_op jit(solution)/shard_map/final/pallas_call | solution.py:412
  (13 shorter events, 0.0 us)
Async XLA Ops:
  4.1 6.4 %copy-start.1 = (bf16[2,1,160,256]{3,2,1,0:T(8,128)(2,1)S(1)}, bf16[2,1,160,256]{3,2,1,0:T(8,128)(2,1)}, u32[]{:S(2)}) copy-start(bf16[2,1,160,256]{3,2,1,0:T(8,128)(2,1)} %param.9) | copy-start | bytes 491524
  4.1 31.9 %all-to-all-start = ((bf16[16,496,128]{2,1,0:T(8,128)(2,1)}), bf16[16,496,128]{2,1,0:T(8,128)(2,1)S(1)}, u32[]{:S(2)}, u32[]{:S(2)}) async-start(bf16[16,496,128]{2,1,0:T(8,128)(2,1)} %bitcast.17), calls=%async_computation | async-start | bytes 4063232 | tf_op jit(solution)/shard_map/all_to_all | solution.py:338
  10.5 10.2 %collective-permute-start.1 = (bf16[2,160,256]{2,1,0:T(8,128)(2,1)S(1)}, bf16[2,160,256]{2,1,0:T(8,128)(2,1)S(1)}, u32[]{:S(2)}, u32[]{:S(2)}) collective-permute-start(bf16[2,160,256]{2,1,0:T(8,128)(2,1)S(1)} %bitcast.23), channel_id=1, source_target_pairs={{4,0},{8,4},{12,8},{16,12},{20,16},{24,20},{28,24},{32,28},{36,32}... | collective-permute-start | bytes 491528 | tf_op jit(solution)/shard_map/ppermute | solution.py:321
  20.8 19.3 %copy-start.2 = (bf16[2,160,256]{2,1,0:T(8,128)(2,1)}, bf16[2,160,256]{2,1,0:T(8,128)(2,1)S(1)}, u32[]{:S(2)}) copy-start(bf16[2,160,256]{2,1,0:T(8,128)(2,1)S(1)} %collective-permute-done.1.later_ref) | copy-start | bytes 491524
  21.5 18.5 %collective-permute-start.2 = (bf16[4,160,256]{2,1,0:T(8,128)(2,1)}, bf16[4,160,256]{2,1,0:T(8,128)(2,1)S(1)}, u32[]{:S(2)}, u32[]{:S(2)}) collective-permute-start(bf16[4,160,256]{2,1,0:T(8,128)(2,1)} %pad_maximum_fusion), channel_id=1, source_target_pairs={{0,1},{1,2},{2,3},{3,0},{4,5},{5,6},{6,7},{7,4},{8,9},{9,10},{10,1... | collective-permute-start | bytes 983048 | tf_op jit(solution)/shard_map/ppermute | solution.py:323
  23.0 17.1 %collective-permute-start.3 = (bf16[4,160,256]{2,1,0:T(8,128)(2,1)}, bf16[4,160,256]{2,1,0:T(8,128)(2,1)S(1)}, u32[]{:S(2)}, u32[]{:S(2)}) collective-permute-start(bf16[4,160,256]{2,1,0:T(8,128)(2,1)} %pad_maximum_fusion), channel_id=1, source_target_pairs={{1,0},{2,1},{3,2},{0,3},{5,4},{6,5},{7,6},{4,7},{9,8},{10,9},{11,1... | collective-permute-start | bytes 983048 | tf_op jit(solution)/shard_map/ppermute | solution.py:324
  36.0 16.6 %copy-start = (bf16[16,496,128]{2,1,0:T(8,128)(2,1)}, bf16[16,496,128]{2,1,0:T(8,128)(2,1)S(1)}, u32[]{:S(2)}) copy-start(bf16[16,496,128]{2,1,0:T(8,128)(2,1)S(1)} %all-to-all-done) | copy-start | bytes 6094852
  36.8 50.0 %collective-permute-start = (bf16[4,320,128]{2,1,0:T(8,128)(2,1)}, bf16[4,320,128]{2,1,0:T(8,128)(2,1)S(1)}, u32[]{:S(2)}, u32[]{:S(2)}) collective-permute-start(bf16[4,320,128]{2,1,0:T(8,128)(2,1)} %slice_bitcast_fusion), channel_id=1, source_target_pairs={{0,16},{4,20},{8,24},{12,28},{16,32},{20,36},{24,40},{28,44},{32,4... | collective-permute-start | bytes 983048 | tf_op jit(solution)/shard_map/ppermute | solution.py:344
  40.1 0.7 copy-start.3
  40.8 0.7 copy-start.4
  74.9 19.8 %all-to-all-start.2 = ((f32[16,8,128]{2,1,0:T(8,128)}), f32[16,8,128]{2,1,0:T(8,128)S(1)}, u32[]{:S(2)}, u32[]{:S(2)}) async-start(f32[16,8,128]{2,1,0:T(8,128)} %get-tuple-element.12), calls=%async_computation.2 | async-start | bytes 131072 | tf_op jit(solution)/shard_map/all_to_all | solution.py:338
  86.7 0.7 copy-start.5
  94.7 0.6 copy-start.6

commit v3 on v2

--- a/solution.py
+++ b/solution.py
@@ -77,11 +77,11 @@
             load_ref[j, r, positions + cols :, :] = parts
 
 
-def combine_kernel(count, load_ref, dense_ref, out_ref):
+def combine_kernel(count, load_ref, out_ref):
     stats = []
     for j in range(load_ref.shape[0]):
         for r in range(load_ref.shape[1]):
-            parts = load_ref[j, r].astype(F32)
+            parts = load_ref[j, r, load_ref.shape[2] - 16 :].astype(F32)
             stats.append(parts[0:1] + parts[1:2] + parts[2:3])
     total = stats[0]
     for stat in stats[1:]:
@@ -96,14 +96,14 @@
     out_ref[...] = jnp.broadcast_to(result[None], out_ref.shape)
 
 
-def dense_kernel(up_ref, later_ref, above_ref, below_ref, weight_ref, out_ref, slabs):
+def dense_kernel(now_ref, later_ref, weight_ref, out_ref, slabs):
     step = pl.program_id(0)
     time_tap = step // 3
     row_tap = step % 3
     time_index = lax.axis_index("tm")
     row_index = lax.axis_index("rows")
     positions = out_ref.shape[0]
-    cols = up_ref.shape[1]
+    cols = now_ref.shape[2]
 
     @pl.when(step == 0)
     def _():
@@ -112,11 +112,10 @@
         up_ok = (row_index > 0).astype(F32)
         down_ok = (row_index < lax.axis_size("rows") - 1).astype(F32)
         for f in range(4):
-            own = up_ref[f] if f < 2 else later_ref[f - 2]
+            source = now_ref if f < 2 else later_ref
             tail = jnp.float32(1.0) if f < 2 else more
-            for r, slab, keep in ((0, above_ref[f], up_ok), (1, own, None), (2, below_ref[f], down_ok)):
-                scale = tail if keep is None else keep * tail
-                slab = (slab.astype(F32) * scale).astype(BF16)
+            for r, keep in ((0, up_ok), (1, jnp.float32(1.0)), (2, down_ok)):
+                slab = (source[r, f % 2].astype(F32) * (keep * tail)).astype(BF16)
                 for c, moved in enumerate(col_shifts(slab)):
                     slabs[c, r, f] = moved
 
@@ -186,7 +185,8 @@
     total = load_ref[0]
     for g in range(1, load_ref.shape[0]):
         total = total + load_ref[g]
-    out_ref[...] = jnp.broadcast_to(total[None], out_ref.shape)
+    place = (out_ref.shape[0],) + total.shape
+    out_ref[:, out_ref.shape[1] - total.shape[0] :, :] = jnp.broadcast_to(total[None], place)
 
 
 def weight_kernel(teams, load_ref, halo_ref, norm_ref, gain_ref, bias_ref, out_ref, hidden, acc):
@@ -216,20 +216,26 @@
     for f in range(frames + 2):
         hidden[f, 0] = jnp.zeros(hidden.shape[2:], BF16)
         hidden[f, rows + 1] = jnp.zeros(hidden.shape[2:], BF16)
+    opening = (time_index < TEAM).astype(F32)
     for j in range(TEAM):
         for r in range(rows):
             for f in range(2):
-                hidden[2 + 2 * j + f, 1 + r] = silu(load_ref[j, r, f * cols : (f + 1) * cols, :])
-    for r in range(rows):
-        for f in range(2):
-            source = jnp.where(time_index < TEAM, load_ref[0, r, 0:cols, :], halo_ref[r, f * cols : (f + 1) * cols, :])
-            hidden[f, 1 + r] = silu(source)
+                value = silu(load_ref[j, r, f * cols : (f + 1) * cols, :])
+                hidden[2 + 2 * j + f, 1 + r] = value
+                if j == 0 and f == 0:
+                    value = (value.astype(F32) * opening).astype(BF16)
+                    hidden[0, 1 + r] = value
+                    hidden[1, 1 + r] = value
 
     lanes = iota((cols, 128), 1) < 64
-    for j in range(TEAM):
+    more = (time_index < lax.axis_size("tm") - TEAM).astype(F32)
+    for j in range(TEAM + 1):
         halves = [[], []]
         for r in range(rows):
-            pair = load_ref[j, r, 2 * cols : 3 * cols, :].astype(F32)
+            if j < TEAM:
+                pair = load_ref[j, r, 2 * cols : 3 * cols, :].astype(F32)
+            else:
+                pair = halo_ref[r].astype(F32) * more
             row = iota(pair.shape, 0)
             ahead = jnp.where(row < cols - 1, pltpu.roll(pair, cols - 1, 0), 0.0)
             behind = jnp.where(row > 0, pltpu.roll(pair, 1, 0), 0.0)
@@ -239,16 +245,18 @@
             halves[1].append(jnp.concatenate([right, behind[:, 64:128]], axis=1))
         for f in range(2):
             ups = jnp.concatenate(halves[f], axis=0).astype(BF16)
+            frame = 2 * j + f
+            depth = min(3, frames + 2 - frame)
             taps = [
-                hidden[2 * j + f + a, b : b + rows].reshape(rows * cols, wide) for a in range(3) for b in range(3)
+                hidden[frame + a, b : b + rows].reshape(rows * cols, wide) for a in range(depth) for b in range(3)
             ]
             term = lax.dot_general(
                 ups, jnp.concatenate(taps, axis=1), (((0,), (0,)), ((), ())), preferred_element_type=F32
             )
-            if j == 0 and f == 0:
+            if frame == 0:
                 acc[...] = term
             else:
-                acc[...] += term
+                acc[:, 0 : 3 * depth * wide] += term
 
     groups = out_ref.shape[0]
     tail = None
@@ -311,37 +319,42 @@
     groups = tms // TEAM
     wide = chans // TEAM
     count = positions * devices * (chans // GROUPS)
-    params = pltpu.CompilerParams(vmem_limit_bytes=60 * 1024 * 1024)
+    vmem = pl.BlockSpec(memory_space=pltpu.VMEM)
+
+    def params(mebibytes):
+        return pltpu.CompilerParams(vmem_limit_bytes=mebibytes * 1024 * 1024)
 
     feats = features.reshape(positions, chans)
     ups = upstream.reshape(frames, cols, outs)
     gain = norm_gain.reshape(1, chans)
     bias = norm_bias.reshape(1, chans)
-
-    later = lax.ppermute(ups, "tm", [((i + 1) % tms, i) for i in range(tms)])
-    four = jnp.concatenate([ups, later], axis=0)
-    above = lax.ppermute(four, "rows", [(i, (i + 1) % rows) for i in range(rows)])
-    below = lax.ppermute(four, "rows", [((i + 1) % rows, i) for i in range(rows)])
-
+    size = TEAM * rows
     length = positions + cols + 16
+    teams = [[size * g + i for i in range(size)] for g in range(groups)]
+    ranks = [[TEAM * g + j for g in range(groups)] for j in range(TEAM)]
+
+    def in_teams(value):
+        return lax.all_to_all(value, ("tm", "rows"), 0, 0, tiled=True, axis_index_groups=teams)
+
+    def in_ranks(value):
+        return lax.all_to_all(value, "tm", 0, 0, tiled=True, axis_index_groups=ranks)
+
+    above = lax.ppermute(ups, "rows", [(i, (i + 1) % rows) for i in range(rows)])
+    below = lax.ppermute(ups, "rows", [((i + 1) % rows, i) for i in range(rows)])
+
     load = pl.pallas_call(
         functools.partial(pack_kernel, tms),
         out_shape=jax.ShapeDtypeStruct((TEAM, rows, length, wide), BF16),
-        compiler_params=params,
+        compiler_params=params(62),
         name="pack",
     )(feats, ups)
-    size = TEAM * rows
-    teams = [[size * g + i for i in range(size)] for g in range(groups)]
-    ranks = [[TEAM * g + j for g in range(groups)] for j in range(TEAM)]
-
-    def in_teams(value):
-        return lax.all_to_all(value, ("tm", "rows"), 0, 0, tiled=True, axis_index_groups=teams)
-
-    def in_ranks(value):
-        return lax.all_to_all(value, "tm", 0, 0, tiled=True, axis_index_groups=ranks)
-
     load = in_teams(load.reshape(size, length, wide)).reshape(TEAM, rows, length, wide)
-    halo = lax.ppermute(load[TEAM - 1, :, :positions], "tm", [(i, (i + TEAM) % tms) for i in range(tms)])
+
+    now = jnp.stack([above, ups, below])
+    later = lax.ppermute(now, "tm", [((i + 1) % tms, i) for i in range(tms)])
+    halo = lax.ppermute(
+        load[0, :, positions : positions + cols], "tm", [((i + TEAM) % tms, i) for i in range(tms)]
+    )
 
     def whole(shape):
         return pl.BlockSpec(shape, lambda *s: (0,) * len(shape))
@@ -350,74 +363,74 @@
         dense_kernel,
         grid=(9,),
         in_specs=[
-            whole((2, cols, outs)), whole((2, cols, outs)), whole((4, cols, outs)), whole((4, cols, outs)),
+            whole((3, frames, cols, outs)), whole((3, frames, cols, outs)),
             pl.BlockSpec((1, 1, 3, chans, outs), lambda s: (s // 3, s % 3, 0, 0, 0)),
         ],
         out_specs=whole((positions, chans)),
         out_shape=jax.ShapeDtypeStruct((positions, chans), F32),
         scratch_shapes=[pltpu.VMEM((3, 3, 4, cols, outs), BF16)],
-        compiler_params=params,
+        compiler_params=params(62),
         name="dense",
     )
-    dense = dense_call(ups, later, above, below, weight)
+    dense = dense_call(now, later, weight)
 
     stats = pl.pallas_call(
         functools.partial(combine_kernel, float(positions * (chans // GROUPS))),
-        grid=(1,),
-        in_specs=[
-            pl.BlockSpec((TEAM, rows, 16, wide), lambda s: (0, 0, (positions + cols) // 16, 0)),
-            pl.BlockSpec(memory_space=pl.ANY),
-        ],
-        out_specs=whole((groups, 8, 128)),
+        in_specs=[vmem],
+        out_specs=vmem,
         out_shape=jax.ShapeDtypeStruct((groups, 8, 128), F32),
-        compiler_params=params,
+        compiler_params=params(16),
         name="combine",
-    )(load, dense)
+    )(load)
     stats = in_ranks(stats)
 
     act, sums, norm = pl.pallas_call(
         functools.partial(act_kernel, positions * size),
+        in_specs=[pl.BlockSpec(), pl.BlockSpec(), pl.BlockSpec(), vmem, pl.BlockSpec()],
         out_shape=(
             jax.ShapeDtypeStruct((positions, chans), F32),
             jax.ShapeDtypeStruct((size, 8, 128), F32),
             jax.ShapeDtypeStruct((16, chans), F32),
         ),
-        compiler_params=params,
+        compiler_params=params(62),
         name="act",
     )(feats, gain, bias, stats, dense)
     sums = in_teams(sums)
 
-    part = pl.pallas_call(
+    weight_call = pl.pallas_call(
         functools.partial(weight_kernel, tms),
+        in_specs=[vmem] + [pl.BlockSpec()] * 4,
+        out_specs=vmem,
         out_shape=jax.ShapeDtypeStruct((groups, 14 * step + 8, 128), F32),
         scratch_shapes=[
             pltpu.VMEM((2 * TEAM + 2, rows + 2, cols, wide), BF16),
             pltpu.VMEM((3 * 64, 9 * wide), F32),
         ],
-        compiler_params=params,
+        compiler_params=params(61),
         name="wgrad",
-    )(load, halo, norm, gain, bias)
+    )
+    part = weight_call(load, halo, norm, gain, bias)
     part = pl.pallas_call(
         append_kernel,
-        grid=(1,),
-        in_specs=[pl.BlockSpec(memory_space=pl.ANY), whole((size, 8, 128))],
-        out_specs=pl.BlockSpec((groups, 8, 128), lambda s: (0, 14 * step // 8, 0)),
+        in_specs=[vmem, vmem],
+        out_specs=vmem,
         out_shape=jax.ShapeDtypeStruct((groups, 14 * step + 8, 128), F32),
         input_output_aliases={0: 0},
-        compiler_params=params,
+        compiler_params=params(16),
         name="append",
     )(part, sums)
     part = in_ranks(part)
 
     grad_features, grad_weight, grad_gain, grad_bias = pl.pallas_call(
         functools.partial(final_kernel, count),
+        in_specs=[vmem] + [pl.BlockSpec()] * 4,
         out_shape=(
             jax.ShapeDtypeStruct((positions, chans), BF16),
             jax.ShapeDtypeStruct((9, 3, step, outs // rows), F32),
             jax.ShapeDtypeStruct((1, chans), F32),
             jax.ShapeDtypeStruct((1, chans), F32),
         ),
-        compiler_params=params,
+        compiler_params=params(16),
         name="final",
     )(part, act, feats, norm, gain)
     return (

time: 135 us -> 119 us (0.88)
  the two profiles are of different devices: /device:TPU:8 before, /device:TPU:0 now
where the time goes in v3:
time: 119 us; the launch traced here: 118 us
  blocking collectives  32.8 us (28%)
  starting transfers between devices  28.3 us (24%)
  Pallas kernels  28.1 us (24%)
  waiting for transfers between devices  26.4 us (22%)
  local copies, waits for them, and re-layouts  1.91 us (2%)
    all_to_all x1, blocking collectives, in_ranks(): lax.all_to_all(value, 'tm', 0, 0, tiled=True, axis_index_groups=ranks)  32.8 us
    ppermute x1, waiting for transfers between devices, on_device(): lax.ppermute(ups, 'rows', [((i + 1) % rows, i) for i in range(rows)])  25.2 us
    pallas_call x1, Pallas kernels, on_device(): dense = dense_call(now, later, weight)  11.1 us
    all_to_all x2, starting transfers between devices, in_teams(): lax.all_to_all(value, ('tm', 'rows'), 0, 0, tiled=True, axis_index_groups...  7.85 us
    pallas_call x1, Pallas kernels, on_device(): part = weight_call(load, halo, norm, gain, bias)  7.44 us
    ppermute x1, starting transfers between devices, on_device(): later = lax.ppermute(now, 'tm', [((i + 1) % tms, i) for i in range(tms)])  7.01 us
    ppermute x1, starting transfers between devices, on_device(): lax.ppermute(load[0, :, positions:positions + cols], 'tm', [((i + TEAM) %...  6.06 us
    all_to_all x1, starting transfers between devices, in_ranks(): lax.all_to_all(value, 'tm', 0, 0, tiled=True, axis_index_groups=ranks)  4.16 us
  transfers between devices with their start and end apart: 7, of which 2 were waited for; matrix products, arithmetic and copies ran while one was open for 1% of the time, Pallas kernels for 19%

profile of v3, /device:TPU:0, one launch (start us, length us, event | category | flops | bytes accessed | tf_op | source)
XLA Modules:
  0.0 118.3 jit_solution(12025150001159259987)
XLA Ops:
  0.6 3.5 %pack.1 = bf16[4,4,496,128]{3,2,1,0:T(8,128)(2,1)} custom-call(bf16[320,512]{1,0:T(8,128)(2,1)} %bitcast.20, bf16[2,160,256]{2,1,0:T(8,128)(2,1)} %bitcast.27), custom_call_target="tpu_custom_call" | custom-call | tf_op jit(solution)/shard_map/pack/pallas_call | solution.py:345
  4.1 4.3 %all-to-all-start = ((bf16[16,496,128]{2,1,0:T(8,128)(2,1)}), bf16[16,496,128]{2,1,0:T(8,128)(2,1)S(1)}, u32[]{:S(2)}, u32[]{:S(2)}) async-start(bf16[16,496,128]{2,1,0:T(8,128)(2,1)} %bitcast.26), calls=%async_computation | async-start | bytes 4063232 | tf_op jit(solution)/shard_map/all_to_all | solution.py:337
  8.5 3.2 %collective-permute-start.2 = (bf16[2,160,256]{2,1,0:T(8,128)(2,1)S(1)}, bf16[2,160,256]{2,1,0:T(8,128)(2,1)S(1)}, u32[]{:S(2)}, u32[]{:S(2)}) collective-permute-start(bf16[2,160,256]{2,1,0:T(8,128)(2,1)S(1)} %bitcast.28), channel_id=1, source_target_pairs={{1,0},{2,1},{3,2},{0,3},{5,4},{6,5},{7,6},{4,7},{9,8},{10,9},{11,1... | collective-permute-start | bytes 491528 | tf_op jit(solution)/shard_map/ppermute | solution.py:343
  11.7 0.0 collective-permute-start.1
  11.7 25.2 %collective-permute-done.2 = bf16[2,160,256]{2,1,0:T(8,128)(2,1)S(1)} collective-permute-done((bf16[2,160,256]{2,1,0:T(8,128)(2,1)S(1)}, bf16[2,160,256]{2,1,0:T(8,128)(2,1)S(1)}, u32[]{:S(2)}, u32[]{:S(2)}) %collective-permute-start.2) | collective-permute-done | bytes 163872 | tf_op jit(solution)/shard_map/ppermute | solution.py:343
  36.9 1.2 collective-permute-done.1
  38.0 0.1 pad_maximum_fusion.now_ref
  38.1 7.0 %collective-permute-start.3 = (bf16[3,2,160,256]{3,2,1,0:T(8,128)(2,1)S(1)}, bf16[3,2,160,256]{3,2,1,0:T(8,128)(2,1)}, u32[]{:S(2)}, u32[]{:S(2)}) collective-permute-start(bf16[3,2,160,256]{3,2,1,0:T(8,128)(2,1)S(1)} %pad_maximum_fusion.now_ref), channel_id=1, source_target_pairs={{4,0},{8,4},{12,8},{16,12},{20,16},{24,20},{28,24},{32,28},{36,32}... | collective-permute-start | bytes 1474568 | tf_op jit(solution)/shard_map/ppermute | solution.py:354
  45.1 0.0 all-to-all-done
  45.1 0.9 combine.1
  46.0 4.2 %all-to-all-start.1 = ((f32[16,8,128]{2,1,0:T(8,128)}), f32[16,8,128]{2,1,0:T(8,128)}, u32[]{:S(2)}, u32[]{:S(2)}) async-start(f32[16,8,128]{2,1,0:T(8,128)} %combine.1), calls=%async_computation.1 | async-start | bytes 131072 | tf_op jit(solution)/shard_map/all_to_all | solution.py:340
  50.2 0.7 slice_bitcast_fusion
  50.9 6.1 %collective-permute-start = (bf16[4,160,128]{2,1,0:T(8,128)(2,1)}, bf16[4,160,128]{2,1,0:T(8,128)(2,1)}, u32[]{:S(2)}, u32[]{:S(2)}) collective-permute-start(bf16[4,160,128]{2,1,0:T(8,128)(2,1)} %slice_bitcast_fusion), channel_id=1, source_target_pairs={{16,0},{20,4},{24,8},{28,12},{32,16},{36,20},{40,24},{44,28},{48,3... | collective-permute-start | bytes 491528 | tf_op jit(solution)/shard_map/ppermute | solution.py:355
  56.9 0.0 collective-permute-done.3.later_ref
  56.9 11.1 %dense.1.dense_ref = f32[320,512]{1,0:T(8,128)} custom-call(bf16[3,2,160,256]{3,2,1,0:T(8,128)(2,1)} %copy-done.6, bf16[3,2,160,256]{3,2,1,0:T(8,128)(2,1)} %collective-permute-done.3.later_ref, bf16[3,3,3,512,256]{4,3,2,1,0:T(8,128)(2,1)} %weight_ref.1), custom_call_target="tpu_custom_call" | custom-call | tf_op jit(solution)/shard_map/dense/pallas_call | solution.py:375
  68.0 0.0 all-to-all-done.1.stats_ref
  68.0 3.3 %act.1 = (f32[320,512]{1,0:T(8,128)}, f32[16,8,128]{2,1,0:T(8,128)}, f32[16,512]{1,0:T(8,128)}) custom-call(bf16[320,512]{1,0:T(8,128)(2,1)} %bitcast.21, f32[1,512]{1,0:T(1,128)} %bitcast.23, f32[1,512]{1,0:T(1,128)} %bitcast.33, f32[16,8,128]{2,1,0:T(8,128)} %all-to-all-done.1.stats_ref, f32[320,512]{1,0:T(8,128)} %dense.1.dense_ref), custom_call_target="tpu_custom_call" | custom-call | tf_op jit(solution)/shard_map/act/pallas_call | solution.py:387
  71.3 3.5 %all-to-all-start.2 = ((f32[16,8,128]{2,1,0:T(8,128)}), f32[16,8,128]{2,1,0:T(8,128)S(1)}, u32[]{:S(2)}, u32[]{:S(2)}) async-start(f32[16,8,128]{2,1,0:T(8,128)} %get-tuple-element.12), calls=%async_computation.2 | async-start | bytes 131072 | tf_op jit(solution)/shard_map/all_to_all | solution.py:337
  74.9 0.0 collective-permute-done.halo_ref
  74.9 7.4 %wgrad.1.part_ref = f32[16,120,128]{2,1,0:T(8,128)} custom-call(bf16[4,4,496,128]{3,2,1,0:T(8,128)(2,1)} %bitcast.19, bf16[4,160,128]{2,1,0:T(8,128)(2,1)} %collective-permute-done.halo_ref, f32[16,512]{1,0:T(8,128)} %get-tuple-element.11.norm_ref, f32[1,512]{1,0:T(1,128)} %bitcast.24, f32[1,512]{1,0:T(1,128)} %bitcast.34), custom_call_target="tpu_custom_call" | custom-call | tf_op jit(solution)/shard_map/wgrad/pallas_call | solution.py:412
  82.3 0.0 all-to-all-done.2.load_ref
  82.3 1.2 %copy-done.1 = f32[16,120,128]{2,1,0:T(8,128)S(1)} copy-done((f32[16,120,128]{2,1,0:T(8,128)S(1)}, f32[16,120,128]{2,1,0:T(8,128)}, u32[]{:S(2)}) %copy-start.1) | copy-done | bytes 983064
  83.6 32.8 %all_to_all.20.load_ref = f32[16,120,128]{2,1,0:T(8,128)S(1)} all-to-all(f32[16,120,128]{2,1,0:T(8,128)S(1)} %append.1), channel_id=1, replica_groups={{0,16,32,48,64,80,96,112,128,144,160,176,192,208,224,240},{4,20,36,52,6..., dimensions={0} | all-to-all | bytes 1966080 | tf_op jit(solution)/shard_map/all_to_all | solution.py:340
  116.4 1.9 %final.1 = (bf16[320,512]{1,0:T(8,128)(2,1)}, f32[9,3,8,64]{3,2,1,0:T(8,128)}, f32[1,512]{1,0:T(1,128)}, f32[1,512]{1,0:T(1,128)}) custom-call(f32[16,120,128]{2,1,0:T(8,128)S(1)} %all_to_all.20.load_ref, f32[320,512]{1,0:T(8,128)S(1)} %copy-done.3, bf16[320,512]{1,0:T(8,128)(2,1)S(1)} %bitcast.22, f32[16,512]{1,0:T(8,128)S(1)} %copy-done.4, ...), custom_call_target="tpu_custom_call" | custom-call | tf_op jit(solution)/shard_map/final/pallas_call | solution.py:424
  (16 shorter events, 0.1 us)
Async XLA Ops:
  4.1 4.4 %copy-start.7 = (bf16[2,1,160,256]{3,2,1,0:T(8,128)(2,1)S(1)}, bf16[2,1,160,256]{3,2,1,0:T(8,128)(2,1)}, u32[]{:S(2)}) copy-start(bf16[2,1,160,256]{3,2,1,0:T(8,128)(2,1)} %param.9) | copy-start | bytes 491524
  4.1 41.0 %all-to-all-start = ((bf16[16,496,128]{2,1,0:T(8,128)(2,1)}), bf16[16,496,128]{2,1,0:T(8,128)(2,1)S(1)}, u32[]{:S(2)}, u32[]{:S(2)}) async-start(bf16[16,496,128]{2,1,0:T(8,128)(2,1)} %bitcast.26), calls=%async_computation | async-start | bytes 4063232 | tf_op jit(solution)/shard_map/all_to_all | solution.py:337
  8.5 28.4 %collective-permute-start.2 = (bf16[2,160,256]{2,1,0:T(8,128)(2,1)S(1)}, bf16[2,160,256]{2,1,0:T(8,128)(2,1)S(1)}, u32[]{:S(2)}, u32[]{:S(2)}) collective-permute-start(bf16[2,160,256]{2,1,0:T(8,128)(2,1)S(1)} %bitcast.28), channel_id=1, source_target_pairs={{1,0},{2,1},{3,2},{0,3},{5,4},{6,5},{7,6},{4,7},{9,8},{10,9},{11,1... | collective-permute-start | bytes 491528 | tf_op jit(solution)/shard_map/ppermute | solution.py:343
  11.7 26.4 %collective-permute-start.1 = (bf16[2,160,256]{2,1,0:T(8,128)(2,1)S(1)}, bf16[2,160,256]{2,1,0:T(8,128)(2,1)S(1)}, u32[]{:S(2)}, u32[]{:S(2)}) collective-permute-start(bf16[2,160,256]{2,1,0:T(8,128)(2,1)S(1)} %bitcast.29), channel_id=1, source_target_pairs={{0,1},{1,2},{2,3},{3,0},{4,5},{5,6},{6,7},{7,4},{8,9},{9,10},{10,1... | collective-permute-start | bytes 491528 | tf_op jit(solution)/shard_map/ppermute | solution.py:342
  38.1 7.0 %copy-start.6 = (bf16[3,2,160,256]{3,2,1,0:T(8,128)(2,1)}, bf16[3,2,160,256]{3,2,1,0:T(8,128)(2,1)S(1)}, u32[]{:S(2)}) copy-start(bf16[3,2,160,256]{3,2,1,0:T(8,128)(2,1)S(1)} %pad_maximum_fusion.now_ref) | copy-start | bytes 1474564
  38.1 18.8 %collective-permute-start.3 = (bf16[3,2,160,256]{3,2,1,0:T(8,128)(2,1)S(1)}, bf16[3,2,160,256]{3,2,1,0:T(8,128)(2,1)}, u32[]{:S(2)}, u32[]{:S(2)}) collective-permute-start(bf16[3,2,160,256]{3,2,1,0:T(8,128)(2,1)S(1)} %pad_maximum_fusion.now_ref), channel_id=1, source_target_pairs={{4,0},{8,4},{12,8},{16,12},{20,16},{24,20},{28,24},{32,28},{36,32}... | collective-permute-start | bytes 1474568 | tf_op jit(solution)/shard_map/ppermute | solution.py:354
  45.1 22.9 %copy-start = (bf16[16,496,128]{2,1,0:T(8,128)(2,1)}, bf16[16,496,128]{2,1,0:T(8,128)(2,1)S(1)}, u32[]{:S(2)}) copy-start(bf16[16,496,128]{2,1,0:T(8,128)(2,1)S(1)} %all-to-all-done) | copy-start | bytes 6094852
  46.0 22.0 %all-to-all-start.1 = ((f32[16,8,128]{2,1,0:T(8,128)}), f32[16,8,128]{2,1,0:T(8,128)}, u32[]{:S(2)}, u32[]{:S(2)}) async-start(f32[16,8,128]{2,1,0:T(8,128)} %combine.1), calls=%async_computation.1 | async-start | bytes 131072 | tf_op jit(solution)/shard_map/all_to_all | solution.py:340
  50.9 24.0 %collective-permute-start = (bf16[4,160,128]{2,1,0:T(8,128)(2,1)}, bf16[4,160,128]{2,1,0:T(8,128)(2,1)}, u32[]{:S(2)}, u32[]{:S(2)}) collective-permute-start(bf16[4,160,128]{2,1,0:T(8,128)(2,1)} %slice_bitcast_fusion), channel_id=1, source_target_pairs={{16,0},{20,4},{24,8},{28,12},{32,16},{36,20},{40,24},{44,28},{48,3... | collective-permute-start | bytes 491528 | tf_op jit(solution)/shard_map/ppermute | solution.py:355
  71.3 11.0 %all-to-all-start.2 = ((f32[16,8,128]{2,1,0:T(8,128)}), f32[16,8,128]{2,1,0:T(8,128)S(1)}, u32[]{:S(2)}, u32[]{:S(2)}) async-start(f32[16,8,128]{2,1,0:T(8,128)} %get-tuple-element.12), calls=%async_computation.2 | async-start | bytes 131072 | tf_op jit(solution)/shard_map/all_to_all | solution.py:337
  82.3 1.2 %copy-start.1 = (f32[16,120,128]{2,1,0:T(8,128)S(1)}, f32[16,120,128]{2,1,0:T(8,128)}, u32[]{:S(2)}) copy-start(f32[16,120,128]{2,1,0:T(8,128)} %wgrad.1.part_ref) | copy-start | bytes 2949124
  83.5 32.9 %copy-start.2 = (bf16[2,1,160,512]{3,2,1,0:T(8,128)(2,1)S(1)}, bf16[2,1,160,512]{3,2,1,0:T(8,128)(2,1)}, u32[]{:S(2)}) copy-start(bf16[2,1,160,512]{3,2,1,0:T(8,128)(2,1)} %param.5) | copy-start | bytes 983044
  83.5 32.9 %copy-start.3 = (f32[320,512]{1,0:T(8,128)S(1)}, f32[320,512]{1,0:T(8,128)}, u32[]{:S(2)}) copy-start(f32[320,512]{1,0:T(8,128)} %get-tuple-element.13.act_ref) | copy-start | bytes 1966084
  83.5 32.9 %copy-start.4 = (f32[16,512]{1,0:T(8,128)S(1)}, f32[16,512]{1,0:T(8,128)}, u32[]{:S(2)}) copy-start(f32[16,512]{1,0:T(8,128)} %get-tuple-element.11.norm_ref) | copy-start | bytes 98308
  83.5 32.9 %copy-start.5 = (f32[512]{0:T(512)S(1)}, f32[512]{0:T(512)}, u32[]{:S(2)}) copy-start(f32[512]{0:T(512)} %param.6) | copy-start | bytes 6148

commit v4 on v3

--- a/solution.py
+++ b/solution.py
@@ -11,6 +11,7 @@
 GROUPS = 32
 EPS = 1e-06
 TEAM = 4
+EDGES = ((0, -1), (0, 1), (1, 0), (1, -1), (1, 1))
 F32 = jnp.float32
 BF16 = jnp.bfloat16
 
@@ -19,15 +20,35 @@
     return lax.broadcasted_iota(jnp.int32, shape, dim)
 
 
-def exact_dot(a, b, dims=((1,), (0,))):
-    return lax.dot_general(
-        a, b, (dims, ((), ())), precision=lax.Precision.HIGHEST, preferred_element_type=F32
-    )
+def shift_of(value):
+    return value.bit_length() - 1
+
+
+def exact_dot(a, ones, dims=((1,), (0,))):
+    high = a.astype(BF16).astype(F32)
+    rest = a - high
+    mid = rest.astype(BF16).astype(F32)
+    parts = jnp.concatenate([high, mid, rest - mid, jnp.zeros_like(a)], axis=0).astype(BF16)
+    out = lax.dot_general(parts, ones, (dims, ((), ())), preferred_element_type=F32)
+    return out[0:8] + out[8:16] + out[16:24]
+
+
+def ones_where(mask):
+    return jnp.where(mask, 1.0, 0.0).astype(BF16)
 
 
 def members(chans, offset):
-    size = chans // GROUPS
-    return (iota((chans, 128), 0) // size + offset == iota((chans, 128), 1)).astype(F32)
+    bits = shift_of(chans // GROUPS)
+    return ones_where(lax.shift_right_logical(iota((chans, 128), 0), bits) == iota((chans, 128), 1) - offset)
+
+
+def sources(lane, chans, teams, spot):
+    step = chans // teams
+    return (lane & -step) * TEAM + spot * step + (lane & (step - 1))
+
+
+def sigmoid(value):
+    return 0.5 * jnp.tanh(0.5 * value) + 0.5
 
 
 def col_shifts(slab):
@@ -44,11 +65,10 @@
     cols = up_ref.shape[1]
     rows = load_ref.shape[1]
     feats = feats_ref[...]
-    lane = iota((chans, chans), 1)
     wide = chans // TEAM
-    step = chans // teams
-    source = (lane % wide) // step * (step * TEAM) + lane // wide * step + lane % step
-    mover = (iota((chans, chans), 0) == source).astype(BF16)
+    lane = iota((1, chans), 1)
+    source = sources(lane & (wide - 1), chans, teams, lax.shift_right_logical(lane, shift_of(wide)))
+    mover = ones_where(iota((chans, chans), 0) == source)
     moved = jnp.dot(feats, mover, preferred_element_type=F32).astype(BF16)
     outs = up_ref.shape[2] // rows
     for r in range(rows):
@@ -96,14 +116,16 @@
     out_ref[...] = jnp.broadcast_to(result[None], out_ref.shape)
 
 
-def dense_kernel(now_ref, later_ref, weight_ref, out_ref, slabs):
+def dense_kernel(
+    up_ref, above_ref, below_ref, later_ref, later_above_ref, later_below_ref, weight_ref, out_ref, slabs
+):
     step = pl.program_id(0)
     time_tap = step // 3
     row_tap = step % 3
     time_index = lax.axis_index("tm")
     row_index = lax.axis_index("rows")
     positions = out_ref.shape[0]
-    cols = now_ref.shape[2]
+    cols = up_ref.shape[1]
 
     @pl.when(step == 0)
     def _():
@@ -112,10 +134,10 @@
         up_ok = (row_index > 0).astype(F32)
         down_ok = (row_index < lax.axis_size("rows") - 1).astype(F32)
         for f in range(4):
-            source = now_ref if f < 2 else later_ref
+            trio = (above_ref, up_ref, below_ref) if f < 2 else (later_above_ref, later_ref, later_below_ref)
             tail = jnp.float32(1.0) if f < 2 else more
-            for r, keep in ((0, up_ok), (1, jnp.float32(1.0)), (2, down_ok)):
-                slab = (source[r, f % 2].astype(F32) * (keep * tail)).astype(BF16)
+            for r, keep in enumerate((up_ok, jnp.float32(1.0), down_ok)):
+                slab = (trio[r][f % 2].astype(F32) * (keep * tail)).astype(BF16)
                 for c, moved in enumerate(col_shifts(slab)):
                     slabs[c, r, f] = moved
 
@@ -170,7 +192,7 @@
     inverse = inverse[0:1]
     normed = (feats_ref[...].astype(F32) - centre) * inverse
     preact = normed * gain_ref[...] + bias_ref[...]
-    sig = 1.0 / (1.0 + jnp.exp(-preact))
+    sig = sigmoid(preact)
     act = dense_ref[...] * sig * (1.0 + preact * (1.0 - sig))
     act_ref[...] = act
     gains = jnp.sum(act * normed, axis=0, keepdims=True)
@@ -196,9 +218,9 @@
     chans = gain_ref.shape[1]
     wide = chans // TEAM
     step = chans // teams
-    spot = time_index % TEAM
-    lane = iota((chans, wide), 1)
-    mover = (iota((chans, wide), 0) == lane // step * (step * TEAM) + spot * step + lane % step).astype(F32)
+    mover = ones_where(
+        iota((chans, wide), 0) == sources(iota((1, wide), 1), chans, teams, time_index & (TEAM - 1))
+    )
 
     def slice_of(value):
         return exact_dot(value, mover)[0:1]
@@ -210,7 +232,7 @@
 
     def silu(value):
         preact = (value.astype(F32) - centre) * inverse * gain + bias
-        return (preact * (1.0 / (1.0 + jnp.exp(-preact)))).astype(BF16)
+        return (preact * sigmoid(preact)).astype(BF16)
 
     frames = 2 * TEAM
     for f in range(frames + 2):
@@ -339,8 +361,15 @@
     def in_ranks(value):
         return lax.all_to_all(value, "tm", 0, 0, tiled=True, axis_index_groups=ranks)
 
-    above = lax.ppermute(ups, "rows", [(i, (i + 1) % rows) for i in range(rows)])
-    below = lax.ppermute(ups, "rows", [((i + 1) % rows, i) for i in range(rows)])
+    def neighbour(tm_step, row_step):
+        pairs = [
+            (((t + tm_step) % tms) * rows + (r + row_step) % rows, t * rows + r)
+            for t in range(tms)
+            for r in range(rows)
+        ]
+        return lax.ppermute(ups, ("tm", "rows"), pairs)
+
+    halos = [neighbour(a, b) for a, b in EDGES]
 
     load = pl.pallas_call(
         functools.partial(pack_kernel, tms),
@@ -350,8 +379,6 @@
     )(feats, ups)
     load = in_teams(load.reshape(size, length, wide)).reshape(TEAM, rows, length, wide)
 
-    now = jnp.stack([above, ups, below])
-    later = lax.ppermute(now, "tm", [((i + 1) % tms, i) for i in range(tms)])
     halo = lax.ppermute(
         load[0, :, positions : positions + cols], "tm", [((i + TEAM) % tms, i) for i in range(tms)]
     )
@@ -363,7 +390,7 @@
         dense_kernel,
         grid=(9,),
         in_specs=[
-            whole((3, frames, cols, outs)), whole((3, frames, cols, outs)),
+            *[whole((frames, cols, outs))] * 6,
             pl.BlockSpec((1, 1, 3, chans, outs), lambda s: (s // 3, s % 3, 0, 0, 0)),
         ],
         out_specs=whole((positions, chans)),
@@ -372,7 +399,7 @@
         compiler_params=params(62),
         name="dense",
     )
-    dense = dense_call(now, later, weight)
+    dense = dense_call(ups, *halos, weight)
 
     stats = pl.pallas_call(
         functools.partial(combine_kernel, float(positions * (chans // GROUPS))),

time: 119 us -> 117 us (0.983)
  the two profiles are of different devices: /device:TPU:0 before, /device:TPU:32 now
where the time goes in v4:
time: 117 us; the launch traced here: 116 us
  starting transfers between devices  41 us (35%)
  blocking collectives  32.1 us (27%)
  Pallas kernels  25.1 us (21%)
  waiting for transfers between devices  14.2 us (12%)
  local copies, waits for them, and re-layouts  3.25 us (3%)
    all_to_all x1, blocking collectives, in_ranks(): lax.all_to_all(value, 'tm', 0, 0, tiled=True, axis_index_groups=ranks)  32.1 us
    all_to_all x2, waiting for transfers between devices, in_teams(): lax.all_to_all(value, ('tm', 'rows'), 0, 0, tiled=True, axis_index_groups...  14.2 us
    ppermute x5, starting transfers between devices, neighbour(): return lax.ppermute(ups, ('tm', 'rows'), pairs)  13 us
    all_to_all x2, starting transfers between devices, in_teams(): lax.all_to_all(value, ('tm', 'rows'), 0, 0, tiled=True, axis_index_groups...  12.3 us
    pallas_call x1, Pallas kernels, on_device(): dense = dense_call(ups, *halos, weight)  9.8 us
    all_to_all x1, starting transfers between devices, in_ranks(): lax.all_to_all(value, 'tm', 0, 0, tiled=True, axis_index_groups=ranks)  9.64 us
    pallas_call x1, Pallas kernels, on_device(): part = weight_call(load, halo, norm, gain, bias)  7.07 us
    ppermute x1, starting transfers between devices, on_device(): lax.ppermute(load[0, :, positions:positions + cols], 'tm', [((i + TEAM) %...  6.1 us
  transfers between devices with their start and end apart: 9, of which 1 were waited for; matrix products, arithmetic and copies ran while one was open for 1% of the time, Pallas kernels for 18%

profile of v4, /device:TPU:32, one launch (start us, length us, event | category | flops | bytes accessed | tf_op | source)
XLA Modules:
  0.0 116.5 jit_solution(14095399929184733450)
XLA Ops:
  0.6 3.1 %pack.1 = bf16[4,4,496,128]{3,2,1,0:T(8,128)(2,1)} custom-call(bf16[320,512]{1,0:T(8,128)(2,1)} %bitcast.17, bf16[2,160,256]{2,1,0:T(8,128)(2,1)} %bitcast.24), custom_call_target="tpu_custom_call" | custom-call | tf_op jit(solution)/shard_map/pack/pallas_call | solution.py:374
  3.7 6.1 %all-to-all-start = ((bf16[16,496,128]{2,1,0:T(8,128)(2,1)}), bf16[16,496,128]{2,1,0:T(8,128)(2,1)S(1)}, u32[]{:S(2)}, u32[]{:S(2)}) async-start(bf16[16,496,128]{2,1,0:T(8,128)(2,1)} %bitcast.23), calls=%async_computation | async-start | bytes 4063232 | tf_op jit(solution)/shard_map/all_to_all | solution.py:359
  9.8 1.5 %collective-permute-start.1 = (bf16[2,160,256]{2,1,0:T(8,128)(2,1)S(1)}, bf16[2,160,256]{2,1,0:T(8,128)(2,1)S(1)}, u32[]{:S(2)}, u32[]{:S(2)}) collective-permute-start(bf16[2,160,256]{2,1,0:T(8,128)(2,1)S(1)} %bitcast.26), channel_id=1, source_target_pairs={{3,0},{0,1},{1,2},{2,3},{7,4},{4,5},{5,6},{6,7},{11,8},{8,9},{9,10... | collective-permute-start | bytes 491528 | tf_op jit(solution)/shard_map/ppermute | solution.py:370
  11.4 1.8 %collective-permute-start.2 = (bf16[2,160,256]{2,1,0:T(8,128)(2,1)S(1)}, bf16[2,160,256]{2,1,0:T(8,128)(2,1)S(1)}, u32[]{:S(2)}, u32[]{:S(2)}) collective-permute-start(bf16[2,160,256]{2,1,0:T(8,128)(2,1)S(1)} %bitcast.27), channel_id=1, source_target_pairs={{1,0},{2,1},{3,2},{0,3},{5,4},{6,5},{7,6},{4,7},{9,8},{10,9},{11,1... | collective-permute-start | bytes 491528 | tf_op jit(solution)/shard_map/ppermute | solution.py:370
  13.1 0.0 collective-permute-start.3
  13.1 0.4 collective-permute-start.4
  13.5 9.4 %collective-permute-start.5 = (bf16[2,160,256]{2,1,0:T(8,128)(2,1)S(1)}, bf16[2,160,256]{2,1,0:T(8,128)(2,1)}, u32[]{:S(2)}, u32[]{:S(2)}) collective-permute-start(bf16[2,160,256]{2,1,0:T(8,128)(2,1)S(1)} %bitcast.30), channel_id=1, source_target_pairs={{5,0},{6,1},{7,2},{4,3},{9,4},{10,5},{11,6},{8,7},{13,8},{14,9},{1... | collective-permute-start | bytes 491528 | tf_op jit(solution)/shard_map/ppermute | solution.py:370
  22.9 14.2 %all-to-all-done = bf16[16,496,128]{2,1,0:T(8,128)(2,1)S(1)} async-done(((bf16[16,496,128]{2,1,0:T(8,128)(2,1)}), bf16[16,496,128]{2,1,0:T(8,128)(2,1)S(1)}, u32[]{:S(2)}, u32[]{:S(2)}) %all-to-all-start) | async-done | bytes 2031648 | tf_op jit(solution)/shard_map/all_to_all | solution.py:359
  37.1 0.9 combine.1
  37.9 9.6 %all-to-all-start.1 = ((f32[16,8,128]{2,1,0:T(8,128)}), f32[16,8,128]{2,1,0:T(8,128)}, u32[]{:S(2)}, u32[]{:S(2)}) async-start(f32[16,8,128]{2,1,0:T(8,128)} %combine.1), calls=%async_computation.1 | async-start | bytes 131072 | tf_op jit(solution)/shard_map/all_to_all | solution.py:362
  47.6 0.7 slice_bitcast_fusion
  48.3 0.0 collective-permute-done.1.above_ref
  48.3 6.1 %collective-permute-start = (bf16[4,160,128]{2,1,0:T(8,128)(2,1)}, bf16[4,160,128]{2,1,0:T(8,128)(2,1)}, u32[]{:S(2)}, u32[]{:S(2)}) collective-permute-start(bf16[4,160,128]{2,1,0:T(8,128)(2,1)} %slice_bitcast_fusion), channel_id=1, source_target_pairs={{16,0},{20,4},{24,8},{28,12},{32,16},{36,20},{40,24},{44,28},{48,3... | collective-permute-start | bytes 491528 | tf_op jit(solution)/shard_map/ppermute | solution.py:382
  54.4 0.0 collective-permute-done.3.later_ref
  54.4 0.6 copy-done.8
  55.1 0.1 copy-done.9
  55.1 0.7 copy-done.10
  55.8 9.8 %dense.1.dense_ref = f32[320,512]{1,0:T(8,128)} custom-call(bf16[2,160,256]{2,1,0:T(8,128)(2,1)} %bitcast.25, bf16[2,160,256]{2,1,0:T(8,128)(2,1)} %copy-done.7, bf16[2,160,256]{2,1,0:T(8,128)(2,1)} %copy-done.8, bf16[2,160,256]{2,1,0:T(8,128)(2,1)} %copy-done.9, bf16[2,160,256]{2,1,0:T(8,128)(2,1)} %copy-done.10, ...), custom_call_target="tpu_custom_call" | custom-call | tf_op jit(solution)/shard_map/dense/pallas_call | solution.py:402
  65.6 2.9 %act.1 = (f32[320,512]{1,0:T(8,128)}, f32[16,8,128]{2,1,0:T(8,128)}, f32[16,512]{1,0:T(8,128)}) custom-call(bf16[320,512]{1,0:T(8,128)(2,1)} %bitcast.18, f32[1,512]{1,0:T(1,128)} %bitcast.20, f32[1,512]{1,0:T(1,128)} %bitcast.31, f32[16,8,128]{2,1,0:T(8,128)} %all-to-all-done.1.stats_ref, f32[320,512]{1,0:T(8,128)} %dense.1.dense_ref), custom_call_target="tpu_custom_call" | custom-call | tf_op jit(solution)/shard_map/act/pallas_call | solution.py:414
  68.4 6.2 %all-to-all-start.2 = ((f32[16,8,128]{2,1,0:T(8,128)}), f32[16,8,128]{2,1,0:T(8,128)S(1)}, u32[]{:S(2)}, u32[]{:S(2)}) async-start(f32[16,8,128]{2,1,0:T(8,128)} %get-tuple-element.12), calls=%async_computation.2 | async-start | bytes 131072 | tf_op jit(solution)/shard_map/all_to_all | solution.py:359
  74.6 7.1 %wgrad.1.part_ref = f32[16,120,128]{2,1,0:T(8,128)} custom-call(bf16[4,4,496,128]{3,2,1,0:T(8,128)(2,1)} %bitcast.16, bf16[4,160,128]{2,1,0:T(8,128)(2,1)} %collective-permute-done.halo_ref, f32[16,512]{1,0:T(8,128)} %get-tuple-element.11.norm_ref, f32[1,512]{1,0:T(1,128)} %bitcast.21, f32[1,512]{1,0:T(1,128)} %bitcast.32), custom_call_target="tpu_custom_call" | custom-call | tf_op jit(solution)/shard_map/wgrad/pallas_call | solution.py:439
  81.7 1.2 %copy-done.1 = f32[16,120,128]{2,1,0:T(8,128)S(1)} copy-done((f32[16,120,128]{2,1,0:T(8,128)S(1)}, f32[16,120,128]{2,1,0:T(8,128)}, u32[]{:S(2)}) %copy-start.1) | copy-done | bytes 983064
  82.9 32.1 %all_to_all.20.load_ref = f32[16,120,128]{2,1,0:T(8,128)S(1)} all-to-all(f32[16,120,128]{2,1,0:T(8,128)S(1)} %append.1), channel_id=1, replica_groups={{0,16,32,48,64,80,96,112,128,144,160,176,192,208,224,240},{4,20,36,52,6..., dimensions={0} | all-to-all | bytes 1966080 | tf_op jit(solution)/shard_map/all_to_all | solution.py:362
  115.1 1.4 %final.1 = (bf16[320,512]{1,0:T(8,128)(2,1)}, f32[9,3,8,64]{3,2,1,0:T(8,128)}, f32[1,512]{1,0:T(1,128)}, f32[1,512]{1,0:T(1,128)}) custom-call(f32[16,120,128]{2,1,0:T(8,128)S(1)} %all_to_all.20.load_ref, f32[320,512]{1,0:T(8,128)S(1)} %copy-done.3, bf16[320,512]{1,0:T(8,128)(2,1)S(1)} %bitcast.19, f32[16,512]{1,0:T(8,128)S(1)} %copy-done.4, ...), custom_call_target="tpu_custom_call" | custom-call | tf_op jit(solution)/shard_map/final/pallas_call | solution.py:451
  (25 shorter events, 0.1 us)
Async XLA Ops:
  3.7 6.1 %copy-start.6 = (bf16[2,1,160,256]{3,2,1,0:T(8,128)(2,1)S(1)}, bf16[2,1,160,256]{3,2,1,0:T(8,128)(2,1)}, u32[]{:S(2)}) copy-start(bf16[2,1,160,256]{3,2,1,0:T(8,128)(2,1)} %param.9) | copy-start | bytes 491524
  3.7 33.3 %all-to-all-start = ((bf16[16,496,128]{2,1,0:T(8,128)(2,1)}), bf16[16,496,128]{2,1,0:T(8,128)(2,1)S(1)}, u32[]{:S(2)}, u32[]{:S(2)}) async-start(bf16[16,496,128]{2,1,0:T(8,128)(2,1)} %bitcast.23), calls=%async_computation | async-start | bytes 4063232 | tf_op jit(solution)/shard_map/all_to_all | solution.py:359
  9.8 38.5 %collective-permute-start.1 = (bf16[2,160,256]{2,1,0:T(8,128)(2,1)S(1)}, bf16[2,160,256]{2,1,0:T(8,128)(2,1)S(1)}, u32[]{:S(2)}, u32[]{:S(2)}) collective-permute-start(bf16[2,160,256]{2,1,0:T(8,128)(2,1)S(1)} %bitcast.26), channel_id=1, source_target_pairs={{3,0},{0,1},{1,2},{2,3},{7,4},{4,5},{5,6},{6,7},{11,8},{8,9},{9,10... | collective-permute-start | bytes 491528 | tf_op jit(solution)/shard_map/ppermute | solution.py:370
  11.4 43.0 %collective-permute-start.2 = (bf16[2,160,256]{2,1,0:T(8,128)(2,1)S(1)}, bf16[2,160,256]{2,1,0:T(8,128)(2,1)S(1)}, u32[]{:S(2)}, u32[]{:S(2)}) collective-permute-start(bf16[2,160,256]{2,1,0:T(8,128)(2,1)S(1)} %bitcast.27), channel_id=1, source_target_pairs={{1,0},{2,1},{3,2},{0,3},{5,4},{6,5},{7,6},{4,7},{9,8},{10,9},{11,1... | collective-permute-start | bytes 491528 | tf_op jit(solution)/shard_map/ppermute | solution.py:370
  13.1 41.3 %collective-permute-start.3 = (bf16[2,160,256]{2,1,0:T(8,128)(2,1)S(1)}, bf16[2,160,256]{2,1,0:T(8,128)(2,1)S(1)}, u32[]{:S(2)}, u32[]{:S(2)}) collective-permute-start(bf16[2,160,256]{2,1,0:T(8,128)(2,1)S(1)} %bitcast.28), channel_id=1, source_target_pairs={{4,0},{5,1},{6,2},{7,3},{8,4},{9,5},{10,6},{11,7},{12,8},{13,9},{1... | collective-permute-start | bytes 491528 | tf_op jit(solution)/shard_map/ppermute | solution.py:370
  13.1 41.3 %collective-permute-start.4 = (bf16[2,160,256]{2,1,0:T(8,128)(2,1)S(1)}, bf16[2,160,256]{2,1,0:T(8,128)(2,1)S(1)}, u32[]{:S(2)}, u32[]{:S(2)}) collective-permute-start(bf16[2,160,256]{2,1,0:T(8,128)(2,1)S(1)} %bitcast.29), channel_id=1, source_target_pairs={{7,0},{4,1},{5,2},{6,3},{11,4},{8,5},{9,6},{10,7},{15,8},{12,9},{1... | collective-permute-start | bytes 491528 | tf_op jit(solution)/shard_map/ppermute | solution.py:370
  13.5 42.3 %collective-permute-start.5 = (bf16[2,160,256]{2,1,0:T(8,128)(2,1)S(1)}, bf16[2,160,256]{2,1,0:T(8,128)(2,1)}, u32[]{:S(2)}, u32[]{:S(2)}) collective-permute-start(bf16[2,160,256]{2,1,0:T(8,128)(2,1)S(1)} %bitcast.30), channel_id=1, source_target_pairs={{5,0},{6,1},{7,2},{4,3},{9,4},{10,5},{11,6},{8,7},{13,8},{14,9},{1... | collective-permute-start | bytes 491528 | tf_op jit(solution)/shard_map/ppermute | solution.py:370
  37.1 28.5 %copy-start = (bf16[16,496,128]{2,1,0:T(8,128)(2,1)}, bf16[16,496,128]{2,1,0:T(8,128)(2,1)S(1)}, u32[]{:S(2)}) copy-start(bf16[16,496,128]{2,1,0:T(8,128)(2,1)S(1)} %all-to-all-done) | copy-start | bytes 6094852
  37.9 27.6 %all-to-all-start.1 = ((f32[16,8,128]{2,1,0:T(8,128)}), f32[16,8,128]{2,1,0:T(8,128)}, u32[]{:S(2)}, u32[]{:S(2)}) async-start(f32[16,8,128]{2,1,0:T(8,128)} %combine.1), calls=%async_computation.1 | async-start | bytes 131072 | tf_op jit(solution)/shard_map/all_to_all | solution.py:362
  48.3 6.1 %copy-start.7 = (bf16[2,160,256]{2,1,0:T(8,128)(2,1)}, bf16[2,160,256]{2,1,0:T(8,128)(2,1)S(1)}, u32[]{:S(2)}) copy-start(bf16[2,160,256]{2,1,0:T(8,128)(2,1)S(1)} %collective-permute-done.1.above_ref) | copy-start | bytes 491524
  48.3 26.3 %collective-permute-start = (bf16[4,160,128]{2,1,0:T(8,128)(2,1)}, bf16[4,160,128]{2,1,0:T(8,128)(2,1)}, u32[]{:S(2)}, u32[]{:S(2)}) collective-permute-start(bf16[4,160,128]{2,1,0:T(8,128)(2,1)} %slice_bitcast_fusion), channel_id=1, source_target_pairs={{16,0},{20,4},{24,8},{28,12},{32,16},{36,20},{40,24},{44,28},{48,3... | collective-permute-start | bytes 491528 | tf_op jit(solution)/shard_map/ppermute | solution.py:382
  54.4 0.7 copy-start.8
  54.4 0.7 copy-start.9
  55.1 0.7 copy-start.10
  68.4 13.3 %all-to-all-start.2 = ((f32[16,8,128]{2,1,0:T(8,128)}), f32[16,8,128]{2,1,0:T(8,128)S(1)}, u32[]{:S(2)}, u32[]{:S(2)}) async-start(f32[16,8,128]{2,1,0:T(8,128)} %get-tuple-element.12), calls=%async_computation.2 | async-start | bytes 131072 | tf_op jit(solution)/shard_map/all_to_all | solution.py:359
  81.7 1.2 %copy-start.1 = (f32[16,120,128]{2,1,0:T(8,128)S(1)}, f32[16,120,128]{2,1,0:T(8,128)}, u32[]{:S(2)}) copy-start(f32[16,120,128]{2,1,0:T(8,128)} %wgrad.1.part_ref) | copy-start | bytes 2949124
  82.9 32.2 %copy-start.2 = (bf16[2,1,160,512]{3,2,1,0:T(8,128)(2,1)S(1)}, bf16[2,1,160,512]{3,2,1,0:T(8,128)(2,1)}, u32[]{:S(2)}) copy-start(bf16[2,1,160,512]{3,2,1,0:T(8,128)(2,1)} %param.5) | copy-start | bytes 983044
  82.9 32.2 %copy-start.3 = (f32[320,512]{1,0:T(8,128)S(1)}, f32[320,512]{1,0:T(8,128)}, u32[]{:S(2)}) copy-start(f32[320,512]{1,0:T(8,128)} %get-tuple-element.13.act_ref) | copy-start | bytes 1966084
  82.9 32.2 %copy-start.4 = (f32[16,512]{1,0:T(8,128)S(1)}, f32[16,512]{1,0:T(8,128)}, u32[]{:S(2)}) copy-start(f32[16,512]{1,0:T(8,128)} %get-tuple-element.11.norm_ref) | copy-start | bytes 98308
  82.9 32.2 %copy-start.5 = (f32[512]{0:T(512)S(1)}, f32[512]{0:T(512)}, u32[]{:S(2)}) copy-start(f32[512]{0:T(512)} %param.6) | copy-start | bytes 6148

commit v5 on v4

--- a/solution.py
+++ b/solution.py
@@ -42,9 +42,11 @@
     return ones_where(lax.shift_right_logical(iota((chans, 128), 0), bits) == iota((chans, 128), 1) - offset)
 
 
-def sources(lane, chans, teams, spot):
-    step = chans // teams
-    return (lane & -step) * TEAM + spot * step + (lane & (step - 1))
+def sources(lane, step, chip, core):
+    owner = lax.shift_right_logical(lane, shift_of(step))
+    place = lax.shift_right_logical(owner, 2) * 32 + (owner & 3) * 4
+    place = place + lax.shift_right_logical(chip, 1) * 16 + (chip & 1) * 2 + core
+    return place * step + (lane & (step - 1))
 
 
 def sigmoid(value):
@@ -65,19 +67,31 @@
     cols = up_ref.shape[1]
     rows = load_ref.shape[1]
     feats = feats_ref[...]
-    wide = chans // TEAM
+    core = lax.axis_index("tm") & 1
     lane = iota((1, chans), 1)
-    source = sources(lane & (wide - 1), chans, teams, lax.shift_right_logical(lane, shift_of(wide)))
+    source = sources(
+        lane & 63, chans // teams, lax.shift_right_logical(lane, 7), lax.shift_right_logical(lane, 6) & 1
+    )
     mover = ones_where(iota((chans, chans), 0) == source)
-    moved = jnp.dot(feats, mover, preferred_element_type=F32).astype(BF16)
+    moved = jnp.dot(feats, mover, preferred_element_type=F32)
     outs = up_ref.shape[2] // rows
+    left = iota((cols, 128), 1) < 64
+    for j in range(TEAM):
+        early = moved[0:cols, j * 128 : (j + 1) * 128]
+        late = moved[cols:, j * 128 : (j + 1) * 128]
+        lower = jnp.where(left, early, pltpu.roll(late, 64, 1)).astype(BF16)
+        upper = jnp.where(left, pltpu.roll(early, 64, 1), late).astype(BF16)
+        keep = jnp.where(core == 0, lower, upper)
+        send = jnp.where(core == 0, upper, lower)
+        for r in range(rows):
+            load_ref[j, r, 0:cols, :] = keep
+            load_ref[j, r, cols : 2 * cols, :] = send
     for r in range(rows):
         pair = jnp.concatenate(
             [up_ref[0, :, r * outs : (r + 1) * outs], up_ref[1, :, r * outs : (r + 1) * outs]], axis=1
         )
         for j in range(TEAM):
-            load_ref[j, r, 0:positions, :] = moved[:, j * wide : (j + 1) * wide]
-            load_ref[j, r, positions : positions + cols, :] = pair
+            load_ref[j, r, 2 * cols : 3 * cols, :] = pair
     floats = feats.astype(F32)
     first = members(chans, 0)
     second = members(chans, GROUPS)
@@ -94,7 +108,7 @@
     parts = jnp.concatenate([parts, jnp.zeros_like(parts)], axis=0).astype(BF16)
     for r in range(rows):
         for j in range(TEAM):
-            load_ref[j, r, positions + cols :, :] = parts
+            load_ref[j, r, 3 * cols :, :] = parts
 
 
 def combine_kernel(count, load_ref, out_ref):
@@ -211,16 +225,18 @@
     out_ref[:, out_ref.shape[1] - total.shape[0] :, :] = jnp.broadcast_to(total[None], place)
 
 
-def weight_kernel(teams, load_ref, halo_ref, norm_ref, gain_ref, bias_ref, out_ref, hidden, acc):
+def weight_kernel(
+    teams, load_ref, other_ref, halo0_ref, halo1_ref, moved0_ref, moved1_ref, norm_ref, gain_ref, bias_ref,
+    out_ref, hidden, acc,
+):
     time_index = lax.axis_index("tm")
+    core = time_index & 1
     rows = load_ref.shape[1]
-    cols = hidden.shape[2]
+    cols = hidden.shape[3]
     chans = gain_ref.shape[1]
-    wide = chans // TEAM
     step = chans // teams
-    mover = ones_where(
-        iota((chans, wide), 0) == sources(iota((1, wide), 1), chans, teams, time_index & (TEAM - 1))
-    )
+    chip = (lax.shift_right_logical(time_index, 4) & 1) * 2 + (lax.shift_right_logical(time_index, 1) & 1)
+    mover = ones_where(iota((chans, 128), 0) == sources(iota((1, 128), 1) & 63, step, chip, core))
 
     def slice_of(value):
         return exact_dot(value, mover)[0:1]
@@ -229,69 +245,79 @@
     inverse = slice_of(norm_ref[8:16])
     gain = slice_of(jnp.broadcast_to(gain_ref[...], (8, chans)))
     bias = slice_of(jnp.broadcast_to(bias_ref[...], (8, chans)))
-
-    def silu(value):
-        preact = (value.astype(F32) - centre) * inverse * gain + bias
-        return (preact * sigmoid(preact)).astype(BF16)
-
-    frames = 2 * TEAM
-    for f in range(frames + 2):
-        hidden[f, 0] = jnp.zeros(hidden.shape[2:], BF16)
-        hidden[f, rows + 1] = jnp.zeros(hidden.shape[2:], BF16)
-    opening = (time_index < TEAM).astype(F32)
-    for j in range(TEAM):
-        for r in range(rows):
-            for f in range(2):
-                value = silu(load_ref[j, r, f * cols : (f + 1) * cols, :])
-                hidden[2 + 2 * j + f, 1 + r] = value
-                if j == 0 and f == 0:
-                    value = (value.astype(F32) * opening).astype(BF16)
-                    hidden[0, 1 + r] = value
-                    hidden[1, 1 + r] = value
-
-    lanes = iota((cols, 128), 1) < 64
-    more = (time_index < lax.axis_size("tm") - TEAM).astype(F32)
-    for j in range(TEAM + 1):
-        halves = [[], []]
-        for r in range(rows):
-            if j < TEAM:
-                pair = load_ref[j, r, 2 * cols : 3 * cols, :].astype(F32)
-            else:
-                pair = halo_ref[r].astype(F32) * more
-            row = iota(pair.shape, 0)
-            ahead = jnp.where(row < cols - 1, pltpu.roll(pair, cols - 1, 0), 0.0)
-            behind = jnp.where(row > 0, pltpu.roll(pair, 1, 0), 0.0)
-            left = jnp.where(lanes, ahead, pltpu.roll(pair, 64, 1))
-            right = jnp.where(lanes, pltpu.roll(ahead, 64, 1), pair)
-            halves[0].append(jnp.concatenate([left, behind[:, 0:64]], axis=1))
-            halves[1].append(jnp.concatenate([right, behind[:, 64:128]], axis=1))
-        for f in range(2):
-            ups = jnp.concatenate(halves[f], axis=0).astype(BF16)
-            frame = 2 * j + f
-            depth = min(3, frames + 2 - frame)
+    left = iota((cols, 128), 1) < 64
+    start = (time_index & ~19) == 0
+    end = (time_index | 19) == lax.axis_size("tm") - 1
+
+    for x in range(2):
+        for q in range(6):
+            hidden[x, q, 0] = jnp.zeros(hidden.shape[3:], BF16)
+            hidden[x, q, rows + 1] = jnp.zeros(hidden.shape[3:], BF16)
+        for q in range(4):
+            for r in range(rows):
+                j = 2 * x + q // 2
+                pair = jnp.where(core == q % 2, load_ref[j, r, 0:cols, :], other_ref[j, r, 0:cols, :])
+                preact = (pair.astype(F32) - centre) * inverse * gain + bias
+                value = preact * sigmoid(preact)
+                hidden[x, q + 1, r + 1] = value.astype(BF16)
+                if q == 0:
+                    before = jnp.zeros_like(value)
+                    if x == 0:
+                        before = jnp.where(start, jnp.where(left, value, pltpu.roll(value, 64, 1)), before)
+                    hidden[x, 0, r + 1] = before.astype(BF16)
+                    hidden[x, 5, r + 1] = jnp.zeros(hidden.shape[3:], BF16)
+
+    for x in range(2):
+        for q in range(5):
+            sides = [[], [], []]
+            for r in range(rows):
+                j = 2 * x + q // 2
+                if q < 4:
+                    pair = jnp.where(
+                        core == q % 2, load_ref[j, r, 2 * cols : 3 * cols, :], other_ref[j, r, cols : 2 * cols, :]
+                    )
+                else:
+                    near, far = ((halo0_ref, moved0_ref), (halo1_ref, moved1_ref))[x]
+                    pair = jnp.where(core == 0, near[r], far[r])
+                wide = pair.astype(F32)
+                if q == 4 and x == 1:
+                    wide = jnp.where(end, 0.0, wide)
+                row = iota(wide.shape, 0)
+                sides[0].append(jnp.where(row < cols - 1, pltpu.roll(wide, cols - 1, 0), 0.0).astype(BF16))
+                sides[1].append(wide.astype(BF16))
+                sides[2].append(jnp.where(row > 0, pltpu.roll(wide, 1, 0), 0.0).astype(BF16))
+            ups = jnp.concatenate([jnp.concatenate(side, axis=0) for side in sides], axis=1)
             taps = [
-                hidden[frame + a, b : b + rows].reshape(rows * cols, wide) for a in range(depth) for b in range(3)
+                hidden[x, q + n, b : b + rows].reshape(rows * cols, 128) for b in range(3) for n in range(2)
             ]
             term = lax.dot_general(
                 ups, jnp.concatenate(taps, axis=1), (((0,), (0,)), ((), ())), preferred_element_type=F32
             )
-            if frame == 0:
+            if x == 0 and q == 0:
                 acc[...] = term
             else:
-                acc[:, 0 : 3 * depth * wide] += term
+                acc[...] += term
 
     groups = out_ref.shape[0]
-    tail = None
-    for ab in range(9):
-        block = acc[:, ab * wide : (ab + 1) * wide].T
-        out_ref[:, ab * step : (ab + 1) * step, :] = block[:, 0:128].reshape(groups, step, 128)
-        last = block[:, 128:192]
-        if ab % 2 == 0:
-            tail = last
-        if ab % 2 == 1 or ab == 8:
-            both = jnp.concatenate([tail, last], axis=1)
-            at = (9 + ab // 2) * step
-            out_ref[:, at : at + step, :] = both.reshape(groups, step, 128)
+    low = iota((192, 128), 1) < 64
+
+    def store(index, block):
+        out_ref[:, index * step : (index + 1) * step, :] = block.reshape(groups, step, 128)
+
+    thirds = []
+    for b in range(3):
+        blocks = [acc[c * 128 : (c + 1) * 128, b * 256 : (b + 1) * 256].T for c in range(3)]
+        first = blocks[0][0:192] + pltpu.roll(blocks[0][64:256], 64, 1)
+        second = pltpu.roll(blocks[1][0:192], 64, 1) + blocks[1][64:256]
+        both = jnp.where(low, first, second)
+        for a in range(3):
+            store(3 * a + b, both[a * 64 : (a + 1) * 64])
+        thirds.append(blocks[2][0:192] + pltpu.roll(blocks[2][64:256], 64, 1))
+    both = jnp.where(low, thirds[0], pltpu.roll(thirds[1], 64, 1))
+    for a in range(3):
+        store(9 + a, both[a * 64 : (a + 1) * 64])
+    store(12, jnp.where(low[0:64], thirds[2][0:64], pltpu.roll(thirds[2][64:128], 64, 1)))
+    store(13, thirds[2][128:192])
 
 
 def final_kernel(
@@ -303,13 +329,14 @@
     total = load_ref[0]
     for g in range(1, load_ref.shape[0]):
         total = total + load_ref[g]
-    for ab in range(9):
-        part = total[ab * step : (ab + 1) * step]
-        grad_ref[ab, 0] = part[:, 0:64]
-        grad_ref[ab, 1] = part[:, 64:128]
-        at = (9 + ab // 2) * step
-        side = 64 * (ab % 2)
-        grad_ref[ab, 2] = total[at : at + step, side : side + 64]
+    for a in range(3):
+        for b in range(3):
+            part = total[(3 * a + b) * step : (3 * a + b + 1) * step]
+            grad_ref[3 * a + b, 0] = part[:, 0:64]
+            grad_ref[3 * a + b, 1] = part[:, 64:128]
+            index = 9 + a if b < 2 else 12 + a // 2
+            side = 64 * (b if b < 2 else a % 2)
+            grad_ref[3 * a + b, 2] = total[index * step : (index + 1) * step, side : side + 64]
     total = total[14 * step :]
     gains = jnp.concatenate([total[p : p + 1] for p in range(pieces)], axis=1)
     biases = jnp.concatenate([total[pieces + p : pieces + p + 1] for p in range(pieces)], axis=1)
@@ -338,7 +365,7 @@
     devices = tms * rows
     positions = frames * rows_dev * cols
     step = chans // tms
-    groups = tms // TEAM
+    groups = tms // (2 * TEAM)
     wide = chans // TEAM
     count = positions * devices * (chans // GROUPS)
     vmem = pl.BlockSpec(memory_space=pltpu.VMEM)
@@ -352,22 +379,37 @@
     bias = norm_bias.reshape(1, chans)
     size = TEAM * rows
     length = positions + cols + 16
-    teams = [[size * g + i for i in range(size)] for g in range(groups)]
-    ranks = [[TEAM * g + j for g in range(groups)] for j in range(TEAM)]
+    places = [(big, z) for big in range(groups // 4) for z in range(4)]
+    chips = [(x, z) for x in range(2) for z in range(2)]
+
+    def place(outer, inner, core):
+        return outer[0] * 32 + inner[0] * 16 + outer[1] * 4 + inner[1] * 2 + core
+
+    every = range(rows)
+    teams = [[place(o, i, c) * rows + r for i in chips for r in every] for o in places for c in range(2)]
+    pairs = [[place(o, i, c) * rows + r for i in chips for c in range(2) for r in every] for o in places]
+    stars = [[place(o, i, c) for o in places for c in range(2)] for i in chips]
+    ranks = [[place(o, i, c) for o in places] for i in chips for c in range(2)]
 
     def in_teams(value):
         return lax.all_to_all(value, ("tm", "rows"), 0, 0, tiled=True, axis_index_groups=teams)
 
+    def in_pairs(value):
+        return lax.all_to_all(value, ("tm", "rows"), 0, 0, tiled=True, axis_index_groups=pairs)
+
+    def in_stars(value):
+        return lax.all_to_all(value, "tm", 0, 0, tiled=True, axis_index_groups=stars)
+
     def in_ranks(value):
         return lax.all_to_all(value, "tm", 0, 0, tiled=True, axis_index_groups=ranks)
 
     def neighbour(tm_step, row_step):
-        pairs = [
+        moves = [
             (((t + tm_step) % tms) * rows + (r + row_step) % rows, t * rows + r)
             for t in range(tms)
             for r in range(rows)
         ]
-        return lax.ppermute(ups, ("tm", "rows"), pairs)
+        return lax.ppermute(ups, ("tm", "rows"), moves)
 
     halos = [neighbour(a, b) for a, b in EDGES]
 
@@ -379,9 +421,18 @@
     )(feats, ups)
     load = in_teams(load.reshape(size, length, wide)).reshape(TEAM, rows, length, wide)
 
-    halo = lax.ppermute(
-        load[0, :, positions : positions + cols], "tm", [((i + TEAM) % tms, i) for i in range(tms)]
-    )
+    other = lax.ppermute(load[:, :, cols : 3 * cols], "tm", [(t, t ^ 1) for t in range(tms)])
+    opens = lax.shift_right_logical(lax.axis_index("tm"), 2) & 3 == 0
+    runs = [load[2 * x, :, 2 * cols : 3 * cols] for x in range(2)]
+    halo = []
+    for x in range(2):
+        moves = []
+        for o in places:
+            goal = (o[0], o[1] + 1) if o[1] < 3 else ((o[0] + x) % (groups // 4), 0)
+            moves += [(place(goal, i, 0), place(o, i, 0)) for i in chips]
+        halo.append(lax.ppermute(jnp.where(opens, runs[1 - x], runs[x]), "tm", moves))
+    for x in range(2):
+        halo.append(lax.ppermute(halo[x], "tm", [(t, t + 1) for t in range(0, tms, 2)]))
 
     def whole(shape):
         return pl.BlockSpec(shape, lambda *s: (0,) * len(shape))
@@ -405,38 +456,38 @@
         functools.partial(combine_kernel, float(positions * (chans // GROUPS))),
         in_specs=[vmem],
         out_specs=vmem,
-        out_shape=jax.ShapeDtypeStruct((groups, 8, 128), F32),
+        out_shape=jax.ShapeDtypeStruct((2 * groups, 8, 128), F32),
         compiler_params=params(16),
         name="combine",
     )(load)
-    stats = in_ranks(stats)
+    stats = in_stars(stats)
 
     act, sums, norm = pl.pallas_call(
         functools.partial(act_kernel, positions * size),
         in_specs=[pl.BlockSpec(), pl.BlockSpec(), pl.BlockSpec(), vmem, pl.BlockSpec()],
         out_shape=(
             jax.ShapeDtypeStruct((positions, chans), F32),
-            jax.ShapeDtypeStruct((size, 8, 128), F32),
+            jax.ShapeDtypeStruct((2 * size, 8, 128), F32),
             jax.ShapeDtypeStruct((16, chans), F32),
         ),
         compiler_params=params(62),
         name="act",
     )(feats, gain, bias, stats, dense)
-    sums = in_teams(sums)
+    sums = in_pairs(sums)
 
     weight_call = pl.pallas_call(
         functools.partial(weight_kernel, tms),
-        in_specs=[vmem] + [pl.BlockSpec()] * 4,
+        in_specs=[vmem] + [pl.BlockSpec()] * 8,
         out_specs=vmem,
         out_shape=jax.ShapeDtypeStruct((groups, 14 * step + 8, 128), F32),
         scratch_shapes=[
-            pltpu.VMEM((2 * TEAM + 2, rows + 2, cols, wide), BF16),
-            pltpu.VMEM((3 * 64, 9 * wide), F32),
+            pltpu.VMEM((2, 6, rows + 2, cols, 128), BF16),
+            pltpu.VMEM((384, 768), F32),
         ],
         compiler_params=params(61),
         name="wgrad",
     )
-    part = weight_call(load, halo, norm, gain, bias)
+    part = weight_call(load, other, *halo, norm, gain, bias)
     part = pl.pallas_call(
         append_kernel,
         in_specs=[vmem, vmem],

time: 117 us -> 127 us (1.085)
  the two profiles are of different devices: /device:TPU:32 before, /device:TPU:34 now
where the time goes in v5:
time: 127 us; the launch traced here: 126 us
  blocking collectives  53.8 us (42%)
  starting transfers between devices  39.7 us (31%)
  Pallas kernels  27 us (21%)
  local copies, waits for them, and re-layouts  3.35 us (3%)
    all_to_all x1, blocking collectives, in_teams(): lax.all_to_all(value, ('tm', 'rows'), 0, 0, tiled=True, axis_index_groups...  32.2 us
    all_to_all x1, blocking collectives, in_ranks(): lax.all_to_all(value, 'tm', 0, 0, tiled=True, axis_index_groups=ranks)  21.6 us
    ppermute x2, starting transfers between devices, on_device(): lax.ppermute(jnp.where(opens, runs[1 - x], runs[x]), 'tm', moves)  12.3 us
    pallas_call x1, Pallas kernels, on_device(): dense = dense_call(ups, *halos, weight)  9.84 us
    all_to_all x1, starting transfers between devices, in_stars(): lax.all_to_all(value, 'tm', 0, 0, tiled=True, axis_index_groups=stars)  9.29 us
    pallas_call x1, Pallas kernels, on_device(): part = weight_call(load, other, *halo, norm, gain, bias)  8.94 us
    all_to_all x1, starting transfers between devices, in_pairs(): lax.all_to_all(value, ('tm', 'rows'), 0, 0, tiled=True, axis_index_groups...  7.4 us
    ppermute x5, starting transfers between devices, neighbour(): return lax.ppermute(ups, ('tm', 'rows'), moves)  7.11 us
  transfers between devices with their start and end apart: 12, of which 1 were waited for; matrix products, arithmetic and copies ran while one was open for 1% of the time, Pallas kernels for 18%

profile of v5, /device:TPU:34, one launch (start us, length us, event | category | flops | bytes accessed | tf_op | source)
XLA Modules:
  0.0 126.2 jit_solution(17764591199434235864)
XLA Ops:
  0.6 3.2 %pack.1 = bf16[4,4,496,128]{3,2,1,0:T(8,128)(2,1)} custom-call(bf16[320,512]{1,0:T(8,128)(2,1)} %bitcast.20, bf16[2,160,256]{2,1,0:T(8,128)(2,1)} %bitcast.27), custom_call_target="tpu_custom_call" | custom-call | tf_op jit(solution)/shard_map/pack/pallas_call | solution.py:416
  3.8 32.2 %all_to_all.20 = bf16[16,496,128]{2,1,0:T(8,128)(2,1)S(1)} all-to-all(bf16[16,496,128]{2,1,0:T(8,128)(2,1)} %bitcast.26), channel_id=1, replica_groups={{0,1,2,3,8,9,10,11,64,65,66,67,72,73,74,75},{4,5,6,7,12,13,14,15,68,69,..., dimensions={0} | all-to-all | bytes 4063232 | tf_op jit(solution)/shard_map/all_to_all | solution.py:395
  36.0 1.2 slice.12
  37.2 0.6 collective-permute-start.5
  37.8 2.7 %collective-permute-start.6 = (bf16[2,160,256]{2,1,0:T(8,128)(2,1)S(1)}, bf16[2,160,256]{2,1,0:T(8,128)(2,1)}, u32[]{:S(2)}, u32[]{:S(2)}) collective-permute-start(bf16[2,160,256]{2,1,0:T(8,128)(2,1)S(1)} %bitcast.30), channel_id=1, source_target_pairs={{1,0},{2,1},{3,2},{0,3},{5,4},{6,5},{7,6},{4,7},{9,8},{10,9},{11,1... | collective-permute-start | bytes 491528 | tf_op jit(solution)/shard_map/ppermute | solution.py:412
  40.5 1.0 collective-permute-start.7
  41.5 0.7 combine.1
  42.2 9.3 %all-to-all-start.1 = ((f32[16,8,128]{2,1,0:T(8,128)}), f32[16,8,128]{2,1,0:T(8,128)}, u32[]{:S(2)}, u32[]{:S(2)}) async-start(f32[16,8,128]{2,1,0:T(8,128)} %combine.1), calls=%async_computation.1 | async-start | bytes 131072 | tf_op jit(solution)/shard_map/all_to_all | solution.py:401
  51.5 2.9 %collective-permute-start.9 = (bf16[2,160,256]{2,1,0:T(8,128)(2,1)S(1)}, bf16[2,160,256]{2,1,0:T(8,128)(2,1)}, u32[]{:S(2)}, u32[]{:S(2)}) collective-permute-start(bf16[2,160,256]{2,1,0:T(8,128)(2,1)S(1)} %bitcast.33), channel_id=1, source_target_pairs={{5,0},{6,1},{7,2},{4,3},{9,4},{10,5},{11,6},{8,7},{13,8},{14,9},{1... | collective-permute-start | bytes 491528 | tf_op jit(solution)/shard_map/ppermute | solution.py:412
  54.4 0.7 select_bitcast_fusion
  55.1 5.6 %collective-permute-start.1 = (bf16[4,160,128]{2,1,0:T(8,128)(2,1)}, bf16[4,160,128]{2,1,0:T(8,128)(2,1)S(1)}, u32[]{:S(2)}, u32[]{:S(2)}) collective-permute-start(bf16[4,160,128]{2,1,0:T(8,128)(2,1)} %get-tuple-element.23), channel_id=1, source_target_pairs={{16,0},{24,8},{80,64},{88,72},{32,16},{40,24},{96,80},{104,88},{48... | collective-permute-start | bytes 491528 | tf_op jit(solution)/shard_map/ppermute | solution.py:433
  60.8 6.7 %collective-permute-start.2 = (bf16[4,160,128]{2,1,0:T(8,128)(2,1)}, bf16[4,160,128]{2,1,0:T(8,128)(2,1)S(1)}, u32[]{:S(2)}, u32[]{:S(2)}) collective-permute-start(bf16[4,160,128]{2,1,0:T(8,128)(2,1)} %get-tuple-element.22), channel_id=1, source_target_pairs={{16,0},{24,8},{80,64},{88,72},{32,16},{40,24},{96,80},{104,88},{48... | collective-permute-start | bytes 491528 | tf_op jit(solution)/shard_map/ppermute | solution.py:433
  67.5 9.8 %dense.1.dense_ref = f32[320,512]{1,0:T(8,128)} custom-call(bf16[2,160,256]{2,1,0:T(8,128)(2,1)} %bitcast.28, bf16[2,160,256]{2,1,0:T(8,128)(2,1)} %collective-permute-done.5.above_ref, bf16[2,160,256]{2,1,0:T(8,128)(2,1)} %collective-permute-done.6.below_ref, bf16[2,160,256]{2,1,0:T(8,128)(2,1)} %collective-permute-done.7.later_ref, ...), custom_call_target="tpu_custom_call" | custom-call | tf_op jit(solution)/shard_map/dense/pallas_call | solution.py:453
  77.3 2.9 %act.1 = (f32[320,512]{1,0:T(8,128)}, f32[32,8,128]{2,1,0:T(8,128)}, f32[16,512]{1,0:T(8,128)}) custom-call(bf16[320,512]{1,0:T(8,128)(2,1)} %bitcast.21, f32[1,512]{1,0:T(1,128)} %bitcast.23, f32[1,512]{1,0:T(1,128)} %bitcast.34, f32[16,8,128]{2,1,0:T(8,128)} %all-to-all-done.1.stats_ref, f32[320,512]{1,0:T(8,128)} %dense.1.dense_ref), custom_call_target="tpu_custom_call" | custom-call | tf_op jit(solution)/shard_map/act/pallas_call | solution.py:465
  80.2 7.4 %all-to-all-start.2 = ((f32[32,8,128]{2,1,0:T(8,128)}), f32[32,8,128]{2,1,0:T(8,128)S(1)}, u32[]{:S(2)}, u32[]{:S(2)}) async-start(f32[32,8,128]{2,1,0:T(8,128)} %get-tuple-element.12), calls=%async_computation.2 | async-start | bytes 262144 | tf_op jit(solution)/shard_map/all_to_all | solution.py:398
  87.7 2.1 %collective-permute-start.3 = (bf16[4,160,128]{2,1,0:T(8,128)(2,1)S(1)}, bf16[4,160,128]{2,1,0:T(8,128)(2,1)S(1)}, u32[]{:S(2)}, u32[]{:S(2)}) collective-permute-start(bf16[4,160,128]{2,1,0:T(8,128)(2,1)S(1)} %collective-permute-done.1.halo0_ref), channel_id=1, source_target_pairs={{0,4},{8,12},{16,20},{24,28},{32,36},{40,44},{48,52},{56,60},{64,6... | collective-permute-start | bytes 491528 | tf_op jit(solution)/shard_map/ppermute | solution.py:435
  89.8 1.5 %collective-permute-start.4 = (bf16[4,160,128]{2,1,0:T(8,128)(2,1)S(1)}, bf16[4,160,128]{2,1,0:T(8,128)(2,1)S(1)}, u32[]{:S(2)}, u32[]{:S(2)}) collective-permute-start(bf16[4,160,128]{2,1,0:T(8,128)(2,1)S(1)} %collective-permute-done.2.halo1_ref), channel_id=1, source_target_pairs={{0,4},{8,12},{16,20},{24,28},{32,36},{40,44},{48,52},{56,60},{64,6... | collective-permute-start | bytes 491528 | tf_op jit(solution)/shard_map/ppermute | solution.py:435
  91.3 0.8 collective-permute-done.4.moved1_ref
  92.1 0.6 copy-done.11
  92.7 0.5 copy-done.6
  93.2 8.9 %wgrad.1.part_ref = f32[8,120,128]{2,1,0:T(8,128)} custom-call(bf16[4,4,496,128]{3,2,1,0:T(8,128)(2,1)} %bitcast.19, bf16[4,4,320,128]{3,2,1,0:T(8,128)(2,1)} %copy-done.6, bf16[4,160,128]{2,1,0:T(8,128)(2,1)} %copy-done.8, bf16[4,160,128]{2,1,0:T(8,128)(2,1)} %copy-done.9, bf16[4,160,128]{2,1,0:T(8,128)(2,1)} %copy-done.10, ...), custom_call_target="tpu_custom_call" | custom-call | tf_op jit(solution)/shard_map/wgrad/pallas_call | solution.py:490
  102.1 1.0 copy-done.1
  103.2 21.6 %all_to_all.21.load_ref = f32[8,120,128]{2,1,0:T(8,128)S(1)} all-to-all(f32[8,120,128]{2,1,0:T(8,128)S(1)} %append.1), channel_id=1, replica_groups={{0,16,32,48,128,144,160,176},{4,20,36,52,132,148,164,180},{8,24,40,56,1..., dimensions={0} | all-to-all | bytes 983040 | tf_op jit(solution)/shard_map/all_to_all | solution.py:404
  124.8 1.4 %final.1 = (bf16[320,512]{1,0:T(8,128)(2,1)}, f32[9,3,8,64]{3,2,1,0:T(8,128)}, f32[1,512]{1,0:T(1,128)}, f32[1,512]{1,0:T(1,128)}) custom-call(f32[8,120,128]{2,1,0:T(8,128)S(1)} %all_to_all.21.load_ref, f32[320,512]{1,0:T(8,128)S(1)} %copy-done.3, bf16[320,512]{1,0:T(8,128)(2,1)S(1)} %bitcast.22, f32[16,512]{1,0:T(8,128)S(1)} %copy-done.4, ...), custom_call_target="tpu_custom_call" | custom-call | tf_op jit(solution)/shard_map/final/pallas_call | solution.py:502
  (35 shorter events, 0.1 us)
Async XLA Ops:
  36.0 18.4 %copy-start = (bf16[16,496,128]{2,1,0:T(8,128)(2,1)}, bf16[16,496,128]{2,1,0:T(8,128)(2,1)S(1)}, u32[]{:S(2)}) copy-start(bf16[16,496,128]{2,1,0:T(8,128)(2,1)S(1)} %all_to_all.20) | copy-start | bytes 6094852
  36.0 1.2 copy-start.7
  37.2 54.8 %collective-permute-start = (bf16[4,4,320,128]{3,2,1,0:T(8,128)(2,1)}, bf16[4,4,320,128]{3,2,1,0:T(8,128)(2,1)S(1)}, u32[]{:S(2)}, u32[]{:S(2)}) collective-permute-start(bf16[4,4,320,128]{3,2,1,0:T(8,128)(2,1)} %slice.12), channel_id=1, source_target_pairs={{0,4},{4,0},{8,12},{12,8},{16,20},{20,16},{24,28},{28,24},{32,36},... | collective-permute-start | bytes 3932168 | tf_op jit(solution)/shard_map/ppermute | solution.py:424
  37.2 14.3 %collective-permute-start.5 = (bf16[2,160,256]{2,1,0:T(8,128)(2,1)S(1)}, bf16[2,160,256]{2,1,0:T(8,128)(2,1)}, u32[]{:S(2)}, u32[]{:S(2)}) collective-permute-start(bf16[2,160,256]{2,1,0:T(8,128)(2,1)S(1)} %bitcast.29), channel_id=1, source_target_pairs={{3,0},{0,1},{1,2},{2,3},{7,4},{4,5},{5,6},{6,7},{11,8},{8,9},{9,10... | collective-permute-start | bytes 491528 | tf_op jit(solution)/shard_map/ppermute | solution.py:412
  37.8 17.3 %collective-permute-start.6 = (bf16[2,160,256]{2,1,0:T(8,128)(2,1)S(1)}, bf16[2,160,256]{2,1,0:T(8,128)(2,1)}, u32[]{:S(2)}, u32[]{:S(2)}) collective-permute-start(bf16[2,160,256]{2,1,0:T(8,128)(2,1)S(1)} %bitcast.30), channel_id=1, source_target_pairs={{1,0},{2,1},{3,2},{0,3},{5,4},{6,5},{7,6},{4,7},{9,8},{10,9},{11,1... | collective-permute-start | bytes 491528 | tf_op jit(solution)/shard_map/ppermute | solution.py:412
  40.5 20.3 %collective-permute-start.7 = (bf16[2,160,256]{2,1,0:T(8,128)(2,1)S(1)}, bf16[2,160,256]{2,1,0:T(8,128)(2,1)}, u32[]{:S(2)}, u32[]{:S(2)}) collective-permute-start(bf16[2,160,256]{2,1,0:T(8,128)(2,1)S(1)} %bitcast.31), channel_id=1, source_target_pairs={{4,0},{5,1},{6,2},{7,3},{8,4},{9,5},{10,6},{11,7},{12,8},{13,9},{1... | collective-permute-start | bytes 491528 | tf_op jit(solution)/shard_map/ppermute | solution.py:412
  41.5 26.0 %collective-permute-start.8 = (bf16[2,160,256]{2,1,0:T(8,128)(2,1)S(1)}, bf16[2,160,256]{2,1,0:T(8,128)(2,1)}, u32[]{:S(2)}, u32[]{:S(2)}) collective-permute-start(bf16[2,160,256]{2,1,0:T(8,128)(2,1)S(1)} %bitcast.32), channel_id=1, source_target_pairs={{7,0},{4,1},{5,2},{6,3},{11,4},{8,5},{9,6},{10,7},{15,8},{12,9},{1... | collective-permute-start | bytes 491528 | tf_op jit(solution)/shard_map/ppermute | solution.py:412
  42.2 35.1 %all-to-all-start.1 = ((f32[16,8,128]{2,1,0:T(8,128)}), f32[16,8,128]{2,1,0:T(8,128)}, u32[]{:S(2)}, u32[]{:S(2)}) async-start(f32[16,8,128]{2,1,0:T(8,128)} %combine.1), calls=%async_computation.1 | async-start | bytes 131072 | tf_op jit(solution)/shard_map/all_to_all | solution.py:401
  51.5 16.0 %collective-permute-start.9 = (bf16[2,160,256]{2,1,0:T(8,128)(2,1)S(1)}, bf16[2,160,256]{2,1,0:T(8,128)(2,1)}, u32[]{:S(2)}, u32[]{:S(2)}) collective-permute-start(bf16[2,160,256]{2,1,0:T(8,128)(2,1)S(1)} %bitcast.33), channel_id=1, source_target_pairs={{5,0},{6,1},{7,2},{4,3},{9,4},{10,5},{11,6},{8,7},{13,8},{14,9},{1... | collective-permute-start | bytes 491528 | tf_op jit(solution)/shard_map/ppermute | solution.py:412
  55.1 32.5 %collective-permute-start.1 = (bf16[4,160,128]{2,1,0:T(8,128)(2,1)}, bf16[4,160,128]{2,1,0:T(8,128)(2,1)S(1)}, u32[]{:S(2)}, u32[]{:S(2)}) collective-permute-start(bf16[4,160,128]{2,1,0:T(8,128)(2,1)} %get-tuple-element.23), channel_id=1, source_target_pairs={{16,0},{24,8},{80,64},{88,72},{32,16},{40,24},{96,80},{104,88},{48... | collective-permute-start | bytes 491528 | tf_op jit(solution)/shard_map/ppermute | solution.py:433
  60.8 28.9 %collective-permute-start.2 = (bf16[4,160,128]{2,1,0:T(8,128)(2,1)}, bf16[4,160,128]{2,1,0:T(8,128)(2,1)S(1)}, u32[]{:S(2)}, u32[]{:S(2)}) collective-permute-start(bf16[4,160,128]{2,1,0:T(8,128)(2,1)} %get-tuple-element.22), channel_id=1, source_target_pairs={{16,0},{24,8},{80,64},{88,72},{32,16},{40,24},{96,80},{104,88},{48... | collective-permute-start | bytes 491528 | tf_op jit(solution)/shard_map/ppermute | solution.py:433
  80.2 21.9 %all-to-all-start.2 = ((f32[32,8,128]{2,1,0:T(8,128)}), f32[32,8,128]{2,1,0:T(8,128)S(1)}, u32[]{:S(2)}, u32[]{:S(2)}) async-start(f32[32,8,128]{2,1,0:T(8,128)} %get-tuple-element.12), calls=%async_computation.2 | async-start | bytes 262144 | tf_op jit(solution)/shard_map/all_to_all | solution.py:398
  87.7 4.4 %copy-start.8 = (bf16[4,160,128]{2,1,0:T(8,128)(2,1)}, bf16[4,160,128]{2,1,0:T(8,128)(2,1)S(1)}, u32[]{:S(2)}) copy-start(bf16[4,160,128]{2,1,0:T(8,128)(2,1)S(1)} %collective-permute-done.1.halo0_ref) | copy-start | bytes 491524
  87.7 3.6 %collective-permute-start.3 = (bf16[4,160,128]{2,1,0:T(8,128)(2,1)S(1)}, bf16[4,160,128]{2,1,0:T(8,128)(2,1)S(1)}, u32[]{:S(2)}, u32[]{:S(2)}) collective-permute-start(bf16[4,160,128]{2,1,0:T(8,128)(2,1)S(1)} %collective-permute-done.1.halo0_ref), channel_id=1, source_target_pairs={{0,4},{8,12},{16,20},{24,28},{32,36},{40,44},{48,52},{56,60},{64,6... | collective-permute-start | bytes 491528 | tf_op jit(solution)/shard_map/ppermute | solution.py:435
  89.7 2.3 %copy-start.9 = (bf16[4,160,128]{2,1,0:T(8,128)(2,1)}, bf16[4,160,128]{2,1,0:T(8,128)(2,1)S(1)}, u32[]{:S(2)}) copy-start(bf16[4,160,128]{2,1,0:T(8,128)(2,1)S(1)} %collective-permute-done.2.halo1_ref) | copy-start | bytes 491524
  89.8 2.3 %collective-permute-start.4 = (bf16[4,160,128]{2,1,0:T(8,128)(2,1)S(1)}, bf16[4,160,128]{2,1,0:T(8,128)(2,1)S(1)}, u32[]{:S(2)}, u32[]{:S(2)}) collective-permute-start(bf16[4,160,128]{2,1,0:T(8,128)(2,1)S(1)} %collective-permute-done.2.halo1_ref), channel_id=1, source_target_pairs={{0,4},{8,12},{16,20},{24,28},{32,36},{40,44},{48,52},{56,60},{64,6... | collective-permute-start | bytes 491528 | tf_op jit(solution)/shard_map/ppermute | solution.py:435
  91.2 0.8 copy-start.10
  92.1 0.7 copy-start.11
  92.1 1.1 copy-start.6
  102.1 1.0 copy-start.1
  103.1 21.6 %copy-start.2 = (bf16[2,1,160,512]{3,2,1,0:T(8,128)(2,1)S(1)}, bf16[2,1,160,512]{3,2,1,0:T(8,128)(2,1)}, u32[]{:S(2)}) copy-start(bf16[2,1,160,512]{3,2,1,0:T(8,128)(2,1)} %param.5) | copy-start | bytes 983044
  103.1 21.6 %copy-start.3 = (f32[320,512]{1,0:T(8,128)S(1)}, f32[320,512]{1,0:T(8,128)}, u32[]{:S(2)}) copy-start(f32[320,512]{1,0:T(8,128)} %get-tuple-element.13.act_ref) | copy-start | bytes 1966084
  103.1 21.6 %copy-start.4 = (f32[16,512]{1,0:T(8,128)S(1)}, f32[16,512]{1,0:T(8,128)}, u32[]{:S(2)}) copy-start(f32[16,512]{1,0:T(8,128)} %get-tuple-element.11.norm_ref) | copy-start | bytes 98308
  103.2 21.6 %copy-start.5 = (f32[512]{0:T(512)S(1)}, f32[512]{0:T(512)}, u32[]{:S(2)}) copy-start(f32[512]{0:T(512)} %param.6) | copy-start | bytes 6148

commit v6 on v5

--- a/solution.py
+++ b/solution.py
@@ -197,8 +197,21 @@
     return centre, inverse
 
 
-def act_kernel(positions, feats_ref, gain_ref, bias_ref, stats_ref, dense_ref, act_ref, sums_ref, norm_ref):
+def act_kernel(
+    positions, feats_ref, gain_ref, bias_ref, stats_ref, dense_ref, load_ref, halo0_ref, halo1_ref,
+    act_ref, sums_ref, norm_ref, swap_ref, sems,
+):
     chans = gain_ref.shape[1]
+    cols = halo0_ref.shape[1]
+    slots = load_ref.shape[0]
+    tail = pl.ds(slots, halo0_ref.shape[0])
+    copies = [
+        pltpu.make_async_copy(load_ref.at[:, pl.ds(cols, 2 * cols)], swap_ref.at[pl.ds(0, slots)], sems.at[0]),
+        pltpu.make_async_copy(halo0_ref, swap_ref.at[tail, pl.ds(0, cols)], sems.at[1]),
+        pltpu.make_async_copy(halo1_ref, swap_ref.at[tail, pl.ds(cols, cols)], sems.at[2]),
+    ]
+    for copy in copies:
+        copy.start()
     centre, inverse = norm_rows(stats_ref, chans, positions)
     norm_ref[0:8] = centre
     norm_ref[8:16] = inverse
@@ -215,19 +228,23 @@
     rows = [gains[:, p * 128 : (p + 1) * 128] for p in range(pieces)]
     rows = rows + [biases[:, p * 128 : (p + 1) * 128] for p in range(pieces)]
     sums_ref[...] = jnp.broadcast_to(jnp.concatenate(rows, axis=0)[None], sums_ref.shape)
-
-
-def append_kernel(part_ref, load_ref, out_ref):
+    for copy in copies:
+        copy.wait()
+
+
+def append_kernel(part_ref, load_ref, out_ref, sums, sem):
     total = load_ref[0]
     for g in range(1, load_ref.shape[0]):
         total = total + load_ref[g]
-    place = (out_ref.shape[0],) + total.shape
-    out_ref[:, out_ref.shape[1] - total.shape[0] :, :] = jnp.broadcast_to(total[None], place)
+    sums[...] = jnp.broadcast_to(total[None], sums.shape)
+    size = sums.shape[1]
+    copy = pltpu.make_async_copy(sums, out_ref.at[:, pl.ds(out_ref.shape[1] - size, size)], sem)
+    copy.start()
+    copy.wait()
 
 
 def weight_kernel(
-    teams, load_ref, other_ref, halo0_ref, halo1_ref, moved0_ref, moved1_ref, norm_ref, gain_ref, bias_ref,
-    out_ref, hidden, acc,
+    teams, load_ref, other_ref, halo0_ref, halo1_ref, norm_ref, gain_ref, bias_ref, out_ref, hidden, acc
 ):
     time_index = lax.axis_index("tm")
     core = time_index & 1
@@ -256,7 +273,7 @@
         for q in range(4):
             for r in range(rows):
                 j = 2 * x + q // 2
-                pair = jnp.where(core == q % 2, load_ref[j, r, 0:cols, :], other_ref[j, r, 0:cols, :])
+                pair = jnp.where(core == q % 2, load_ref[j, r, 0:cols, :], other_ref[j * rows + r, 0:cols, :])
                 preact = (pair.astype(F32) - centre) * inverse * gain + bias
                 value = preact * sigmoid(preact)
                 hidden[x, q + 1, r + 1] = value.astype(BF16)
@@ -267,36 +284,46 @@
                     hidden[x, 0, r + 1] = before.astype(BF16)
                     hidden[x, 5, r + 1] = jnp.zeros(hidden.shape[3:], BF16)
 
-    for x in range(2):
-        for q in range(5):
-            sides = [[], [], []]
-            for r in range(rows):
-                j = 2 * x + q // 2
-                if q < 4:
-                    pair = jnp.where(
-                        core == q % 2, load_ref[j, r, 2 * cols : 3 * cols, :], other_ref[j, r, cols : 2 * cols, :]
-                    )
-                else:
-                    near, far = ((halo0_ref, moved0_ref), (halo1_ref, moved1_ref))[x]
-                    pair = jnp.where(core == 0, near[r], far[r])
-                wide = pair.astype(F32)
-                if q == 4 and x == 1:
-                    wide = jnp.where(end, 0.0, wide)
-                row = iota(wide.shape, 0)
-                sides[0].append(jnp.where(row < cols - 1, pltpu.roll(wide, cols - 1, 0), 0.0).astype(BF16))
-                sides[1].append(wide.astype(BF16))
-                sides[2].append(jnp.where(row > 0, pltpu.roll(wide, 1, 0), 0.0).astype(BF16))
-            ups = jnp.concatenate([jnp.concatenate(side, axis=0) for side in sides], axis=1)
-            taps = [
-                hidden[x, q + n, b : b + rows].reshape(rows * cols, 128) for b in range(3) for n in range(2)
-            ]
-            term = lax.dot_general(
-                ups, jnp.concatenate(taps, axis=1), (((0,), (0,)), ((), ())), preferred_element_type=F32
-            )
-            if x == 0 and q == 0:
-                acc[...] = term
+    def ups_of(x, q):
+        sides = [[], [], []]
+        for r in range(rows):
+            j = 2 * x + q // 2
+            if q < 4:
+                pair = jnp.where(
+                    core == q % 2,
+                    load_ref[j, r, 2 * cols : 3 * cols, :],
+                    other_ref[j * rows + r, cols : 2 * cols, :],
+                )
             else:
-                acc[...] += term
+                near = (halo0_ref, halo1_ref)[x]
+                pair = jnp.where(
+                    core == 0, near[r], other_ref[TEAM * rows + r, x * cols : (x + 1) * cols, :]
+                )
+            wide = pair.astype(F32)
+            if q == 4 and x == 1:
+                wide = jnp.where(end, 0.0, wide)
+            row = iota(wide.shape, 0)
+            sides[0].append(jnp.where(row < cols - 1, pltpu.roll(wide, cols - 1, 0), 0.0).astype(BF16))
+            sides[1].append(wide.astype(BF16))
+            sides[2].append(jnp.where(row > 0, pltpu.roll(wide, 1, 0), 0.0).astype(BF16))
+        return jnp.concatenate([jnp.concatenate(side, axis=0) for side in sides], axis=1)
+
+    def taps_of(x, q, width):
+        taps = [hidden[x, q + n, b : b + rows].reshape(rows * cols, 128) for n in range(width) for b in range(3)]
+        return jnp.concatenate(taps, axis=1)
+
+    plans = [([(x, q), (x, q + 1)], 2) for x in range(2) for q in (0, 2)] + [([(0, 4), (1, 4)], 1)]
+    for index, (units, width) in enumerate(plans):
+        term = lax.dot_general(
+            jnp.concatenate([ups_of(x, q) for x, q in units], axis=0),
+            jnp.concatenate([taps_of(x, q, width) for x, q in units], axis=0),
+            (((0,), (0,)), ((), ())),
+            preferred_element_type=F32,
+        )
+        if index == 0:
+            acc[...] = term
+        else:
+            acc[:, 0 : 384 * width] += term
 
     groups = out_ref.shape[0]
     low = iota((192, 128), 1) < 64
@@ -306,7 +333,12 @@
 
     thirds = []
     for b in range(3):
-        blocks = [acc[c * 128 : (c + 1) * 128, b * 256 : (b + 1) * 256].T for c in range(3)]
+        blocks = [
+            jnp.concatenate(
+                [acc[c * 128 : (c + 1) * 128, m + b * 128 : m + (b + 1) * 128].T for m in (0, 384)], axis=0
+            )
+            for c in range(3)
+        ]
         first = blocks[0][0:192] + pltpu.roll(blocks[0][64:256], 64, 1)
         second = pltpu.roll(blocks[1][0:192], 64, 1) + blocks[1][64:256]
         both = jnp.where(low, first, second)
@@ -369,6 +401,8 @@
     wide = chans // TEAM
     count = positions * devices * (chans // GROUPS)
     vmem = pl.BlockSpec(memory_space=pltpu.VMEM)
+    anywhere = pl.BlockSpec(memory_space=pl.ANY)
+    far = pl.BlockSpec(memory_space=pltpu.HBM)
 
     def params(mebibytes):
         return pltpu.CompilerParams(vmem_limit_bytes=mebibytes * 1024 * 1024)
@@ -421,7 +455,6 @@
     )(feats, ups)
     load = in_teams(load.reshape(size, length, wide)).reshape(TEAM, rows, length, wide)
 
-    other = lax.ppermute(load[:, :, cols : 3 * cols], "tm", [(t, t ^ 1) for t in range(tms)])
     opens = lax.shift_right_logical(lax.axis_index("tm"), 2) & 3 == 0
     runs = [load[2 * x, :, 2 * cols : 3 * cols] for x in range(2)]
     halo = []
@@ -431,8 +464,6 @@
             goal = (o[0], o[1] + 1) if o[1] < 3 else ((o[0] + x) % (groups // 4), 0)
             moves += [(place(goal, i, 0), place(o, i, 0)) for i in chips]
         halo.append(lax.ppermute(jnp.where(opens, runs[1 - x], runs[x]), "tm", moves))
-    for x in range(2):
-        halo.append(lax.ppermute(halo[x], "tm", [(t, t + 1) for t in range(0, tms, 2)]))
 
     def whole(shape):
         return pl.BlockSpec(shape, lambda *s: (0,) * len(shape))
@@ -462,39 +493,44 @@
     )(load)
     stats = in_stars(stats)
 
-    act, sums, norm = pl.pallas_call(
+    act, sums, norm, swap = pl.pallas_call(
         functools.partial(act_kernel, positions * size),
-        in_specs=[pl.BlockSpec(), pl.BlockSpec(), pl.BlockSpec(), vmem, pl.BlockSpec()],
+        in_specs=[pl.BlockSpec()] * 3 + [vmem, pl.BlockSpec()] + [anywhere] * 3,
+        out_specs=(pl.BlockSpec(), pl.BlockSpec(), pl.BlockSpec(), anywhere),
+        scratch_shapes=[pltpu.SemaphoreType.DMA((3,))],
         out_shape=(
             jax.ShapeDtypeStruct((positions, chans), F32),
             jax.ShapeDtypeStruct((2 * size, 8, 128), F32),
             jax.ShapeDtypeStruct((16, chans), F32),
+            jax.ShapeDtypeStruct((size + rows, 2 * cols, 128), BF16),
         ),
         compiler_params=params(62),
         name="act",
-    )(feats, gain, bias, stats, dense)
+    )(feats, gain, bias, stats, dense, load.reshape(size, length, wide), *halo)
+    other = lax.ppermute(swap, "tm", [(t, t ^ 1) for t in range(tms)])
     sums = in_pairs(sums)
 
     weight_call = pl.pallas_call(
         functools.partial(weight_kernel, tms),
-        in_specs=[vmem] + [pl.BlockSpec()] * 8,
+        in_specs=[vmem, vmem] + [pl.BlockSpec()] * 5,
         out_specs=vmem,
         out_shape=jax.ShapeDtypeStruct((groups, 14 * step + 8, 128), F32),
         scratch_shapes=[
             pltpu.VMEM((2, 6, rows + 2, cols, 128), BF16),
             pltpu.VMEM((384, 768), F32),
         ],
-        compiler_params=params(61),
+        compiler_params=params(62),
         name="wgrad",
     )
     part = weight_call(load, other, *halo, norm, gain, bias)
     part = pl.pallas_call(
         append_kernel,
-        in_specs=[vmem, vmem],
-        out_specs=vmem,
+        in_specs=[far, vmem],
+        out_specs=far,
+        scratch_shapes=[pltpu.VMEM((groups, 8, 128), F32), pltpu.SemaphoreType.DMA],
         out_shape=jax.ShapeDtypeStruct((groups, 14 * step + 8, 128), F32),
         input_output_aliases={0: 0},
-        compiler_params=params(16),
+        compiler_params=params(62),
         name="append",
     )(part, sums)
     part = in_ranks(part)

time: 127 us -> 170 us (1.34)
  the two profiles are of different devices: /device:TPU:34 before, /device:TPU:40 now
where the time goes in v6:
time: 170 us; the launch traced here: 169 us
  Pallas kernels  77.6 us (46%)
  starting transfers between devices  41.7 us (25%)
  blocking collectives  27.8 us (16%)
  waiting for transfers between devices  17.1 us (10%)
  local copies, waits for them, and re-layouts  3.13 us (2%)
    pallas_call x1, Pallas kernels, on_device(): pl.pallas_call(functools.partial(act_kernel, positions * size), in_specs=...  52.9 us
    all_to_all x1, blocking collectives, in_ranks(): lax.all_to_all(value, 'tm', 0, 0, tiled=True, axis_index_groups=ranks)  27.8 us
    all_to_all x1, waiting for transfers between devices, in_teams(): lax.all_to_all(value, ('tm', 'rows'), 0, 0, tiled=True, axis_index_groups...  16.2 us
    ppermute x2, starting transfers between devices, on_device(): lax.ppermute(jnp.where(opens, runs[1 - x], runs[x]), 'tm', moves)  12.5 us
    ppermute x5, starting transfers between devices, neighbour(): return lax.ppermute(ups, ('tm', 'rows'), moves)  10.3 us
    pallas_call x1, Pallas kernels, on_device(): dense = dense_call(ups, *halos, weight)  9.8 us
    pallas_call x1, Pallas kernels, on_device(): part = weight_call(load, other, *halo, norm, gain, bias)  8.01 us
    all_to_all x1, starting transfers between devices, in_pairs(): lax.all_to_all(value, ('tm', 'rows'), 0, 0, tiled=True, axis_index_groups...  6.98 us
  transfers between devices with their start and end apart: 11, of which 2 were waited for; matrix products, arithmetic and copies ran while one was open for 0% of the time, Pallas kernels for 11%

profile of v6, /device:TPU:40, one launch (start us, length us, event | category | flops | bytes accessed | tf_op | source)
XLA Modules:
  0.0 168.9 jit_solution(91350044964781201)
XLA Ops:
  0.6 3.2 %pack.1 = bf16[4,4,496,128]{3,2,1,0:T(8,128)(2,1)} custom-call(bf16[320,512]{1,0:T(8,128)(2,1)} %bitcast.19, bf16[2,160,256]{2,1,0:T(8,128)(2,1)} %bitcast.26), custom_call_target="tpu_custom_call" | custom-call | tf_op jit(solution)/shard_map/pack/pallas_call | solution.py:450
  3.8 6.9 %all-to-all-start = ((bf16[16,496,128]{2,1,0:T(8,128)(2,1)}), bf16[16,496,128]{2,1,0:T(8,128)(2,1)S(1)}, u32[]{:S(2)}, u32[]{:S(2)}) async-start(bf16[16,496,128]{2,1,0:T(8,128)(2,1)} %bitcast.25), calls=%async_computation | async-start | bytes 4063232 | tf_op jit(solution)/shard_map/all_to_all | solution.py:429
  10.8 1.7 %collective-permute-start.3 = (bf16[2,160,256]{2,1,0:T(8,128)(2,1)S(1)}, bf16[2,160,256]{2,1,0:T(8,128)(2,1)S(1)}, u32[]{:S(2)}, u32[]{:S(2)}) collective-permute-start(bf16[2,160,256]{2,1,0:T(8,128)(2,1)S(1)} %bitcast.29), channel_id=1, source_target_pairs={{7,0},{4,1},{5,2},{6,3},{11,4},{8,5},{9,6},{10,7},{15,8},{12,9},{1... | collective-permute-start | bytes 491528 | tf_op jit(solution)/shard_map/ppermute | solution.py:446
  12.5 6.5 %collective-permute-start.2 = (bf16[2,160,256]{2,1,0:T(8,128)(2,1)S(1)}, bf16[2,160,256]{2,1,0:T(8,128)(2,1)S(1)}, u32[]{:S(2)}, u32[]{:S(2)}) collective-permute-start(bf16[2,160,256]{2,1,0:T(8,128)(2,1)S(1)} %bitcast.30), channel_id=1, source_target_pairs={{4,0},{5,1},{6,2},{7,3},{8,4},{9,5},{10,6},{11,7},{12,8},{13,9},{1... | collective-permute-start | bytes 491528 | tf_op jit(solution)/shard_map/ppermute | solution.py:446
  19.0 0.6 collective-permute-start.1
  19.6 1.5 collective-permute-start
  21.0 16.2 %all-to-all-done.load_ref = bf16[16,496,128]{2,1,0:T(8,128)(2,1)S(1)} async-done(((bf16[16,496,128]{2,1,0:T(8,128)(2,1)}), bf16[16,496,128]{2,1,0:T(8,128)(2,1)S(1)}, u32[]{:S(2)}, u32[]{:S(2)}) %all-to-all-start) | async-done | bytes 2031648 | tf_op jit(solution)/shard_map/all_to_all | solution.py:429
  37.2 0.8 select_bitcast_fusion
  38.0 0.9 collective-permute-done.4.later_below_ref
  38.8 10.5 %collective-permute-start.6 = (bf16[4,160,128]{2,1,0:T(8,128)(2,1)}, bf16[4,160,128]{2,1,0:T(8,128)(2,1)}, u32[]{:S(2)}, u32[]{:S(2)}) collective-permute-start(bf16[4,160,128]{2,1,0:T(8,128)(2,1)} %get-tuple-element.24), channel_id=1, source_target_pairs={{16,0},{24,8},{80,64},{88,72},{32,16},{40,24},{96,80},{104,88},{48... | collective-permute-start | bytes 491528 | tf_op jit(solution)/shard_map/ppermute | solution.py:466
  49.4 1.9 %collective-permute-start.5 = (bf16[4,160,128]{2,1,0:T(8,128)(2,1)}, bf16[4,160,128]{2,1,0:T(8,128)(2,1)}, u32[]{:S(2)}, u32[]{:S(2)}) collective-permute-start(bf16[4,160,128]{2,1,0:T(8,128)(2,1)} %get-tuple-element.25), channel_id=1, source_target_pairs={{16,0},{24,8},{80,64},{88,72},{32,16},{40,24},{96,80},{104,88},{48... | collective-permute-start | bytes 491528 | tf_op jit(solution)/shard_map/ppermute | solution.py:466
  51.3 0.7 combine.1
  52.1 4.6 %all-to-all-start.1 = ((f32[16,8,128]{2,1,0:T(8,128)}), f32[16,8,128]{2,1,0:T(8,128)}, u32[]{:S(2)}, u32[]{:S(2)}) async-start(f32[16,8,128]{2,1,0:T(8,128)} %combine.1), calls=%async_computation.1 | async-start | bytes 131072 | tf_op jit(solution)/shard_map/all_to_all | solution.py:435
  56.7 0.6 copy-done.10
  57.4 0.7 copy-done.11
  58.0 9.8 %dense.1.dense_ref = f32[320,512]{1,0:T(8,128)} custom-call(bf16[2,160,256]{2,1,0:T(8,128)(2,1)} %bitcast.27, bf16[2,160,256]{2,1,0:T(8,128)(2,1)} %collective-permute-done.above_ref, bf16[2,160,256]{2,1,0:T(8,128)(2,1)} %copy-done.11, bf16[2,160,256]{2,1,0:T(8,128)(2,1)} %copy-done.10, bf16[2,160,256]{2,1,0:T(8,128)(2,1)} %copy-done.9, ...), custom_call_target="tpu_custom_call" | custom-call | tf_op jit(solution)/shard_map/dense/pallas_call | solution.py:484
  67.9 52.9 %act.1 = (f32[320,512]{1,0:T(8,128)}, f32[32,8,128]{2,1,0:T(8,128)}, f32[16,512]{1,0:T(8,128)}, bf16[20,320,128]{2,1,0:T(8,128)(2,1)}) custom-call(bf16[320,512]{1,0:T(8,128)(2,1)} %bitcast.20, f32[1,512]{1,0:T(1,128)} %bitcast.22, f32[1,512]{1,0:T(1,128)} %bitcast.33, f32[16,8,128]{2,1,0:T(8,128)} %all-to-all-done.1.stats_ref, f32[320,512]{1,0:T(8,128)} %dense.1.dense_ref, ...), custom_call_target="tpu_custom_call" | custom-call | tf_op jit(solution)/shard_map/act/pallas_call | solution.py:496
  121.2 7.0 %all-to-all-start.2 = ((f32[32,8,128]{2,1,0:T(8,128)}), f32[32,8,128]{2,1,0:T(8,128)S(1)}, u32[]{:S(2)}, u32[]{:S(2)}) async-start(f32[32,8,128]{2,1,0:T(8,128)} %get-tuple-element.14), calls=%async_computation.2 | async-start | bytes 262144 | tf_op jit(solution)/shard_map/all_to_all | solution.py:432
  128.2 1.1 copy-done.5
  129.4 8.0 %wgrad.1.part_ref = f32[8,120,128]{2,1,0:T(8,128)} custom-call(bf16[4,4,496,128]{3,2,1,0:T(8,128)(2,1)} %bitcast.18, bf16[20,320,128]{2,1,0:T(8,128)(2,1)} %copy-done.5, bf16[4,160,128]{2,1,0:T(8,128)(2,1)} %collective-permute-done.5.halo0_ref, bf16[4,160,128]{2,1,0:T(8,128)(2,1)} %collective-permute-done.6.halo1_ref, f32[16,512]{1,0:T(8,128)} %get-tuple-element.13.norm_ref, ...), custom_call_target="tpu_custom_call" | custom-call | tf_op jit(solution)/shard_map/wgrad/pallas_call | solution.py:525
  137.4 0.6 copy-done.7
  138.1 1.6 append.1
  139.7 27.8 %all_to_all.20.load_ref = f32[8,120,128]{2,1,0:T(8,128)S(1)} all-to-all(f32[8,120,128]{2,1,0:T(8,128)} %append.1), channel_id=1, replica_groups={{0,16,32,48,128,144,160,176},{4,20,36,52,132,148,164,180},{8,24,40,56,1..., dimensions={0} | all-to-all | bytes 983040 | tf_op jit(solution)/shard_map/all_to_all | solution.py:438
  167.5 1.4 final.1
  (31 shorter events, 0.6 us)
Async XLA Ops:
  3.8 6.9 %copy-start.6 = (bf16[2,1,160,256]{3,2,1,0:T(8,128)(2,1)S(1)}, bf16[2,1,160,256]{3,2,1,0:T(8,128)(2,1)}, u32[]{:S(2)}) copy-start(bf16[2,1,160,256]{3,2,1,0:T(8,128)(2,1)} %param.9) | copy-start | bytes 491524
  3.8 33.4 %all-to-all-start = ((bf16[16,496,128]{2,1,0:T(8,128)(2,1)}), bf16[16,496,128]{2,1,0:T(8,128)(2,1)S(1)}, u32[]{:S(2)}, u32[]{:S(2)}) async-start(bf16[16,496,128]{2,1,0:T(8,128)(2,1)} %bitcast.25), calls=%async_computation | async-start | bytes 4063232 | tf_op jit(solution)/shard_map/all_to_all | solution.py:429
  10.7 28.1 %collective-permute-start.4 = (bf16[2,160,256]{2,1,0:T(8,128)(2,1)S(1)}, bf16[2,160,256]{2,1,0:T(8,128)(2,1)S(1)}, u32[]{:S(2)}, u32[]{:S(2)}) collective-permute-start(bf16[2,160,256]{2,1,0:T(8,128)(2,1)S(1)} %bitcast.28), channel_id=1, source_target_pairs={{5,0},{6,1},{7,2},{4,3},{9,4},{10,5},{11,6},{8,7},{13,8},{14,9},{1... | collective-permute-start | bytes 491528 | tf_op jit(solution)/shard_map/ppermute | solution.py:446
  10.8 38.6 %collective-permute-start.3 = (bf16[2,160,256]{2,1,0:T(8,128)(2,1)S(1)}, bf16[2,160,256]{2,1,0:T(8,128)(2,1)S(1)}, u32[]{:S(2)}, u32[]{:S(2)}) collective-permute-start(bf16[2,160,256]{2,1,0:T(8,128)(2,1)S(1)} %bitcast.29), channel_id=1, source_target_pairs={{7,0},{4,1},{5,2},{6,3},{11,4},{8,5},{9,6},{10,7},{15,8},{12,9},{1... | collective-permute-start | bytes 491528 | tf_op jit(solution)/shard_map/ppermute | solution.py:446
  12.5 44.1 %collective-permute-start.2 = (bf16[2,160,256]{2,1,0:T(8,128)(2,1)S(1)}, bf16[2,160,256]{2,1,0:T(8,128)(2,1)S(1)}, u32[]{:S(2)}, u32[]{:S(2)}) collective-permute-start(bf16[2,160,256]{2,1,0:T(8,128)(2,1)S(1)} %bitcast.30), channel_id=1, source_target_pairs={{4,0},{5,1},{6,2},{7,3},{8,4},{9,5},{10,6},{11,7},{12,8},{13,9},{1... | collective-permute-start | bytes 491528 | tf_op jit(solution)/shard_map/ppermute | solution.py:446
  19.0 37.7 %collective-permute-start.1 = (bf16[2,160,256]{2,1,0:T(8,128)(2,1)S(1)}, bf16[2,160,256]{2,1,0:T(8,128)(2,1)S(1)}, u32[]{:S(2)}, u32[]{:S(2)}) collective-permute-start(bf16[2,160,256]{2,1,0:T(8,128)(2,1)S(1)} %bitcast.31), channel_id=1, source_target_pairs={{1,0},{2,1},{3,2},{0,3},{5,4},{6,5},{7,6},{4,7},{9,8},{10,9},{11,1... | collective-permute-start | bytes 491528 | tf_op jit(solution)/shard_map/ppermute | solution.py:446
  19.6 38.5 %collective-permute-start = (bf16[2,160,256]{2,1,0:T(8,128)(2,1)S(1)}, bf16[2,160,256]{2,1,0:T(8,128)(2,1)}, u32[]{:S(2)}, u32[]{:S(2)}) collective-permute-start(bf16[2,160,256]{2,1,0:T(8,128)(2,1)S(1)} %bitcast.32), channel_id=1, source_target_pairs={{3,0},{0,1},{1,2},{2,3},{7,4},{4,5},{5,6},{6,7},{11,8},{8,9},{9,10... | collective-permute-start | bytes 491528 | tf_op jit(solution)/shard_map/ppermute | solution.py:446
  37.2 30.6 %copy-start = (bf16[16,496,128]{2,1,0:T(8,128)(2,1)}, bf16[16,496,128]{2,1,0:T(8,128)(2,1)S(1)}, u32[]{:S(2)}) copy-start(bf16[16,496,128]{2,1,0:T(8,128)(2,1)S(1)} %all-to-all-done.load_ref) | copy-start | bytes 6094852
  38.8 17.9 %copy-start.8 = (bf16[2,160,256]{2,1,0:T(8,128)(2,1)}, bf16[2,160,256]{2,1,0:T(8,128)(2,1)S(1)}, u32[]{:S(2)}) copy-start(bf16[2,160,256]{2,1,0:T(8,128)(2,1)S(1)} %collective-permute-done.4.later_below_ref) | copy-start | bytes 491524
  38.8 29.0 %collective-permute-start.6 = (bf16[4,160,128]{2,1,0:T(8,128)(2,1)}, bf16[4,160,128]{2,1,0:T(8,128)(2,1)}, u32[]{:S(2)}, u32[]{:S(2)}) collective-permute-start(bf16[4,160,128]{2,1,0:T(8,128)(2,1)} %get-tuple-element.24), channel_id=1, source_target_pairs={{16,0},{24,8},{80,64},{88,72},{32,16},{40,24},{96,80},{104,88},{48... | collective-permute-start | bytes 491528 | tf_op jit(solution)/shard_map/ppermute | solution.py:466
  49.4 7.3 %copy-start.9 = (bf16[2,160,256]{2,1,0:T(8,128)(2,1)}, bf16[2,160,256]{2,1,0:T(8,128)(2,1)S(1)}, u32[]{:S(2)}) copy-start(bf16[2,160,256]{2,1,0:T(8,128)(2,1)S(1)} %collective-permute-done.3.later_above_ref) | copy-start | bytes 491524
  49.4 18.4 %collective-permute-start.5 = (bf16[4,160,128]{2,1,0:T(8,128)(2,1)}, bf16[4,160,128]{2,1,0:T(8,128)(2,1)}, u32[]{:S(2)}, u32[]{:S(2)}) collective-permute-start(bf16[4,160,128]{2,1,0:T(8,128)(2,1)} %get-tuple-element.25), channel_id=1, source_target_pairs={{16,0},{24,8},{80,64},{88,72},{32,16},{40,24},{96,80},{104,88},{48... | collective-permute-start | bytes 491528 | tf_op jit(solution)/shard_map/ppermute | solution.py:466
  52.1 15.8 %all-to-all-start.1 = ((f32[16,8,128]{2,1,0:T(8,128)}), f32[16,8,128]{2,1,0:T(8,128)}, u32[]{:S(2)}, u32[]{:S(2)}) async-start(f32[16,8,128]{2,1,0:T(8,128)} %combine.1), calls=%async_computation.1 | async-start | bytes 131072 | tf_op jit(solution)/shard_map/all_to_all | solution.py:435
  56.7 0.7 copy-start.10
  57.4 0.7 copy-start.11
  120.8 7.4 %collective-permute-start.7 = (bf16[20,320,128]{2,1,0:T(8,128)(2,1)}, bf16[20,320,128]{2,1,0:T(8,128)(2,1)S(1)}, u32[]{:S(2)}, u32[]{:S(2)}) collective-permute-start(bf16[20,320,128]{2,1,0:T(8,128)(2,1)} %get-tuple-element.12), channel_id=1, source_target_pairs={{0,4},{4,0},{8,12},{12,8},{16,20},{20,16},{24,28},{28,24},{32,36},... | collective-permute-start | bytes 4915208 | tf_op jit(solution)/shard_map/ppermute | solution.py:510
  121.2 16.2 %all-to-all-start.2 = ((f32[32,8,128]{2,1,0:T(8,128)}), f32[32,8,128]{2,1,0:T(8,128)S(1)}, u32[]{:S(2)}, u32[]{:S(2)}) async-start(f32[32,8,128]{2,1,0:T(8,128)} %get-tuple-element.14), calls=%async_computation.2 | async-start | bytes 262144 | tf_op jit(solution)/shard_map/all_to_all | solution.py:432
  128.2 1.2 copy-start.5
  137.4 30.1 %copy-start.1 = (bf16[2,1,160,512]{3,2,1,0:T(8,128)(2,1)S(1)}, bf16[2,1,160,512]{3,2,1,0:T(8,128)(2,1)}, u32[]{:S(2)}) copy-start(bf16[2,1,160,512]{3,2,1,0:T(8,128)(2,1)} %param.5) | copy-start | bytes 983044
  137.4 30.1 %copy-start.2 = (f32[320,512]{1,0:T(8,128)S(1)}, f32[320,512]{1,0:T(8,128)}, u32[]{:S(2)}) copy-start(f32[320,512]{1,0:T(8,128)} %get-tuple-element.15.act_ref) | copy-start | bytes 1966084
  137.4 30.1 %copy-start.3 = (f32[16,512]{1,0:T(8,128)S(1)}, f32[16,512]{1,0:T(8,128)}, u32[]{:S(2)}) copy-start(f32[16,512]{1,0:T(8,128)} %get-tuple-element.13.norm_ref) | copy-start | bytes 98308
  137.4 30.1 %copy-start.4 = (f32[512]{0:T(512)S(1)}, f32[512]{0:T(512)}, u32[]{:S(2)}) copy-start(f32[512]{0:T(512)} %param.6) | copy-start | bytes 6148
  137.4 0.7 copy-start.7

commit v7 on v6

--- a/solution.py
+++ b/solution.py
@@ -11,7 +11,8 @@
 GROUPS = 32
 EPS = 1e-06
 TEAM = 4
-EDGES = ((0, -1), (0, 1), (1, 0), (1, -1), (1, 1))
+SHARE = 208
+EDGES = ((1, 0), (0, -1), (0, 1), (1, -1), (1, 1))
 F32 = jnp.float32
 BF16 = jnp.bfloat16
 
@@ -62,7 +63,7 @@
     return ahead, slab, behind
 
 
-def pack_kernel(teams, feats_ref, up_ref, load_ref):
+def pack_kernel(teams, feats_ref, up_ref, later_ref, load_ref):
     positions, chans = feats_ref.shape
     cols = up_ref.shape[1]
     rows = load_ref.shape[1]
@@ -86,12 +87,23 @@
         for r in range(rows):
             load_ref[j, r, 0:cols, :] = keep
             load_ref[j, r, cols : 2 * cols, :] = send
+    order = lax.axis_index("tm") & 3
     for r in range(rows):
-        pair = jnp.concatenate(
-            [up_ref[0, :, r * outs : (r + 1) * outs], up_ref[1, :, r * outs : (r + 1) * outs]], axis=1
+        own, after = (
+            jnp.concatenate(
+                [ref[0, :, r * outs : (r + 1) * outs], ref[1, :, r * outs : (r + 1) * outs]], axis=1
+            )
+            for ref in (up_ref, later_ref)
         )
-        for j in range(TEAM):
-            load_ref[j, r, 2 * cols : 3 * cols, :] = pair
+        for d in range(4):
+
+            @pl.when(order == d)
+            def _():
+                first = d * (SHARE - cols)
+                share = jnp.concatenate([own[first:], after[0 : min(cols, SHARE - cols + first)]], axis=0)
+                for j in range(TEAM):
+                    load_ref[j, r, 2 * cols : 2 * cols + share.shape[0], :] = share
+
     floats = feats.astype(F32)
     first = members(chans, 0)
     second = members(chans, GROUPS)
@@ -108,10 +120,10 @@
     parts = jnp.concatenate([parts, jnp.zeros_like(parts)], axis=0).astype(BF16)
     for r in range(rows):
         for j in range(TEAM):
-            load_ref[j, r, 3 * cols :, :] = parts
-
-
-def combine_kernel(count, load_ref, out_ref):
+            load_ref[j, r, 2 * cols + SHARE :, :] = parts
+
+
+def combine_kernel(count, load_ref, out_ref, swap_ref):
     stats = []
     for j in range(load_ref.shape[0]):
         for r in range(load_ref.shape[1]):
@@ -128,6 +140,9 @@
     moved = pltpu.roll(jnp.broadcast_to(spans, (8, 128)), GROUPS, 1)
     result = jnp.where(lane < GROUPS, jnp.broadcast_to(mean, (8, 128)), total + count * moved)
     out_ref[...] = jnp.broadcast_to(result[None], out_ref.shape)
+    size = swap_ref.shape[2]
+    start = load_ref.shape[2] - 16 - size
+    swap_ref[...] = load_ref[:, :, start : start + size, :]
 
 
 def dense_kernel(
@@ -197,21 +212,8 @@
     return centre, inverse
 
 
-def act_kernel(
-    positions, feats_ref, gain_ref, bias_ref, stats_ref, dense_ref, load_ref, halo0_ref, halo1_ref,
-    act_ref, sums_ref, norm_ref, swap_ref, sems,
-):
+def act_kernel(positions, feats_ref, gain_ref, bias_ref, stats_ref, dense_ref, act_ref, sums_ref, norm_ref):
     chans = gain_ref.shape[1]
-    cols = halo0_ref.shape[1]
-    slots = load_ref.shape[0]
-    tail = pl.ds(slots, halo0_ref.shape[0])
-    copies = [
-        pltpu.make_async_copy(load_ref.at[:, pl.ds(cols, 2 * cols)], swap_ref.at[pl.ds(0, slots)], sems.at[0]),
-        pltpu.make_async_copy(halo0_ref, swap_ref.at[tail, pl.ds(0, cols)], sems.at[1]),
-        pltpu.make_async_copy(halo1_ref, swap_ref.at[tail, pl.ds(cols, cols)], sems.at[2]),
-    ]
-    for copy in copies:
-        copy.start()
     centre, inverse = norm_rows(stats_ref, chans, positions)
     norm_ref[0:8] = centre
     norm_ref[8:16] = inverse
@@ -228,8 +230,6 @@
     rows = [gains[:, p * 128 : (p + 1) * 128] for p in range(pieces)]
     rows = rows + [biases[:, p * 128 : (p + 1) * 128] for p in range(pieces)]
     sums_ref[...] = jnp.broadcast_to(jnp.concatenate(rows, axis=0)[None], sums_ref.shape)
-    for copy in copies:
-        copy.wait()
 
 
 def append_kernel(part_ref, load_ref, out_ref, sums, sem):
@@ -244,7 +244,7 @@
 
 
 def weight_kernel(
-    teams, load_ref, other_ref, halo0_ref, halo1_ref, norm_ref, gain_ref, bias_ref, out_ref, hidden, acc
+    teams, load_ref, other_ref, norm_ref, gain_ref, bias_ref, out_ref, hidden, acc
 ):
     time_index = lax.axis_index("tm")
     core = time_index & 1
@@ -273,7 +273,7 @@
         for q in range(4):
             for r in range(rows):
                 j = 2 * x + q // 2
-                pair = jnp.where(core == q % 2, load_ref[j, r, 0:cols, :], other_ref[j * rows + r, 0:cols, :])
+                pair = jnp.where(core == q % 2, load_ref[j, r, 0:cols, :], other_ref[j, r, 0:cols, :])
                 preact = (pair.astype(F32) - centre) * inverse * gain + bias
                 value = preact * sigmoid(preact)
                 hidden[x, q + 1, r + 1] = value.astype(BF16)
@@ -284,21 +284,24 @@
                     hidden[x, 0, r + 1] = before.astype(BF16)
                     hidden[x, 5, r + 1] = jnp.zeros(hidden.shape[3:], BF16)
 
+    def share_of(x, d, r, first, last):
+        j = 2 * x + d // 2
+        return jnp.where(
+            core == d % 2,
+            load_ref[j, r, 2 * cols + first : 2 * cols + last, :],
+            other_ref[j, r, cols + first : cols + last, :],
+        )
+
     def ups_of(x, q):
         sides = [[], [], []]
         for r in range(rows):
-            j = 2 * x + q // 2
-            if q < 4:
-                pair = jnp.where(
-                    core == q % 2,
-                    load_ref[j, r, 2 * cols : 3 * cols, :],
-                    other_ref[j * rows + r, cols : 2 * cols, :],
-                )
-            else:
-                near = (halo0_ref, halo1_ref)[x]
-                pair = jnp.where(
-                    core == 0, near[r], other_ref[TEAM * rows + r, x * cols : (x + 1) * cols, :]
-                )
+            pieces = []
+            for d in range(4):
+                first = max(q * cols, d * SHARE) - d * SHARE
+                last = min((q + 1) * cols, (d + 1) * SHARE) - d * SHARE
+                if first < last:
+                    pieces.append(share_of(x, d, r, first, last))
+            pair = jnp.concatenate(pieces, axis=0)
             wide = pair.astype(F32)
             if q == 4 and x == 1:
                 wide = jnp.where(end, 0.0, wide)
@@ -401,7 +404,6 @@
     wide = chans // TEAM
     count = positions * devices * (chans // GROUPS)
     vmem = pl.BlockSpec(memory_space=pltpu.VMEM)
-    anywhere = pl.BlockSpec(memory_space=pl.ANY)
     far = pl.BlockSpec(memory_space=pltpu.HBM)
 
     def params(mebibytes):
@@ -412,7 +414,7 @@
     gain = norm_gain.reshape(1, chans)
     bias = norm_bias.reshape(1, chans)
     size = TEAM * rows
-    length = positions + cols + 16
+    length = positions + SHARE + 16
     places = [(big, z) for big in range(groups // 4) for z in range(4)]
     chips = [(x, z) for x in range(2) for z in range(2)]
 
@@ -452,18 +454,8 @@
         out_shape=jax.ShapeDtypeStruct((TEAM, rows, length, wide), BF16),
         compiler_params=params(62),
         name="pack",
-    )(feats, ups)
+    )(feats, ups, halos[0])
     load = in_teams(load.reshape(size, length, wide)).reshape(TEAM, rows, length, wide)
-
-    opens = lax.shift_right_logical(lax.axis_index("tm"), 2) & 3 == 0
-    runs = [load[2 * x, :, 2 * cols : 3 * cols] for x in range(2)]
-    halo = []
-    for x in range(2):
-        moves = []
-        for o in places:
-            goal = (o[0], o[1] + 1) if o[1] < 3 else ((o[0] + x) % (groups // 4), 0)
-            moves += [(place(goal, i, 0), place(o, i, 0)) for i in chips]
-        halo.append(lax.ppermute(jnp.where(opens, runs[1 - x], runs[x]), "tm", moves))
 
     def whole(shape):
         return pl.BlockSpec(shape, lambda *s: (0,) * len(shape))
@@ -481,38 +473,37 @@
         compiler_params=params(62),
         name="dense",
     )
-    dense = dense_call(ups, *halos, weight)
-
-    stats = pl.pallas_call(
+    dense = dense_call(ups, halos[1], halos[2], halos[0], halos[3], halos[4], weight)
+
+    stats, swap = pl.pallas_call(
         functools.partial(combine_kernel, float(positions * (chans // GROUPS))),
         in_specs=[vmem],
-        out_specs=vmem,
-        out_shape=jax.ShapeDtypeStruct((2 * groups, 8, 128), F32),
-        compiler_params=params(16),
+        out_shape=(
+            jax.ShapeDtypeStruct((2 * groups, 8, 128), F32),
+            jax.ShapeDtypeStruct((TEAM, rows, cols + SHARE, 128), BF16),
+        ),
+        compiler_params=params(60),
         name="combine",
     )(load)
+    other = lax.ppermute(swap, "tm", [(t, t ^ 1) for t in range(tms)])
     stats = in_stars(stats)
 
-    act, sums, norm, swap = pl.pallas_call(
+    act, sums, norm = pl.pallas_call(
         functools.partial(act_kernel, positions * size),
-        in_specs=[pl.BlockSpec()] * 3 + [vmem, pl.BlockSpec()] + [anywhere] * 3,
-        out_specs=(pl.BlockSpec(), pl.BlockSpec(), pl.BlockSpec(), anywhere),
-        scratch_shapes=[pltpu.SemaphoreType.DMA((3,))],
+        in_specs=[pl.BlockSpec()] * 3 + [vmem, pl.BlockSpec()],
         out_shape=(
             jax.ShapeDtypeStruct((positions, chans), F32),
             jax.ShapeDtypeStruct((2 * size, 8, 128), F32),
             jax.ShapeDtypeStruct((16, chans), F32),
-            jax.ShapeDtypeStruct((size + rows, 2 * cols, 128), BF16),
         ),
         compiler_params=params(62),
         name="act",
-    )(feats, gain, bias, stats, dense, load.reshape(size, length, wide), *halo)
-    other = lax.ppermute(swap, "tm", [(t, t ^ 1) for t in range(tms)])
+    )(feats, gain, bias, stats, dense)
     sums = in_pairs(sums)
 
     weight_call = pl.pallas_call(
         functools.partial(weight_kernel, tms),
-        in_specs=[vmem, vmem] + [pl.BlockSpec()] * 5,
+        in_specs=[vmem, vmem] + [pl.BlockSpec()] * 3,
         out_specs=vmem,
         out_shape=jax.ShapeDtypeStruct((groups, 14 * step + 8, 128), F32),
         scratch_shapes=[
@@ -522,7 +513,7 @@
         compiler_params=params(62),
         name="wgrad",
     )
-    part = weight_call(load, other, *halo, norm, gain, bias)
+    part = weight_call(load, other, norm, gain, bias)
     part = pl.pallas_call(
         append_kernel,
         in_specs=[far, vmem],

time: 170 us -> 126 us (0.74)
  Pallas kernels: 77.6 us -> 30.6 us
  blocking collectives: 27.8 us -> 63 us
  starting transfers between devices: 41.7 us -> 23.2 us
  waiting for transfers between devices: 17.1 us -> 3.16 us
    pallas_call x1, Pallas kernels: 52.9 us -> 2.87 us  [on_device(): pl.pallas_call(functools.partial(act_kernel, positions * size), in_specs=...]
    all_to_all x0 -> x1, blocking collectives: none -> 36 us  [in_teams(): lax.all_to_all(value, ('tm', 'rows'), 0, 0, tiled=True, axis_index_groups...]
    all_to_all x1 -> x0, waiting for transfers between devices: 16.2 us -> none  [in_teams(): lax.all_to_all(value, ('tm', 'rows'), 0, 0, tiled=True, axis_index_groups...]
    ppermute x2 -> x0, starting transfers between devices: 12.5 us -> none  [on_device(): lax.ppermute(jnp.where(opens, runs[1 - x], runs[x]), 'tm', moves)]
    all_to_all x1 -> x0, starting transfers between devices: 6.89 us -> none  [in_teams(): lax.all_to_all(value, ('tm', 'rows'), 0, 0, tiled=True, axis_index_groups...]
    all_to_all x1, starting transfers between devices: 4.59 us -> 10.1 us  [in_stars(): lax.all_to_all(value, 'tm', 0, 0, tiled=True, axis_index_groups=stars)]
    ppermute x5, starting transfers between devices: 10.3 us -> 5.71 us  [neighbour(): return lax.ppermute(ups, ('tm', 'rows'), moves)]
    ppermute x5, waiting for transfers between devices: 0.87 us -> 3.16 us  [neighbour(): return lax.ppermute(ups, ('tm', 'rows'), moves)]
  transfers between devices with their start and end apart: 11 -> 8, of which waited for: 2 -> 1; matrix products, arithmetic and copies ran while one was open for 0% -> 0% of each run, Pallas kernels for 11% -> 17%
where the time goes in v7:
time: 126 us; the launch traced here: 125 us
  blocking collectives  63 us (50%)
  Pallas kernels  30.6 us (24%)
  starting transfers between devices  23.2 us (18%)
  local copies, waits for them, and re-layouts  4.43 us (4%)
  waiting for transfers between devices  3.16 us (3%)
    all_to_all x1, blocking collectives, in_teams(): lax.all_to_all(value, ('tm', 'rows'), 0, 0, tiled=True, axis_index_groups...  36 us
    all_to_all x1, blocking collectives, in_ranks(): lax.all_to_all(value, 'tm', 0, 0, tiled=True, axis_index_groups=ranks)  27 us
    all_to_all x1, starting transfers between devices, in_stars(): lax.all_to_all(value, 'tm', 0, 0, tiled=True, axis_index_groups=stars)  10.1 us
    pallas_call x1, Pallas kernels, on_device(): dense_call(ups, halos[1], halos[2], halos[0], halos[3], halos[4], weight)  9.83 us
    pallas_call x1, Pallas kernels, on_device(): part = weight_call(load, other, norm, gain, bias)  8.03 us
    all_to_all x1, starting transfers between devices, in_pairs(): lax.all_to_all(value, ('tm', 'rows'), 0, 0, tiled=True, axis_index_groups...  7.44 us
    ppermute x5, starting transfers between devices, neighbour(): return lax.ppermute(ups, ('tm', 'rows'), moves)  5.71 us
    unnamed x24, local copies, waits for them, and re-layouts  4.43 us
  transfers between devices with their start and end apart: 8, of which 1 were waited for; matrix products, arithmetic and copies ran while one was open for 0% of the time, Pallas kernels for 17%

profile of v7, /device:TPU:40, one launch (start us, length us, event | category | flops | bytes accessed | tf_op | source)
XLA Modules:
  0.0 125.2 jit_solution(164334221069091652)
XLA Ops:
  0.6 0.1 collective-permute-start
  0.7 3.1 %collective-permute-done.later_ref = bf16[2,160,256]{2,1,0:T(8,128)(2,1)S(1)} collective-permute-done((bf16[2,160,256]{2,1,0:T(8,128)(2,1)}, bf16[2,160,256]{2,1,0:T(8,128)(2,1)S(1)}, u32[]{:S(2)}, u32[]{:S(2)}) %collective-permute-start) | collective-permute-done | bytes 163872 | tf_op jit(solution)/shard_map/ppermute | solution.py:448
  3.9 0.7 copy-done.6
  4.5 4.0 %pack.1 = bf16[4,4,544,128]{3,2,1,0:T(8,128)(2,1)} custom-call(bf16[320,512]{1,0:T(8,128)(2,1)} %bitcast.12, bf16[2,160,256]{2,1,0:T(8,128)(2,1)} %bitcast.22, bf16[2,160,256]{2,1,0:T(8,128)(2,1)} %copy-done.6), custom_call_target="tpu_custom_call" | custom-call | tf_op jit(solution)/shard_map/pack/pallas_call | solution.py:452
  8.6 36.0 %all_to_all.20 = bf16[16,544,128]{2,1,0:T(8,128)(2,1)} all-to-all(bf16[16,544,128]{2,1,0:T(8,128)(2,1)} %bitcast.20), channel_id=1, replica_groups={{0,1,2,3,8,9,10,11,64,65,66,67,72,73,74,75},{4,5,6,7,12,13,14,15,68,69,..., dimensions={0} | all-to-all | bytes 4456448 | tf_op jit(solution)/shard_map/all_to_all | solution.py:431
  44.5 2.9 %combine.1 = (f32[16,8,128]{2,1,0:T(8,128)}, bf16[4,4,368,128]{3,2,1,0:T(8,128)(2,1)}) custom-call(bf16[4,4,544,128]{3,2,1,0:T(8,128)(2,1)} %bitcast.18), custom_call_target="tpu_custom_call" | custom-call | tf_op jit(solution)/shard_map/combine/pallas_call | solution.py:478
  47.4 0.0 collective-permute-start.1
  47.4 1.1 collective-permute-start.2
  48.5 1.0 collective-permute-start.3
  49.5 1.2 collective-permute-start.4
  50.7 2.4 %collective-permute-start.5 = (bf16[2,160,256]{2,1,0:T(8,128)(2,1)S(1)}, bf16[2,160,256]{2,1,0:T(8,128)(2,1)}, u32[]{:S(2)}, u32[]{:S(2)}) collective-permute-start(bf16[2,160,256]{2,1,0:T(8,128)(2,1)S(1)} %bitcast.27), channel_id=1, source_target_pairs={{5,0},{6,1},{7,2},{4,3},{9,4},{10,5},{11,6},{8,7},{13,8},{14,9},{1... | collective-permute-start | bytes 491528 | tf_op jit(solution)/shard_map/ppermute | solution.py:448
  53.1 10.1 %all-to-all-start.1 = ((f32[16,8,128]{2,1,0:T(8,128)}), f32[16,8,128]{2,1,0:T(8,128)S(1)}, u32[]{:S(2)}, u32[]{:S(2)}) async-start(f32[16,8,128]{2,1,0:T(8,128)} %get-tuple-element.14), calls=%async_computation.1 | async-start | bytes 131072 | tf_op jit(solution)/shard_map/all_to_all | solution.py:437
  63.2 0.7 copy-done.10
  63.9 0.7 copy-done.11
  64.5 9.8 %dense.1.dense_ref = f32[320,512]{1,0:T(8,128)} custom-call(bf16[2,160,256]{2,1,0:T(8,128)(2,1)} %bitcast.23, bf16[2,160,256]{2,1,0:T(8,128)(2,1)} %copy-done.9, bf16[2,160,256]{2,1,0:T(8,128)(2,1)} %copy-done.10, bf16[2,160,256]{2,1,0:T(8,128)(2,1)} %copy-done.6, bf16[2,160,256]{2,1,0:T(8,128)(2,1)} %copy-done.11, ...), custom_call_target="tpu_custom_call" | custom-call | tf_op jit(solution)/shard_map/dense/pallas_call | solution.py:476
  74.4 0.6 copy-done.8
  75.0 2.9 %act.1 = (f32[320,512]{1,0:T(8,128)}, f32[32,8,128]{2,1,0:T(8,128)}, f32[16,512]{1,0:T(8,128)}) custom-call(bf16[320,512]{1,0:T(8,128)(2,1)} %bitcast.13, f32[1,512]{1,0:T(1,128)} %bitcast.15, f32[1,512]{1,0:T(1,128)} %bitcast.28, f32[16,8,128]{2,1,0:T(8,128)} %copy-done.8, f32[320,512]{1,0:T(8,128)} %dense.1.dense_ref), custom_call_target="tpu_custom_call" | custom-call | tf_op jit(solution)/shard_map/act/pallas_call | solution.py:491
  77.9 7.4 %all-to-all-start.2 = ((f32[32,8,128]{2,1,0:T(8,128)}), f32[32,8,128]{2,1,0:T(8,128)S(1)}, u32[]{:S(2)}, u32[]{:S(2)}) async-start(f32[32,8,128]{2,1,0:T(8,128)} %get-tuple-element.16), calls=%async_computation.2 | async-start | bytes 262144 | tf_op jit(solution)/shard_map/all_to_all | solution.py:434
  85.3 1.1 copy-done.4
  86.5 8.0 %wgrad.1.part_ref = f32[8,120,128]{2,1,0:T(8,128)} custom-call(bf16[4,4,544,128]{3,2,1,0:T(8,128)(2,1)} %bitcast.19, bf16[4,4,368,128]{3,2,1,0:T(8,128)(2,1)} %copy-done.4, f32[16,512]{1,0:T(8,128)} %get-tuple-element.15.norm_ref, f32[1,512]{1,0:T(1,128)} %bitcast.16, f32[1,512]{1,0:T(1,128)} %bitcast.29), custom_call_target="tpu_custom_call" | custom-call | tf_op jit(solution)/shard_map/wgrad/pallas_call | solution.py:516
  94.5 0.7 copy-done.7
  95.2 1.6 %append.1 = f32[8,120,128]{2,1,0:T(8,128)} custom-call(f32[8,120,128]{2,1,0:T(8,128)} %wgrad.1.part_ref, f32[32,8,128]{2,1,0:T(8,128)} %copy-done.7), custom_call_target="tpu_custom_call", output_to_operand_aliasing={{}: (0, {})} | custom-call | tf_op jit(solution)/shard_map/append/pallas_call | solution.py:517
  96.7 27.0 %all_to_all.21.load_ref = f32[8,120,128]{2,1,0:T(8,128)S(1)} all-to-all(f32[8,120,128]{2,1,0:T(8,128)} %append.1), channel_id=1, replica_groups={{0,16,32,48,128,144,160,176},{4,20,36,52,132,148,164,180},{8,24,40,56,1..., dimensions={0} | all-to-all | bytes 983040 | tf_op jit(solution)/shard_map/all_to_all | solution.py:440
  123.8 1.4 %final.1 = (bf16[320,512]{1,0:T(8,128)(2,1)}, f32[9,3,8,64]{3,2,1,0:T(8,128)}, f32[1,512]{1,0:T(1,128)}, f32[1,512]{1,0:T(1,128)}) custom-call(f32[8,120,128]{2,1,0:T(8,128)S(1)} %all_to_all.21.load_ref, f32[320,512]{1,0:T(8,128)S(1)} %copy-done.1, bf16[320,512]{1,0:T(8,128)(2,1)S(1)} %bitcast.14, f32[16,512]{1,0:T(8,128)S(1)} %copy-done.2, ...), custom_call_target="tpu_custom_call" | custom-call | tf_op jit(solution)/shard_map/final/pallas_call | solution.py:529
  (25 shorter events, 0.1 us)
Async XLA Ops:
  0.6 3.2 %collective-permute-start = (bf16[2,160,256]{2,1,0:T(8,128)(2,1)}, bf16[2,160,256]{2,1,0:T(8,128)(2,1)S(1)}, u32[]{:S(2)}, u32[]{:S(2)}) collective-permute-start(bf16[2,160,256]{2,1,0:T(8,128)(2,1)} %bitcast.21), channel_id=1, source_target_pairs={{4,0},{5,1},{6,2},{7,3},{8,4},{9,5},{10,6},{11,7},{12,8},{13,9},{1... | collective-permute-start | bytes 491528 | tf_op jit(solution)/shard_map/ppermute | solution.py:448
  3.9 0.7 copy-start.6
  44.5 2.9 %copy-start.5 = (bf16[2,1,160,256]{3,2,1,0:T(8,128)(2,1)S(1)}, bf16[2,1,160,256]{3,2,1,0:T(8,128)(2,1)}, u32[]{:S(2)}) copy-start(bf16[2,1,160,256]{3,2,1,0:T(8,128)(2,1)} %param.9) | copy-start | bytes 491524
  47.4 37.9 %collective-permute-start.1 = (bf16[4,4,368,128]{3,2,1,0:T(8,128)(2,1)}, bf16[4,4,368,128]{3,2,1,0:T(8,128)(2,1)S(1)}, u32[]{:S(2)}, u32[]{:S(2)}) collective-permute-start(bf16[4,4,368,128]{3,2,1,0:T(8,128)(2,1)} %get-tuple-element.13), channel_id=1, source_target_pairs={{0,4},{4,0},{8,12},{12,8},{16,20},{20,16},{24,28},{28,24},{32,36},... | collective-permute-start | bytes 4521992 | tf_op jit(solution)/shard_map/ppermute | solution.py:488
  47.4 15.7 %collective-permute-start.2 = (bf16[2,160,256]{2,1,0:T(8,128)(2,1)S(1)}, bf16[2,160,256]{2,1,0:T(8,128)(2,1)S(1)}, u32[]{:S(2)}, u32[]{:S(2)}) collective-permute-start(bf16[2,160,256]{2,1,0:T(8,128)(2,1)S(1)} %bitcast.24), channel_id=1, source_target_pairs={{3,0},{0,1},{1,2},{2,3},{7,4},{4,5},{5,6},{6,7},{11,8},{8,9},{9,10... | collective-permute-start | bytes 491528 | tf_op jit(solution)/shard_map/ppermute | solution.py:448
  48.5 14.6 %collective-permute-start.3 = (bf16[2,160,256]{2,1,0:T(8,128)(2,1)S(1)}, bf16[2,160,256]{2,1,0:T(8,128)(2,1)S(1)}, u32[]{:S(2)}, u32[]{:S(2)}) collective-permute-start(bf16[2,160,256]{2,1,0:T(8,128)(2,1)S(1)} %bitcast.25), channel_id=1, source_target_pairs={{1,0},{2,1},{3,2},{0,3},{5,4},{6,5},{7,6},{4,7},{9,8},{10,9},{11,1... | collective-permute-start | bytes 491528 | tf_op jit(solution)/shard_map/ppermute | solution.py:448
  49.5 13.6 %collective-permute-start.4 = (bf16[2,160,256]{2,1,0:T(8,128)(2,1)S(1)}, bf16[2,160,256]{2,1,0:T(8,128)(2,1)S(1)}, u32[]{:S(2)}, u32[]{:S(2)}) collective-permute-start(bf16[2,160,256]{2,1,0:T(8,128)(2,1)S(1)} %bitcast.26), channel_id=1, source_target_pairs={{7,0},{4,1},{5,2},{6,3},{11,4},{8,5},{9,6},{10,7},{15,8},{12,9},{1... | collective-permute-start | bytes 491528 | tf_op jit(solution)/shard_map/ppermute | solution.py:448
  50.7 13.8 %collective-permute-start.5 = (bf16[2,160,256]{2,1,0:T(8,128)(2,1)S(1)}, bf16[2,160,256]{2,1,0:T(8,128)(2,1)}, u32[]{:S(2)}, u32[]{:S(2)}) collective-permute-start(bf16[2,160,256]{2,1,0:T(8,128)(2,1)S(1)} %bitcast.27), channel_id=1, source_target_pairs={{5,0},{6,1},{7,2},{4,3},{9,4},{10,5},{11,6},{8,7},{13,8},{14,9},{1... | collective-permute-start | bytes 491528 | tf_op jit(solution)/shard_map/ppermute | solution.py:448
  53.1 21.3 %all-to-all-start.1 = ((f32[16,8,128]{2,1,0:T(8,128)}), f32[16,8,128]{2,1,0:T(8,128)S(1)}, u32[]{:S(2)}, u32[]{:S(2)}) async-start(f32[16,8,128]{2,1,0:T(8,128)} %get-tuple-element.14), calls=%async_computation.1 | async-start | bytes 131072 | tf_op jit(solution)/shard_map/all_to_all | solution.py:437
  63.1 1.4 %copy-start.9 = (bf16[2,160,256]{2,1,0:T(8,128)(2,1)}, bf16[2,160,256]{2,1,0:T(8,128)(2,1)S(1)}, u32[]{:S(2)}) copy-start(bf16[2,160,256]{2,1,0:T(8,128)(2,1)S(1)} %collective-permute-done.2.above_ref) | copy-start | bytes 491524
  63.2 0.7 copy-start.10
  63.9 0.7 copy-start.11
  74.4 0.6 copy-start.8
  77.9 16.6 %all-to-all-start.2 = ((f32[32,8,128]{2,1,0:T(8,128)}), f32[32,8,128]{2,1,0:T(8,128)S(1)}, u32[]{:S(2)}, u32[]{:S(2)}) async-start(f32[32,8,128]{2,1,0:T(8,128)} %get-tuple-element.16), calls=%async_computation.2 | async-start | bytes 262144 | tf_op jit(solution)/shard_map/all_to_all | solution.py:434
  85.3 1.1 copy-start.4
  86.4 37.3 %copy-start = (bf16[2,1,160,512]{3,2,1,0:T(8,128)(2,1)S(1)}, bf16[2,1,160,512]{3,2,1,0:T(8,128)(2,1)}, u32[]{:S(2)}) copy-start(bf16[2,1,160,512]{3,2,1,0:T(8,128)(2,1)} %param.5) | copy-start | bytes 983044
  86.4 37.3 %copy-start.1 = (f32[320,512]{1,0:T(8,128)S(1)}, f32[320,512]{1,0:T(8,128)}, u32[]{:S(2)}) copy-start(f32[320,512]{1,0:T(8,128)} %get-tuple-element.17.act_ref) | copy-start | bytes 1966084
  86.5 37.3 %copy-start.2 = (f32[16,512]{1,0:T(8,128)S(1)}, f32[16,512]{1,0:T(8,128)}, u32[]{:S(2)}) copy-start(f32[16,512]{1,0:T(8,128)} %get-tuple-element.15.norm_ref) | copy-start | bytes 98308
  86.5 37.3 %copy-start.3 = (f32[512]{0:T(512)S(1)}, f32[512]{0:T(512)}, u32[]{:S(2)}) copy-start(f32[512]{0:T(512)} %param.6) | copy-start | bytes 6148
  94.5 0.7 copy-start.7

commit v8 on v4

--- a/solution.py
+++ b/solution.py
@@ -11,7 +11,9 @@
 GROUPS = 32
 EPS = 1e-06
 TEAM = 4
-EDGES = ((0, -1), (0, 1), (1, 0), (1, -1), (1, 1))
+SHARES = ((0, 192), (192, 384), (384, 576), (576, 800))
+HALF = 112
+EDGES = ((1, 0), (0, -1), (0, 1), (1, -1), (1, 1))
 F32 = jnp.float32
 BF16 = jnp.bfloat16
 
@@ -60,7 +62,7 @@
     return ahead, slab, behind
 
 
-def pack_kernel(teams, feats_ref, up_ref, load_ref):
+def pack_kernel(teams, feats_ref, up_ref, later_ref, load_ref):
     positions, chans = feats_ref.shape
     cols = up_ref.shape[1]
     rows = load_ref.shape[1]
@@ -71,13 +73,29 @@
     mover = ones_where(iota((chans, chans), 0) == source)
     moved = jnp.dot(feats, mover, preferred_element_type=F32).astype(BF16)
     outs = up_ref.shape[2] // rows
+    for j in range(TEAM):
+        for r in range(rows):
+            load_ref[j, r, 0:positions, :] = moved[:, j * wide : (j + 1) * wide]
+    order = lax.axis_index("tm") & (TEAM - 1)
     for r in range(rows):
-        pair = jnp.concatenate(
-            [up_ref[0, :, r * outs : (r + 1) * outs], up_ref[1, :, r * outs : (r + 1) * outs]], axis=1
+        own, after = (
+            jnp.concatenate(
+                [ref[0, :, r * outs : (r + 1) * outs], ref[1, :, r * outs : (r + 1) * outs]], axis=1
+            )
+            for ref in (up_ref, later_ref)
         )
-        for j in range(TEAM):
-            load_ref[j, r, 0:positions, :] = moved[:, j * wide : (j + 1) * wide]
-            load_ref[j, r, positions : positions + cols, :] = pair
+        for d in range(TEAM):
+
+            @pl.when(order == d)
+            def _():
+                first, last = (value - d * cols for value in SHARES[d])
+                share = jnp.concatenate([own[first:], after[0 : last - cols]], axis=0)
+                size = (last - first) // 2
+                for j in range(TEAM):
+                    core = j % 2
+                    part = share[core * size : (core + 1) * size]
+                    load_ref[j, r, positions : positions + size, :] = part
+
     floats = feats.astype(F32)
     first = members(chans, 0)
     second = members(chans, GROUPS)
@@ -94,10 +112,10 @@
     parts = jnp.concatenate([parts, jnp.zeros_like(parts)], axis=0).astype(BF16)
     for r in range(rows):
         for j in range(TEAM):
-            load_ref[j, r, positions + cols :, :] = parts
-
-
-def combine_kernel(count, load_ref, out_ref):
+            load_ref[j, r, positions + HALF :, :] = parts
+
+
+def combine_kernel(count, load_ref, out_ref, swap_ref):
     stats = []
     for j in range(load_ref.shape[0]):
         for r in range(load_ref.shape[1]):
@@ -114,6 +132,8 @@
     moved = pltpu.roll(jnp.broadcast_to(spans, (8, 128)), GROUPS, 1)
     result = jnp.where(lane < GROUPS, jnp.broadcast_to(mean, (8, 128)), total + count * moved)
     out_ref[...] = jnp.broadcast_to(result[None], out_ref.shape)
+    start = load_ref.shape[2] - 16 - HALF
+    swap_ref[...] = load_ref[:, :, start : start + HALF, :]
 
 
 def dense_kernel(
@@ -211,7 +231,7 @@
     out_ref[:, out_ref.shape[1] - total.shape[0] :, :] = jnp.broadcast_to(total[None], place)
 
 
-def weight_kernel(teams, load_ref, halo_ref, norm_ref, gain_ref, bias_ref, out_ref, hidden, acc):
+def weight_kernel(teams, load_ref, other_ref, norm_ref, gain_ref, bias_ref, out_ref, hidden, acc):
     time_index = lax.axis_index("tm")
     rows = load_ref.shape[1]
     cols = hidden.shape[2]
@@ -249,15 +269,28 @@
                     hidden[0, 1 + r] = value
                     hidden[1, 1 + r] = value
 
+    base = 2 * cols
+
+    def pieces_of(q, r):
+        pieces = []
+        for d, (begin, close) in enumerate(SHARES):
+            size = (close - begin) // 2
+            for half in range(2):
+                first = max(q * cols, begin + half * size) - begin - half * size
+                last = min((q + 1) * cols, begin + (half + 1) * size) - begin - half * size
+                if first < last:
+                    mine = load_ref[d, r, base + first : base + last, :]
+                    pieces.append(jnp.where((time_index & 1) == half, mine, other_ref[d, r, first:last, :]))
+        return pieces
+
     lanes = iota((cols, 128), 1) < 64
     more = (time_index < lax.axis_size("tm") - TEAM).astype(F32)
     for j in range(TEAM + 1):
         halves = [[], []]
         for r in range(rows):
-            if j < TEAM:
-                pair = load_ref[j, r, 2 * cols : 3 * cols, :].astype(F32)
-            else:
-                pair = halo_ref[r].astype(F32) * more
+            pair = jnp.concatenate(pieces_of(j, r), axis=0).astype(F32)
+            if j == TEAM:
+                pair = pair * more
             row = iota(pair.shape, 0)
             ahead = jnp.where(row < cols - 1, pltpu.roll(pair, cols - 1, 0), 0.0)
             behind = jnp.where(row > 0, pltpu.roll(pair, 1, 0), 0.0)
@@ -351,7 +384,7 @@
     gain = norm_gain.reshape(1, chans)
     bias = norm_bias.reshape(1, chans)
     size = TEAM * rows
-    length = positions + cols + 16
+    length = positions + HALF + 16
     teams = [[size * g + i for i in range(size)] for g in range(groups)]
     ranks = [[TEAM * g + j for g in range(groups)] for j in range(TEAM)]
 
@@ -376,12 +409,8 @@
         out_shape=jax.ShapeDtypeStruct((TEAM, rows, length, wide), BF16),
         compiler_params=params(62),
         name="pack",
-    )(feats, ups)
+    )(feats, ups, halos[0])
     load = in_teams(load.reshape(size, length, wide)).reshape(TEAM, rows, length, wide)
-
-    halo = lax.ppermute(
-        load[0, :, positions : positions + cols], "tm", [((i + TEAM) % tms, i) for i in range(tms)]
-    )
 
     def whole(shape):
         return pl.BlockSpec(shape, lambda *s: (0,) * len(shape))
@@ -399,16 +428,19 @@
         compiler_params=params(62),
         name="dense",
     )
-    dense = dense_call(ups, *halos, weight)
-
-    stats = pl.pallas_call(
+    dense = dense_call(ups, halos[1], halos[2], halos[0], halos[3], halos[4], weight)
+
+    stats, swap = pl.pallas_call(
         functools.partial(combine_kernel, float(positions * (chans // GROUPS))),
         in_specs=[vmem],
-        out_specs=vmem,
-        out_shape=jax.ShapeDtypeStruct((groups, 8, 128), F32),
-        compiler_params=params(16),
+        out_shape=(
+            jax.ShapeDtypeStruct((groups, 8, 128), F32),
+            jax.ShapeDtypeStruct((TEAM, rows, HALF, wide), BF16),
+        ),
+        compiler_params=params(40),
         name="combine",
     )(load)
+    other = lax.ppermute(swap, "tm", [(t, t ^ 1) for t in range(tms)])
     stats = in_ranks(stats)
 
     act, sums, norm = pl.pallas_call(
@@ -436,7 +468,7 @@
         compiler_params=params(61),
         name="wgrad",
     )
-    part = weight_call(load, halo, norm, gain, bias)
+    part = weight_call(load, other, norm, gain, bias)
     part = pl.pallas_call(
         append_kernel,
         in_specs=[vmem, vmem],

time: 117 us -> 127 us (1.085)
  blocking collectives: 32.1 us -> 71.6 us
  starting transfers between devices: 41 us -> 21.5 us
  waiting for transfers between devices: 14.2 us -> 3.16 us
    all_to_all x0 -> x1, blocking collectives: none -> 35.3 us  [in_teams(): lax.all_to_all(value, ('tm', 'rows'), 0, 0, tiled=True, axis_index_groups...]
    all_to_all x2 -> x1, waiting for transfers between devices: 14.2 us -> 0.01 us  [in_teams(): lax.all_to_all(value, ('tm', 'rows'), 0, 0, tiled=True, axis_index_groups...]
    ppermute x5, starting transfers between devices: 13 us -> 7.01 us  [neighbour(): return lax.ppermute(ups, ('tm', 'rows'), pairs)]
    ppermute x1, starting transfers between devices: 6.1 us -> 0.41 us  [on_device(): other = lax.ppermute(swap, 'tm', [(t, t ^ 1) for t in range(tms)])]
    all_to_all x2 -> x1, starting transfers between devices: 12.3 us -> 6.62 us  [in_teams(): lax.all_to_all(value, ('tm', 'rows'), 0, 0, tiled=True, axis_index_groups...]
    all_to_all x1, blocking collectives: 32.1 us -> 36.2 us  [in_ranks(): lax.all_to_all(value, 'tm', 0, 0, tiled=True, axis_index_groups=ranks)]
    ppermute x5, waiting for transfers between devices: 0.01 us -> 3.16 us  [neighbour(): return lax.ppermute(ups, ('tm', 'rows'), pairs)]
    all_to_all x1, starting transfers between devices: 9.64 us -> 7.46 us  [in_ranks(): lax.all_to_all(value, 'tm', 0, 0, tiled=True, axis_index_groups=ranks)]
  transfers between devices with their start and end apart: 9 -> 8, of which waited for: 1 -> 1; matrix products, arithmetic and copies ran while one was open for 1% -> 0% of each run, Pallas kernels for 18% -> 16%
where the time goes in v8:
time: 127 us; the launch traced here: 126 us
  blocking collectives  71.6 us (56%)
  Pallas kernels  25.7 us (20%)
  starting transfers between devices  21.5 us (17%)
  local copies, waits for them, and re-layouts  3.26 us (3%)
  waiting for transfers between devices  3.16 us (2%)
    all_to_all x1, blocking collectives, in_ranks(): lax.all_to_all(value, 'tm', 0, 0, tiled=True, axis_index_groups=ranks)  36.2 us
    all_to_all x1, blocking collectives, in_teams(): lax.all_to_all(value, ('tm', 'rows'), 0, 0, tiled=True, axis_index_groups...  35.3 us
    pallas_call x1, Pallas kernels, on_device(): dense_call(ups, halos[1], halos[2], halos[0], halos[3], halos[4], weight)  9.8 us
    all_to_all x1, starting transfers between devices, in_ranks(): lax.all_to_all(value, 'tm', 0, 0, tiled=True, axis_index_groups=ranks)  7.46 us
    pallas_call x1, Pallas kernels, on_device(): part = weight_call(load, other, norm, gain, bias)  7.06 us
    ppermute x5, starting transfers between devices, neighbour(): return lax.ppermute(ups, ('tm', 'rows'), pairs)  7.01 us
    all_to_all x1, starting transfers between devices, in_teams(): lax.all_to_all(value, ('tm', 'rows'), 0, 0, tiled=True, axis_index_groups...  6.62 us
    pallas_call x1, Pallas kernels, on_device(): pl.pallas_call(functools.partial(pack_kernel, tms), out_shape=jax.ShapeDt...  3.69 us
  transfers between devices with their start and end apart: 8, of which 1 were waited for; matrix products, arithmetic and copies ran while one was open for 0% of the time, Pallas kernels for 16%

profile of v8, /device:TPU:32, one launch (start us, length us, event | category | flops | bytes accessed | tf_op | source)
XLA Modules:
  0.0 125.9 jit_solution(2476070612786984020)
XLA Ops:
  0.6 0.1 collective-permute-start
  0.7 3.1 %collective-permute-done.later_ref = bf16[2,160,256]{2,1,0:T(8,128)(2,1)S(1)} collective-permute-done((bf16[2,160,256]{2,1,0:T(8,128)(2,1)}, bf16[2,160,256]{2,1,0:T(8,128)(2,1)S(1)}, u32[]{:S(2)}, u32[]{:S(2)}) %collective-permute-start) | collective-permute-done | bytes 163872 | tf_op jit(solution)/shard_map/ppermute | solution.py:403
  3.9 0.7 copy-done.7
  4.5 3.7 %pack.1 = bf16[4,4,448,128]{3,2,1,0:T(8,128)(2,1)} custom-call(bf16[320,512]{1,0:T(8,128)(2,1)} %bitcast.14, bf16[2,160,256]{2,1,0:T(8,128)(2,1)} %bitcast.22, bf16[2,160,256]{2,1,0:T(8,128)(2,1)} %copy-done.7), custom_call_target="tpu_custom_call" | custom-call | tf_op jit(solution)/shard_map/pack/pallas_call | solution.py:407
  8.2 35.3 %all_to_all.20 = bf16[16,448,128]{2,1,0:T(8,128)(2,1)S(1)} all-to-all(bf16[16,448,128]{2,1,0:T(8,128)(2,1)} %bitcast.20), channel_id=1, replica_groups={{0,1,2,3,4,5,6,7,8,9,10,11,12,13,14,15},{16,17,18,19,20,21,22,23,24,25,..., dimensions={0} | all-to-all | bytes 3670016 | tf_op jit(solution)/shard_map/all_to_all | solution.py:392
  43.6 0.8 combine.1
  44.4 0.4 collective-permute-start.1
  44.8 0.6 collective-permute-start.2
  45.4 2.7 %collective-permute-start.3 = (bf16[2,160,256]{2,1,0:T(8,128)(2,1)S(1)}, bf16[2,160,256]{2,1,0:T(8,128)(2,1)S(1)}, u32[]{:S(2)}, u32[]{:S(2)}) collective-permute-start(bf16[2,160,256]{2,1,0:T(8,128)(2,1)S(1)} %bitcast.25), channel_id=1, source_target_pairs={{1,0},{2,1},{3,2},{0,3},{5,4},{6,5},{7,6},{4,7},{9,8},{10,9},{11,1... | collective-permute-start | bytes 491528 | tf_op jit(solution)/shard_map/ppermute | solution.py:403
  48.0 0.0 collective-permute-start.4
  48.0 3.7 %collective-permute-start.5 = (bf16[2,160,256]{2,1,0:T(8,128)(2,1)S(1)}, bf16[2,160,256]{2,1,0:T(8,128)(2,1)}, u32[]{:S(2)}, u32[]{:S(2)}) collective-permute-start(bf16[2,160,256]{2,1,0:T(8,128)(2,1)S(1)} %bitcast.27), channel_id=1, source_target_pairs={{5,0},{6,1},{7,2},{4,3},{9,4},{10,5},{11,6},{8,7},{13,8},{14,9},{1... | collective-permute-start | bytes 491528 | tf_op jit(solution)/shard_map/ppermute | solution.py:403
  51.7 7.5 %all-to-all-start.1 = ((f32[16,8,128]{2,1,0:T(8,128)}), f32[16,8,128]{2,1,0:T(8,128)}, u32[]{:S(2)}, u32[]{:S(2)}) async-start(f32[16,8,128]{2,1,0:T(8,128)} %get-tuple-element.14), calls=%async_computation.1 | async-start | bytes 131072 | tf_op jit(solution)/shard_map/all_to_all | solution.py:395
  59.2 0.0 collective-permute-done.2.above_ref
  59.2 0.0 collective-permute-done.4.later_above_ref
  59.3 0.6 copy-done.8
  59.9 0.1 copy-done.9
  60.0 0.7 copy-done.10
  60.6 9.8 %dense.1.dense_ref = f32[320,512]{1,0:T(8,128)} custom-call(bf16[2,160,256]{2,1,0:T(8,128)(2,1)} %bitcast.23, bf16[2,160,256]{2,1,0:T(8,128)(2,1)} %copy-done.8, bf16[2,160,256]{2,1,0:T(8,128)(2,1)} %copy-done.9, bf16[2,160,256]{2,1,0:T(8,128)(2,1)} %copy-done.7, bf16[2,160,256]{2,1,0:T(8,128)(2,1)} %copy-done.10, ...), custom_call_target="tpu_custom_call" | custom-call | tf_op jit(solution)/shard_map/dense/pallas_call | solution.py:431
  70.4 2.9 %act.1 = (f32[320,512]{1,0:T(8,128)}, f32[16,8,128]{2,1,0:T(8,128)}, f32[16,512]{1,0:T(8,128)}) custom-call(bf16[320,512]{1,0:T(8,128)(2,1)} %bitcast.15, f32[1,512]{1,0:T(1,128)} %bitcast.17, f32[1,512]{1,0:T(1,128)} %bitcast.28, f32[16,8,128]{2,1,0:T(8,128)} %all-to-all-done.1.stats_ref, f32[320,512]{1,0:T(8,128)} %dense.1.dense_ref), custom_call_target="tpu_custom_call" | custom-call | tf_op jit(solution)/shard_map/act/pallas_call | solution.py:446
  73.3 6.6 %all-to-all-start.2 = ((f32[16,8,128]{2,1,0:T(8,128)}), f32[16,8,128]{2,1,0:T(8,128)S(1)}, u32[]{:S(2)}, u32[]{:S(2)}) async-start(f32[16,8,128]{2,1,0:T(8,128)} %get-tuple-element.16), calls=%async_computation.2 | async-start | bytes 131072 | tf_op jit(solution)/shard_map/all_to_all | solution.py:392
  79.9 7.1 %wgrad.1.part_ref = f32[16,120,128]{2,1,0:T(8,128)} custom-call(bf16[4,4,448,128]{3,2,1,0:T(8,128)(2,1)} %bitcast.13, bf16[4,4,112,128]{3,2,1,0:T(8,128)(2,1)} %collective-permute-done.1.other_ref, f32[16,512]{1,0:T(8,128)} %get-tuple-element.15.norm_ref, f32[1,512]{1,0:T(1,128)} %bitcast.18, f32[1,512]{1,0:T(1,128)} %bitcast.29), custom_call_target="tpu_custom_call" | custom-call | tf_op jit(solution)/shard_map/wgrad/pallas_call | solution.py:471
  87.0 1.2 copy-done.1
  88.2 36.2 %all_to_all.21.load_ref = f32[16,120,128]{2,1,0:T(8,128)S(1)} all-to-all(f32[16,120,128]{2,1,0:T(8,128)S(1)} %append.1), channel_id=1, replica_groups={{0,16,32,48,64,80,96,112,128,144,160,176,192,208,224,240},{4,20,36,52,6..., dimensions={0} | all-to-all | bytes 1966080 | tf_op jit(solution)/shard_map/all_to_all | solution.py:395
  124.5 1.4 %final.1 = (bf16[320,512]{1,0:T(8,128)(2,1)}, f32[9,3,8,64]{3,2,1,0:T(8,128)}, f32[1,512]{1,0:T(1,128)}, f32[1,512]{1,0:T(1,128)}) custom-call(f32[16,120,128]{2,1,0:T(8,128)S(1)} %all_to_all.21.load_ref, f32[320,512]{1,0:T(8,128)S(1)} %copy-done.3, bf16[320,512]{1,0:T(8,128)(2,1)S(1)} %bitcast.16, f32[16,512]{1,0:T(8,128)S(1)} %copy-done.4, ...), custom_call_target="tpu_custom_call" | custom-call | tf_op jit(solution)/shard_map/final/pallas_call | solution.py:483
  (23 shorter events, 0.1 us)
Async XLA Ops:
  0.6 3.2 %collective-permute-start = (bf16[2,160,256]{2,1,0:T(8,128)(2,1)}, bf16[2,160,256]{2,1,0:T(8,128)(2,1)S(1)}, u32[]{:S(2)}, u32[]{:S(2)}) collective-permute-start(bf16[2,160,256]{2,1,0:T(8,128)(2,1)} %bitcast.21), channel_id=1, source_target_pairs={{4,0},{5,1},{6,2},{7,3},{8,4},{9,5},{10,6},{11,7},{12,8},{13,9},{1... | collective-permute-start | bytes 491528 | tf_op jit(solution)/shard_map/ppermute | solution.py:403
  3.9 0.7 copy-start.7
  43.5 26.9 %copy-start = (bf16[16,448,128]{2,1,0:T(8,128)(2,1)}, bf16[16,448,128]{2,1,0:T(8,128)(2,1)S(1)}, u32[]{:S(2)}) copy-start(bf16[16,448,128]{2,1,0:T(8,128)(2,1)S(1)} %all_to_all.20) | copy-start | bytes 5505028
  43.6 1.3 copy-start.6
  44.4 35.5 %collective-permute-start.1 = (bf16[4,4,112,128]{3,2,1,0:T(8,128)(2,1)}, bf16[4,4,112,128]{3,2,1,0:T(8,128)(2,1)}, u32[]{:S(2)}, u32[]{:S(2)}) collective-permute-start(bf16[4,4,112,128]{3,2,1,0:T(8,128)(2,1)} %get-tuple-element.13), channel_id=1, source_target_pairs={{0,4},{4,0},{8,12},{12,8},{16,20},{20,16},{24,28},{28,24},{32,36},... | collective-permute-start | bytes 1376264 | tf_op jit(solution)/shard_map/ppermute | solution.py:443
  44.8 14.4 %collective-permute-start.2 = (bf16[2,160,256]{2,1,0:T(8,128)(2,1)S(1)}, bf16[2,160,256]{2,1,0:T(8,128)(2,1)S(1)}, u32[]{:S(2)}, u32[]{:S(2)}) collective-permute-start(bf16[2,160,256]{2,1,0:T(8,128)(2,1)S(1)} %bitcast.24), channel_id=1, source_target_pairs={{3,0},{0,1},{1,2},{2,3},{7,4},{4,5},{5,6},{6,7},{11,8},{8,9},{9,10... | collective-permute-start | bytes 491528 | tf_op jit(solution)/shard_map/ppermute | solution.py:403
  45.4 13.9 %collective-permute-start.3 = (bf16[2,160,256]{2,1,0:T(8,128)(2,1)S(1)}, bf16[2,160,256]{2,1,0:T(8,128)(2,1)S(1)}, u32[]{:S(2)}, u32[]{:S(2)}) collective-permute-start(bf16[2,160,256]{2,1,0:T(8,128)(2,1)S(1)} %bitcast.25), channel_id=1, source_target_pairs={{1,0},{2,1},{3,2},{0,3},{5,4},{6,5},{7,6},{4,7},{9,8},{10,9},{11,1... | collective-permute-start | bytes 491528 | tf_op jit(solution)/shard_map/ppermute | solution.py:403
  48.0 11.2 %collective-permute-start.4 = (bf16[2,160,256]{2,1,0:T(8,128)(2,1)S(1)}, bf16[2,160,256]{2,1,0:T(8,128)(2,1)S(1)}, u32[]{:S(2)}, u32[]{:S(2)}) collective-permute-start(bf16[2,160,256]{2,1,0:T(8,128)(2,1)S(1)} %bitcast.26), channel_id=1, source_target_pairs={{7,0},{4,1},{5,2},{6,3},{11,4},{8,5},{9,6},{10,7},{15,8},{12,9},{1... | collective-permute-start | bytes 491528 | tf_op jit(solution)/shard_map/ppermute | solution.py:403
  48.0 12.6 %collective-permute-start.5 = (bf16[2,160,256]{2,1,0:T(8,128)(2,1)S(1)}, bf16[2,160,256]{2,1,0:T(8,128)(2,1)}, u32[]{:S(2)}, u32[]{:S(2)}) collective-permute-start(bf16[2,160,256]{2,1,0:T(8,128)(2,1)S(1)} %bitcast.27), channel_id=1, source_target_pairs={{5,0},{6,1},{7,2},{4,3},{9,4},{10,5},{11,6},{8,7},{13,8},{14,9},{1... | collective-permute-start | bytes 491528 | tf_op jit(solution)/shard_map/ppermute | solution.py:403
  51.7 18.7 %all-to-all-start.1 = ((f32[16,8,128]{2,1,0:T(8,128)}), f32[16,8,128]{2,1,0:T(8,128)}, u32[]{:S(2)}, u32[]{:S(2)}) async-start(f32[16,8,128]{2,1,0:T(8,128)} %get-tuple-element.14), calls=%async_computation.1 | async-start | bytes 131072 | tf_op jit(solution)/shard_map/all_to_all | solution.py:395
  59.2 0.7 copy-start.8
  59.2 0.7 copy-start.9
  60.0 0.7 copy-start.10
  73.3 13.7 %all-to-all-start.2 = ((f32[16,8,128]{2,1,0:T(8,128)}), f32[16,8,128]{2,1,0:T(8,128)S(1)}, u32[]{:S(2)}, u32[]{:S(2)}) async-start(f32[16,8,128]{2,1,0:T(8,128)} %get-tuple-element.16), calls=%async_computation.2 | async-start | bytes 131072 | tf_op jit(solution)/shard_map/all_to_all | solution.py:392
  87.0 1.2 copy-start.1
  88.2 36.3 %copy-start.2 = (bf16[2,1,160,512]{3,2,1,0:T(8,128)(2,1)S(1)}, bf16[2,1,160,512]{3,2,1,0:T(8,128)(2,1)}, u32[]{:S(2)}) copy-start(bf16[2,1,160,512]{3,2,1,0:T(8,128)(2,1)} %param.5) | copy-start | bytes 983044
  88.2 36.3 %copy-start.3 = (f32[320,512]{1,0:T(8,128)S(1)}, f32[320,512]{1,0:T(8,128)}, u32[]{:S(2)}) copy-start(f32[320,512]{1,0:T(8,128)} %get-tuple-element.17.act_ref) | copy-start | bytes 1966084
  88.2 36.3 %copy-start.4 = (f32[16,512]{1,0:T(8,128)S(1)}, f32[16,512]{1,0:T(8,128)}, u32[]{:S(2)}) copy-start(f32[16,512]{1,0:T(8,128)} %get-tuple-element.15.norm_ref) | copy-start | bytes 98308
  88.2 36.3 %copy-start.5 = (f32[512]{0:T(512)S(1)}, f32[512]{0:T(512)}, u32[]{:S(2)}) copy-start(f32[512]{0:T(512)} %param.6) | copy-start | bytes 6148
